TPU v7x, 32 devices: a whole 2x2x4 slice. The times are simulated.
32 devices in a mesh: rows: 8 (over z, y), seq: 4 (over x, core).
Axes of the slice: x: 2, y: 2, z: 4, core: 2. Of those that a mesh axis runs over, the one named last changes fastest.
Arguments:
- byte_ids: int32 [32, 2048], P('rows', 'seq'), may hold values from 0 to 255
- lengths: int32 [32], P('rows'), may hold values from 385 to 2048, as said below
- embed: float32 [256, 768], replicated, may hold values from -6 to 6
- conv_weight: float32 [4, 768], replicated, may hold values from -3 to 3
- conv_bias: float32 [768], replicated, may hold values from -3 to 3
- score_weight: float32 [768], replicated, may hold values from -0.4375 to 0.4375
- out_grad: float32 [32, 1024, 768], P('rows', 'seq'), may hold values from -6 to 6
Outputs:
- blocks_out: float32 [32, 1024, 768], P('rows', 'seq')
- embed_grad: float32 [256, 768], replicated
- convolution_tap_gradient: float32 [4, 768], replicated
- conv_bias_grad: float32 [768], replicated
- score_weight_grad: float32 [768], replicated
Inputs may be any that keep to these rules, and one draw needn't show every extreme that they name: `lengths`: real bytes of each row; the first row has 2048.
All inputs are finite; a program needn't handle non-finite values.
Results may differ from a plain program's by a relative error of at most 0.0003.
Values sent between devices are 32-bit elements; how exact they have to be, the bound alone decides.
No kernel may reach another device: no remote copies, remote signals or barrier semaphores. Data moves between devices by JAX's collectives and lax.ppermute only.
A program may use at most 192 MiB of HBM per device.

v0:
```python
import jax
import jax.numpy as jnp
from jax import lax
from jax.sharding import PartitionSpec as P

eps_value = 1e-06
high_precision = lax.Precision.HIGHEST


def extended(x, sides, width):
    for axis, dim in sides:
        count, length = (lax.axis_size(axis), x.shape[dim])
        up = [(i, (i + 1) % count) for i in range(count - 1)]
        down = [(j, i) for i, j in up]
        last = lax.slice_in_dim(x, length - width, length, axis=dim)
        initial = lax.slice_in_dim(x, 0, width, axis=dim)
        before = lax.ppermute(last, axis, up)
        after = lax.ppermute(initial, axis, down)
        x = jnp.concatenate([before, x, after], axis=dim)
    return x


def root_mean(total, count, width):
    return jnp.sqrt(total / (count * width) + eps_value)


def conv_rows(padded, conv_weight, conv_bias, width):
    total = conv_bias
    for tap in range(conv_weight.shape[0]):
        total = total + conv_weight[tap] * padded[:, tap : tap + width]
    return total


def pool_blocks(own, mask, ext, mask_ext, start):
    rows, width, feat = own.shape
    pooled = []
    for size in (1, 2, 3, 4):
        if size == 3:
            phase = (start + jnp.arange(width, dtype=jnp.int32)) % 3
            total = jnp.zeros_like(own)
            count = jnp.zeros_like(mask)
            for offset in range(-2, 3):
                inside = ((phase + offset >= 0) & (phase + offset < 3)).astype(jnp.float32)
                total = total + inside[None, :, None] * ext[:, 2 + offset : 2 + offset + width]
                count = count + inside[None, :] * mask_ext[:, 2 + offset : 2 + offset + width]
        else:
            total = jnp.repeat(own.reshape(rows, width // size, size, feat).sum(2), size, axis=1)
            count = jnp.repeat(mask.reshape(rows, width // size, size).sum(2), size, axis=1)
        pooled.append(total / jnp.maximum(count, 1.0)[:, :, None])
    return jnp.stack(pooled)


def mix_blocks(pooled, score_weight, mask):
    scores = jnp.einsum("brwd,d->brw", pooled, score_weight, precision=high_precision)
    probs = jax.nn.softmax(scores, axis=0)
    return jnp.sum(probs[..., None] * pooled, axis=0) * mask[..., None]


def halve(element_numbers, mask):
    rows, width, feat = element_numbers.shape
    total = element_numbers.reshape(rows, width // 2, 2, feat).sum(2)
    count = mask.reshape(rows, width // 2, 2).sum(2)
    return (total / jnp.maximum(count, 1.0)[..., None], mask[:, 0::2])


def mask_at(first, number, lengths):
    places = first + jnp.arange(number, dtype=jnp.int32)
    inside = (places[None, :] >= 0) & (places[None, :] < lengths[:, None])
    return inside.astype(jnp.float32)


def one_hot_rows(ids, vocab):
    return (ids[..., None] == jnp.arange(vocab, dtype=jnp.int32)).astype(jnp.float32)


def stream_scale(element_numbers, mask):
    totals = lax.psum((jnp.sum(element_numbers * element_numbers), jnp.sum(mask)), ("rows", "seq"))
    return (root_mean(totals[0], totals[1], element_numbers.shape[-1]), totals[1])


def norm_back(grad, element_numbers, scale, count):
    inner = lax.psum(jnp.sum(grad * element_numbers), ("rows", "seq"))
    return (grad / scale, inner / (scale * scale * scale * count * element_numbers.shape[-1]))


def on_device(byte_ids, lengths, embed, conv_weight, conv_bias, score_weight, out_grad):
    rows, width = byte_ids.shape
    vocab = embed.shape[0]
    lead = conv_weight.shape[0] - 1
    start = lax.axis_index("seq") * width
    own_mask = mask_at(start, width, lengths)
    mask_ext = mask_at(start - 2, width + 4, lengths)

    def mixing(ext_values, scorer):
        pooled = pool_blocks(ext_values[:, 2 : 2 + width], own_mask, ext_values, mask_ext, start)
        return mix_blocks(pooled, scorer, own_mask)

    reach = lead + 2
    wide_ids = extended(byte_ids, (("seq", 1),), reach)
    wide_ids = wide_ids[:, : width + reach + 2]
    wide_mask = mask_at(start - reach, width + reach + 2, lengths)
    onehot = one_hot_rows(wide_ids, vocab)
    emb_wide = (
        jnp.einsum("rcv,vd->rcd", onehot, embed, precision=high_precision) * wide_mask[..., None]
    )
    emb = emb_wide[:, reach : reach + width]
    scale_one, count = stream_scale(emb, own_mask)
    act_wide = emb_wide / scale_one

    def convolve(inputs, taps, bias):
        return conv_rows(inputs, taps, bias, width + 4)

    conv_raw, conv_pull = jax.vjp(convolve, act_wide, conv_weight, conv_bias)
    convolution_widened = conv_raw * mask_ext[..., None]
    scale_two, unused_count = stream_scale(convolution_widened[:, 2 : 2 + width], own_mask)
    ext = convolution_widened / scale_two
    mixed, mix_pull = jax.vjp(mixing, ext, score_weight)
    scale_three, unused_three = stream_scale(mixed, own_mask)
    hidden_result = mixed / scale_three

    def coarsen_segments(element_numbers):
        return halve(element_numbers, own_mask)[0]

    coarsened_sequences, coarsen_collect = jax.vjp(coarsen_segments, hidden_result)
    down_mask = own_mask[:, 0::2]
    scale_four, count_four = stream_scale(coarsened_sequences, down_mask)
    blocks_out = coarsened_sequences / scale_four
    first, coef = norm_back(out_grad, coarsened_sequences, scale_four, count_four)
    cotangent_coarsened = first - coef * coarsened_sequences
    cotangent_hidden = coarsen_collect(cotangent_coarsened)[0]
    first, coef = norm_back(cotangent_hidden, mixed, scale_three, count)
    g_mixed = first - coef * mixed
    g_ext, g_score = mix_pull(g_mixed)
    centre = ((jnp.arange(width + 4) >= 2) & (jnp.arange(width + 4) < width + 2)).astype(
        jnp.float32
    )
    first, coef = norm_back(g_ext, convolution_widened, scale_two, count)
    convolution_gradient = (first - coef * convolution_widened * centre[None, :, None]) * mask_ext[
        ..., None
    ]
    g_act, g_taps, g_bias = conv_pull(convolution_gradient)
    span = jnp.arange(width + reach + 2)
    middle = ((span >= reach) & (span < reach + width)).astype(jnp.float32)
    first, coef = norm_back(g_act, emb_wide, scale_one, count)
    g_emb = (first - coef * emb_wide * middle[None, :, None]) * wide_mask[..., None]
    g_table = jnp.einsum("rcv,rcd->vd", onehot, g_emb, precision=high_precision)
    summed = lax.psum((g_table, g_taps, g_bias, g_score), ("rows", "seq"))
    return (blocks_out, summed[0], summed[1], summed[2], summed[3])


def solution(mesh):
    placed = (P("rows", "seq"), P("rows"), P(), P(), P(), P(), P("rows", "seq", None))
    return jax.shard_map(
        on_device,
        mesh=mesh,
        in_specs=placed,
        out_specs=(P("rows", "seq", None), P(), P(), P(), P()),
        check_vma=False,
    )
```

profile of v0, /device:TPU:0, one launch (start us, length us, event | category | flops | bytes accessed | tf_op | source)
XLA Modules:
  0.0 855.0 jit_solution(8216544831082482031)
XLA Ops:
  33.5 44.2 %all-reduce.16 = (f32[]{:T(128)}, f32[]{:T(128)}) all-reduce(f32[]{:T(128)} %fusion.20, f32[]{:T(128)} %get-tuple-element.52), channel_id=1, replica_groups=mesh['rows'=8,'seq'=4] {'rows','seq'}, use_global_device_ids=true, to_apply=%region_1.0 | all-reduce | flops 2 | bytes 16 | tf_op jit(solution)/shard_map/psum | solution.py:77
  88.8 40.7 %psum.106 = f32[]{:T(128)} all-reduce(f32[]{:T(128)} %fusion.19), channel_id=1, replica_groups=mesh['rows'=8,'seq'=4] {'rows','seq'}, use_global_device_ids=true, to_apply=%region_5.0 | all-reduce | flops 1 | bytes 8 | tf_op jit(solution)/shard_map/psum | solution.py:77
  130.3 13.6 %broadcast_divide_fusion = f32[4,516,768]{2,1,0:T(8,128)} fusion(f32[]{:T(128)S(6)} %sqrt.13, f32[4,516]{1,0:T(4,128)S(1)} %and_convert_fusion.1, f32[4,519,768]{2,1,0:T(8,128)} %copy-done.2, f32[768]{0:T(1024)S(1)} %get-tuple-element.14, f32[768]{0:T(1024)S(1)} %get-tuple-element.15, f32[768]{0:T(1024)S(1)} %get-tuple-element.13, ...), kind=kLoop, calls=%fused_computation.55 | loop fusion | flops 15851520 | bytes 31726660 | tf_op jit(solution)/shard_map/div | solution.py:116
  143.9 18.1 %divide_bitcast_fusion = (f32[1,4,512,768]{3,2,1,0:T(8,128)}, f32[1,4,512,768]{3,2,1,0:T(8,128)}, f32[4,512,768]{2,1,0:T(8,128)}) fusion(f32[4,512]{1,0:T(4,128)S(1)} %get-tuple-element.51, f32[4,516,768]{2,1,0:T(8,128)} %broadcast_divide_fusion, f32[4,512]{1,0:T(4,128)S(1)} %fusion.40, f32[512]{0:T(512)S(1)} %get-tuple-element.53, ...), kind=kLoop, calls=%fused_computation.47 | loop fusion | flops 17301504 | bytes 50358272 | tf_op jit(solution)/shard_map/jvp()/div | solution.py:49
  162.0 8.2 reshape.509
  177.8 10.2 %fusion.3 = f32[4,256,2,768]{3,2,1,0:T(2,128)} fusion(f32[4,256,2,768]{3,2,1,0:T(2,128)} %reshape.509), kind=kOutput, calls=%fused_computation.3 | output fusion | flops 786433 | bytes 12582912 | tf_op jit(solution)/shard_map/jvp()/broadcast_in_dim | solution.py:47
  188.0 9.0 %reshape.510 = f32[1,4,512,768]{3,2,1,0:T(8,128)} reshape(f32[4,256,2,768]{3,2,1,0:T(2,128)} %fusion.3) | data formatting | bytes 12582912 | tf_op jit(solution)/shard_map/jvp()/reshape | solution.py:47
  223.2 21.6 %fusion.50 = f32[1,4,4,512]{3,0,2,1:T(1,128)S(1)} fusion(f32[768,1,1,1]{0,1,2,3:T(1,128)S(1)} %reshape.518, f32[1,4,512,768]{3,2,1,0:T(8,128)S(1)} %broadcast_divide_fusion.2, f32[1,4,512,768]{3,2,1,0:T(8,128)S(1)} %bitcast.65, f32[1,4,512,768]{3,2,1,0:T(8,128)S(1)} %broadcast_divide_fusion.3, f32[1,4,512,768]{3,2,1,0:T(8,128)S(1)} %bitcast.61), kind=kOutput, calls=%fused_computation.125 | convolution fusion | flops 94371840 | bytes 25201664 | tf_op jit(solution)/shard_map/jvp(brwd,d->brw)/dot_general | solution.py:54
  253.1 8.2 reduce_sum.246
  261.3 40.4 %psum.107 = f32[]{:T(128)} all-reduce(f32[]{:T(128)} %multiply_reduce_fusion.9), channel_id=1, replica_groups=mesh['rows'=8,'seq'=4] {'rows','seq'}, use_global_device_ids=true, to_apply=%region_14.15 | all-reduce | flops 1 | bytes 8 | tf_op jit(solution)/shard_map/psum | solution.py:77
  302.4 33.1 %fusion.21 = f32[4,256,768]{2,1,0:T(8,128)S(1)} fusion(f32[4,256,2,768]{3,2,1,0:T(2,128)} %reduce_sum.246, f32[]{:T(128)S(6)} %sqrt.14, f32[4,256,2]{2,1,0:T(8,128)S(1)} %copy.31), kind=kLoop, calls=%fused_computation.48 | loop fusion | flops 3932160 | bytes 9445380 | tf_op jit(solution)/shard_map/jvp()/reduce_sum | solution.py:61
  340.7 40.5 %all-reduce.15 = (f32[]{:T(128)}, f32[]{:T(128)}, f32[]{:T(128)}) all-reduce(f32[]{:T(128)} %get-tuple-element.11, f32[]{:T(128)} %reduce_sum.253, f32[]{:T(128)} %get-tuple-element.10), channel_id=1, replica_groups=mesh['rows'=8,'seq'=4] {'rows','seq'}, use_global_device_ids=true, to_apply=%region_17.18 | all-reduce | flops 3 | bytes 24 | tf_op jit(solution)/shard_map/psum | solution.py:77
  393.7 8.5 reshape.513
  409.4 40.7 %psum.111 = f32[]{:T(128)} all-reduce(f32[]{:T(128)} %multiply_reduce_fusion.8), channel_id=1, replica_groups=mesh['rows'=8,'seq'=4] {'rows','seq'}, use_global_device_ids=true, to_apply=%region_23.24 | all-reduce | flops 1 | bytes 8 | tf_op jit(solution)/shard_map/psum | solution.py:82
  456.6 13.3 %multiply_reduce_fusion = f32[4,4,512]{2,1,0:T(4,128)S(1)} fusion(f32[4,512,768]{2,1,0:T(8,128)S(1)} %subtract_multiply_fusion.1, f32[1,4,512,768]{3,2,1,0:T(8,128)} %copy-done.6, f32[1,4,512,768]{3,2,1,0:T(8,128)} %get-tuple-element.45, f32[1,4,512,768]{3,2,1,0:T(8,128)} %copy-done.5, f32[1,4,512,768]{3,2,1,0:T(8,128)S(1)} %bitcast.63), kind=kLoop, calls=%fused_computation.6 | loop fusion | flops 31449088 | bytes 31490048 | tf_op jit(solution)/shard_map/transpose(jvp())/reduce_sum | solution.py:56
  470.1 12.5 %multiply_add_fusion = f32[4,4,512,768]{3,2,1,0:T(8,128)} fusion(f32[768]{0:T(1024)S(1)} %copy-done.39, f32[4,4,512]{2,1,0:T(4,128)S(1)} %add_multiply_fusion.1, f32[4,512,768]{2,1,0:T(8,128)} %copy-done.7, f32[4,4,512]{2,1,0:T(4,128)S(1)} %broadcast_divide_fusion.6), kind=kLoop, calls=%fused_computation.5 | loop fusion | flops 18874368 | bytes 31525888 | tf_op jit(solution)/shard_map/transpose(jvp(brwd,d->brw))/add_any | solution.py:54
  482.6 10.2 %fusion.33 = f32[768]{0:T(1024)S(1)} fusion(f32[4,4,512,1]{2,1,0,3:T(4,128)S(1)} %bitcast.74, f32[1,4,512,768]{3,2,1,0:T(8,128)S(1)} %bitcast.71, f32[1,4,512,768]{3,2,1,0:T(8,128)S(1)} %bitcast.67, f32[1,4,512,768]{3,2,1,0:T(8,128)S(1)} %bitcast.69, f32[1,4,512,768]{3,2,1,0:T(8,128)S(1)} %bitcast.63), kind=kOutput, calls=%fused_computation.81 | convolution fusion | flops 94371840 | bytes 25201664 | tf_op jit(solution)/shard_map/transpose(jvp(brwd,d->brw))/dot_general | solution.py:54
  492.8 10.0 %fusion.55 = (f32[1,4,512,768]{3,2,1,0:T(8,128)}, f32[1,4,512,768]{3,2,1,0:T(8,128)}) fusion(f32[4,4,512,768]{3,2,1,0:T(8,128)} %multiply_add_fusion), kind=kLoop, calls=%fused_computation.148 | loop fusion | bytes 25165824 | tf_op jit(solution)/shard_map/transpose(jvp())/unstack | solution.py:50
  502.8 8.1 unstack.29
  510.9 10.1 %fusion = f32[4,256,2,768]{3,2,1,0:T(2,128)} fusion(f32[4,256,2,768]{3,2,1,0:T(2,128)} %unstack.29, f32[4,256]{1,0:T(4,128)S(1)} %broadcast_maximum_fusion), kind=kOutput, calls=%fused_computation | output fusion | flops 2359297 | bytes 12587008 | tf_op jit(solution)/shard_map/transpose(jvp())/broadcast_in_dim | solution.py:47
  521.0 8.9 %reshape.515 = f32[4,512,768]{2,1,0:T(8,128)} reshape(f32[4,256,2,768]{3,2,1,0:T(2,128)} %fusion) | data formatting | bytes 12582912 | tf_op jit(solution)/shard_map/transpose(jvp())/reshape | solution.py:47
  537.4 8.8 %fusion.1 = f32[4,128,4,768]{3,2,1,0:T(4,128)} fusion(f32[4,128,4,768]{3,2,1,0:T(4,128)} %unstack.27, f32[4,128]{1,0:T(4,128)S(1)} %copy-done.42), kind=kOutput, calls=%fused_computation.1 | output fusion | flops 1966083 | bytes 12584960 | tf_op jit(solution)/shard_map/transpose(jvp())/broadcast_in_dim | solution.py:47
  546.3 7.9 reshape.514
  554.3 17.4 %broadcast_multiply_fusion.5 = (f32[4,512,768]{2,1,0:T(8,128)S(1)}, f32[4,512,768]{2,1,0:T(8,128)S(1)}, f32[4,512,768]{2,1,0:T(8,128)}, f32[4,512,768]{2,1,0:T(8...) fusion(f32[512]{0:T(512)S(1)} %copy-done.32, f32[4,512]{1,0:T(4,128)S(1)} %copy-done.22, ...), kind=kLoop, calls=%fused_computation.70 | loop fusion | flops 14155776 | bytes 62941184 | tf_op jit(solution)/shard_map/transpose(jvp())/mul | solution.py:44
  571.7 13.9 %multiply_reduce_fusion.7 = (f32[]{:T(128)}, f32[4,516,768]{2,1,0:T(8,128)}) fusion(f32[4,512,768]{2,1,0:T(8,128)} %get-tuple-element.37, f32[4,512,768]{2,1,0:T(8,128)} %get-tuple-element.36, f32[4,512,768]{2,1,0:T(8,128)} %get-tuple-element.35, f32[4,512,768]{2,1,0:T(8,128)} %get-tuple-element.34, f32[4,512,768]{2,1,0:T(8,128)S(1)} %get-tuple-element.33, ...), kind=kLoop, calls=%fused_computation.21 | loop fusion | flops 25362432 | bytes 69475392 | tf_op jit(solution)/shard_map/reduce_sum | solution.py:82
  585.6 40.5 %psum.112 = f32[]{:T(128)} all-reduce(f32[]{:T(128)} %get-tuple-element.28), channel_id=1, replica_groups=mesh['rows'=8,'seq'=4] {'rows','seq'}, use_global_device_ids=true, to_apply=%region_29.30 | all-reduce | flops 1 | bytes 8 | tf_op jit(solution)/shard_map/psum | solution.py:82
  627.5 13.6 %multiply_reduce_fusion.5 = (f32[768]{0:T(1024)S(1)}, f32[768]{0:T(1024)S(1)}, f32[768]{0:T(1024)S(1)}, f32[768]{0:T(1024)S(1)}, f32[768]{0:T(1024)S(1)}, /*index=5*/f32[4,516,768]{2,1,0:T(8,128)S(1)}) fusion(f32[4,519,768]{2,1,0:T(8,128)} %copy-done.2, f32[4,516]{1,0:T(4,128)S(1)} %copy-done.10, f32[516]{0:T(1024)S(1)} %copy-done.40, f32[]{:T(128)S(6)} %div.239, ...), kind=kLoop, calls=%fused_computation.11 | loop fusion | flops 36454656 | bytes 38084696 | tf_op jit(solution)/shard_map/transpose(jvp())/reduce_sum | solution.py:30
  641.2 8.9 %broadcast_multiply_fusion = (f32[4,516,768]{2,1,0:T(8,128)}, f32[4,516,768]{2,1,0:T(8,128)}, f32[4,516,768]{2,1,0:T(8,128)}, f32[4,516,768]{2,1,0:T(8,128)}) fusion(f32[4,516,768]{2,1,0:T(8,128)S(1)} %get-tuple-element.25, f32[768]{0:T(1024)S(1)} %copy-done.16, f32[768]{0:T(1024)S(1)} %copy-done.12, f32[768]{0:T(1024)S(1)} %copy-done.14, f32[768]{0:T(1024)S(1)} %copy-done.18), kind=kLoop, calls=%fused_computation.56 | loop fusion | flops 6340608 | bytes 31715328 | tf_op jit(solution)/shard_map/transpose(jvp())/mul | solution.py:30
  650.9 14.8 %multiply_reduce_fusion.6 = (f32[]{:T(128)}, f32[4,519,768]{2,1,0:T(8,128)}) fusion(f32[4,519,768]{2,1,0:T(8,128)} %copy-done.4, f32[4,516,768]{2,1,0:T(8,128)} %get-tuple-element.41, f32[4,516,768]{2,1,0:T(8,128)} %get-tuple-element.42, f32[4,516,768]{2,1,0:T(8,128)} %get-tuple-element.43, f32[4,516,768]{2,1,0:T(8,128)} %get-tuple-element.40), kind=kLoop, calls=%fused_computation.17 | loop fusion | flops 7971839 | bytes 38117380 | tf_op jit(solution)/shard_map/reduce_sum | solution.py:82
  665.7 40.9 %all-reduce.14 = (f32[]{:T(128)}, f32[4,768]{1,0:T(4,128)}, f32[768]{0:T(1024)}, f32[768]{0:T(1024)}) all-reduce(f32[]{:T(128)} %get-tuple-element.26, f32[4,768]{1,0:T(4,128)S(1)} %pad_add_fusion.2, f32[768]{0:T(1024)S(1)} %get-tuple-element.9, f32[768]{0:T(1024)S(1)} %fusion.33), channel_id=1, replica_groups=mesh['rows'=8,'seq'=4] {'rows','seq'}, use_global_device_ids=true, to_apply=%region_31.32 | all-reduce | flops 4609 | bytes 36872 | tf_op jit(solution)/shard_map/psum | solution.py:82
  707.2 9.3 %fusion.30 = f32[256,768]{1,0:T(8,128)} fusion(f32[4,519,768]{2,1,0:T(8,128)} %copy-done.4, f32[4,519,768]{2,1,0:T(8,128)} %get-tuple-element.27, f32[519]{0:T(1024)S(1)} %copy-done.43, f32[]{:T(128)S(6)} %div.241, f32[]{:T(128)S(6)} %sqrt.12, f32[4,519]{1,0:T(4,128)S(1)} %copy-done.28, s32[4,519]{1,0:T(4,128)S(1)} %copy-done.26), kind=kOutput, calls=%fused_computation.79 | convolution fusion | flops 4906401792 | bytes 13560068 | tf_op jit(solution)/shard_map/rcv,rcd->vd/dot_general | solution.py:146
  716.6 129.4 %all-reduce.19.cloned.1.call-done = f32[256,768]{1,0:T(8,128)} async-done(((f32[256,768]{1,0:T(8,128)}), f32[256,768]{1,0:T(8,128)}) %all-reduce.19.cloned.1.call-update) | async-done | bytes 786448 | tf_op jit(solution)/shard_map/psum | solution.py:147
  (198 shorter events, 114.8 us)
Async XLA Ops:
  7.2 18.3 %copy-start = (f32[256,768]{1,0:T(8,128)S(1)}, f32[256,768]{1,0:T(8,128)}, u32[]{:S(2)}) copy-start(f32[256,768]{1,0:T(8,128)} %param.9) | copy-start | bytes 2359300
  7.2 838.8 %all-reduce.19.cloned.1.call-start = ((), (), s32[]{:S(2)}) async-start(), calls=%async_computation | async-start | bytes 1572864 | tf_op jit(solution)/shard_map/psum | solution.py:147
  8.1 16.7 %collective-permute-start = (s32[4,5]{1,0:T(4,128)S(1)}, s32[4,5]{1,0:T(4,128)S(1)}, u32[]{:S(2)}, u32[]{:S(2)}) collective-permute-start(s32[4,5]{1,0:T(4,128)S(1)} %get-tuple-element.49), channel_id=1, source_target_pairs={{0,1},{1,2},{2,3},{4,5},{5,6},{6,7},{8,9},{9,10},{10,11},{12,13},{... | collective-permute-start | bytes 248 | tf_op jit(solution)/shard_map/ppermute | solution.py:17
  10.4 14.3 %collective-permute-start.1 = (s32[4,5]{1,0:T(4,128)S(1)}, s32[4,5]{1,0:T(4,128)S(1)}, u32[]{:S(2)}, u32[]{:S(2)}) collective-permute-start(s32[4,5]{1,0:T(4,128)S(1)} %get-tuple-element.50), channel_id=1, source_target_pairs={{1,0},{2,1},{3,2},{5,4},{6,5},{7,6},{9,8},{10,9},{11,10},{13,12},{... | collective-permute-start | bytes 248 | tf_op jit(solution)/shard_map/ppermute | solution.py:18
  11.8 132.1 %copy-start.29 = (f32[512]{0:T(512)}, f32[512]{0:T(512)S(1)}, u32[]{:S(2)}) copy-start(f32[512]{0:T(512)S(1)} %get-tuple-element.57) | copy-start | bytes 6148
  11.8 132.0 %copy-start.31 = (f32[512]{0:T(512)}, f32[512]{0:T(512)S(1)}, u32[]{:S(2)}) copy-start(f32[512]{0:T(512)S(1)} %get-tuple-element.53) | copy-start | bytes 6148
  11.8 132.0 %copy-start.33 = (f32[512]{0:T(512)}, f32[512]{0:T(512)S(1)}, u32[]{:S(2)}) copy-start(f32[512]{0:T(512)S(1)} %get-tuple-element.54) | copy-start | bytes 6148
  11.9 132.0 %copy-start.35 = (f32[512]{0:T(512)}, f32[512]{0:T(512)S(1)}, u32[]{:S(2)}) copy-start(f32[512]{0:T(512)S(1)} %get-tuple-element.55) | copy-start | bytes 6148
  11.9 132.0 %copy-start.37 = (f32[512]{0:T(512)}, f32[512]{0:T(512)S(1)}, u32[]{:S(2)}) copy-start(f32[512]{0:T(512)S(1)} %get-tuple-element.56) | copy-start | bytes 6148
  13.3 130.6 %copy-start.19 = (f32[4,512]{1,0:T(4,128)}, f32[4,512]{1,0:T(4,128)S(1)}, u32[]{:S(2)}) copy-start(f32[4,512]{1,0:T(4,128)S(1)} %get-tuple-element.51) | copy-start | bytes 24580
  16.2 114.1 %copy-start.11 = (f32[768]{0:T(1024)}, f32[768]{0:T(1024)S(1)}, u32[]{:S(2)}) copy-start(f32[768]{0:T(1024)S(1)} %get-tuple-element.12) | copy-start | bytes 9220
  16.2 114.1 %copy-start.13 = (f32[768]{0:T(1024)}, f32[768]{0:T(1024)S(1)}, u32[]{:S(2)}) copy-start(f32[768]{0:T(1024)S(1)} %get-tuple-element.13) | copy-start | bytes 9220
  16.2 114.1 %copy-start.15 = (f32[768]{0:T(1024)}, f32[768]{0:T(1024)S(1)}, u32[]{:S(2)}) copy-start(f32[768]{0:T(1024)S(1)} %get-tuple-element.14) | copy-start | bytes 9220
  16.2 114.1 %copy-start.17 = (f32[768]{0:T(1024)}, f32[768]{0:T(1024)S(1)}, u32[]{:S(2)}) copy-start(f32[768]{0:T(1024)S(1)} %get-tuple-element.15) | copy-start | bytes 9220
  24.5 105.8 %copy-start.9 = (f32[4,516]{1,0:T(4,128)}, f32[4,516]{1,0:T(4,128)S(1)}, u32[]{:S(2)}) copy-start(f32[4,516]{1,0:T(4,128)S(1)} %and_convert_fusion.1) | copy-start | bytes 24772
  24.6 119.3 %copy-start.21 = (f32[4,512]{1,0:T(4,128)}, f32[4,512]{1,0:T(4,128)S(1)}, u32[]{:S(2)}) copy-start(f32[4,512]{1,0:T(4,128)S(1)} %fusion.40) | copy-start | bytes 24580
  215.9 29.0 %copy-start.5 = (f32[1,4,512,768]{3,2,1,0:T(8,128)}, f32[1,4,512,768]{3,2,1,0:T(8,128)S(1)}, u32[]{:S(2)}) copy-start(f32[1,4,512,768]{3,2,1,0:T(8,128)S(1)} %broadcast_divide_fusion.3) | copy-start | bytes 18874372
  222.3 22.6 %copy-start.6 = (f32[1,4,512,768]{3,2,1,0:T(8,128)}, f32[1,4,512,768]{3,2,1,0:T(8,128)S(1)}, u32[]{:S(2)}) copy-start(f32[1,4,512,768]{3,2,1,0:T(8,128)S(1)} %broadcast_divide_fusion.2) | copy-start | bytes 18874372
  402.2 53.9 %slice-start.4 = ((s8[6291456]{0:T(1024)(128)(4,1)}), s8[2097152]{0:T(1024)(128)(4,1)S(1)}, s32[]{:S(2)}) async-start(s8[6291456]{0:T(1024)(128)(4,1)} %bitcast.62), calls=%async_computation.5 | async-start | bytes 4194304
  456.6 26.0 %slice-start.8 = ((s8[6291456]{0:T(1024)(128)(4,1)}), s8[4194304]{0:T(1024)(128)(4,1)S(1)}, s32[]{:S(2)}) async-start(s8[6291456]{0:T(1024)(128)(4,1)} %bitcast.66), calls=%async_computation.9 | async-start | bytes 8388608
  456.6 26.0 %slice-start.10 = ((s8[6291456]{0:T(1024)(128)(4,1)}), s8[4194304]{0:T(1024)(128)(4,1)S(1)}, s32[]{:S(2)}) async-start(s8[6291456]{0:T(1024)(128)(4,1)} %bitcast.68), calls=%async_computation.11 | async-start | bytes 8388608
  456.6 26.0 %slice-start.12 = ((s8[6291456]{0:T(1024)(128)(4,1)}), s8[4194304]{0:T(1024)(128)(4,1)S(1)}, s32[]{:S(2)}) async-start(s8[6291456]{0:T(1024)(128)(4,1)} %bitcast.70), calls=%async_computation.13 | async-start | bytes 8388608
  546.3 25.4 %slice-start = ((s8[6389760]{0:T(1024)(128)(4,1)}), s8[2195456]{0:T(1024)(128)(4,1)S(1)}, s32[]{:S(2)}) async-start(s8[6389760]{0:T(1024)(128)(4,1)} %bitcast.58), calls=%async_computation.1 | async-start | bytes 4390912
  554.2 17.4 %slice-start.1 = ((s8[6389760]{0:T(1024)(128)(4,1)}), s8[4194304]{0:T(1024)(128)(4,1)S(1)}, s32[]{:S(2)}) async-start(s8[6389760]{0:T(1024)(128)(4,1)} %bitcast.58), calls=%async_computation.2 | async-start | bytes 8388608
  554.2 17.4 %copy-start.10 = (f32[4,516]{1,0:T(4,128)S(1)}, f32[4,516]{1,0:T(4,128)}, u32[]{:S(2)}) copy-start(f32[4,516]{1,0:T(4,128)} %copy-done.9) | copy-start | bytes 24772
  554.2 17.4 %copy-start.12 = (f32[768]{0:T(1024)S(1)}, f32[768]{0:T(1024)}, u32[]{:S(2)}) copy-start(f32[768]{0:T(1024)} %copy-done.11) | copy-start | bytes 9220
  554.2 17.4 %copy-start.14 = (f32[768]{0:T(1024)S(1)}, f32[768]{0:T(1024)}, u32[]{:S(2)}) copy-start(f32[768]{0:T(1024)} %copy-done.13) | copy-start | bytes 9220
  571.7 55.8 %copy-start.40 = (f32[516]{0:T(1024)S(1)}, f32[516]{0:T(1024)}, u32[]{:S(2)}) copy-start(f32[516]{0:T(1024)} %fusion.47) | copy-start | bytes 6196
  650.9 56.3 %copy-start.26 = (s32[4,519]{1,0:T(4,128)S(1)}, s32[4,519]{1,0:T(4,128)}, u32[]{:S(2)}) copy-start(s32[4,519]{1,0:T(4,128)} %copy-done.25) | copy-start | bytes 24916
  650.9 56.3 %copy-start.28 = (f32[4,519]{1,0:T(4,128)S(1)}, f32[4,519]{1,0:T(4,128)}, u32[]{:S(2)}) copy-start(f32[4,519]{1,0:T(4,128)} %copy-done.27) | copy-start | bytes 24916
  650.9 56.3 %copy-start.43 = (f32[519]{0:T(1024)S(1)}, f32[519]{0:T(1024)}, u32[]{:S(2)}) copy-start(f32[519]{0:T(1024)} %fusion.49) | copy-start | bytes 6232
  707.2 140.8 %copy-start.1 = (f32[256,768]{1,0:T(8,128)S(1)}, f32[256,768]{1,0:T(8,128)}, u32[]{:S(2)}) copy-start(f32[256,768]{1,0:T(8,128)} %param.9) | copy-start | bytes 2359300
  (29 other events, 255.5 us)
Sparse Core Ops, SparseCore 0:
  716.7 129.1 all-reduce.18
where the time goes:
time: 866 us; the launch traced here: 855 us
  blocking collectives  288 us (33%)
  other arithmetic  253 us (29%)
  waiting for transfers between devices  129 us (15%)
  local copies, waits for them, and re-layouts  112 us (13%)
  matrix products  44.1 us (5%)
  between operations  24.8 us (3%)
    psum x4, blocking collectives, stream_scale(): lax.psum((jnp.sum(element_numbers * element_numbers), jnp.sum(mask)), ('r...  166 us
    psum x1, waiting for transfers between devices, on_device(): summed = lax.psum((g_table, g_taps, g_bias, g_score), ('rows', 'seq'))  129 us
    psum x3, blocking collectives, norm_back(): inner = lax.psum(jnp.sum(grad * element_numbers), ('rows', 'seq'))  122 us
    reduce_sum x4, other arithmetic, norm_back(): inner = lax.psum(jnp.sum(grad * element_numbers), ('rows', 'seq'))  39.4 us
    reduce_sum x1, other arithmetic, halve(): total = element_numbers.reshape(rows, width // 2, 2, feat).sum(2)  33.1 us
    reshape x4, local copies, waits for them, and re-layouts, pool_blocks(): own.reshape(rows, width // size, size, feat).sum(2)  32.5 us
    dot_general x2, matrix products, mix_blocks(): jnp.einsum('brwd,d->brw', pooled, score_weight, precision=high_precision)  31.8 us
    div x3, other arithmetic, pool_blocks(): pooled.append(total / jnp.maximum(count, 1.0)[:, :, None])  27.9 us
  transfers between devices with their start and end apart: 3, of which 1 were waited for; matrix products, arithmetic and copies ran while one was open for 1% of the time, Pallas kernels for 0%

commit v1 on v0

v1 whole, which is shorter than its diff:
```python
import functools

import jax
import jax.numpy as jnp
from jax import lax
from jax.experimental import pallas as pl
from jax.experimental.pallas import tpu as pltpu
from jax.sharding import PartitionSpec as P

f32 = jnp.float32
EPS = 1e-06
HIGH = lax.Precision.HIGHEST
LANES = 128
RUNS = 8
OFF = 8
LEFT, RIGHT = 5, 2
NT = (((1,), (1,)), ((), ()))
TN = (((0,), (0,)), ((), ()))
AXES = ("rows", "seq")
VMEM = pl.BlockSpec(memory_space=pltpu.VMEM)
SMEM = pl.BlockSpec(memory_space=pltpu.SMEM)


def iota(shape, dim):
    return lax.broadcasted_iota(jnp.int32, shape, dim)


def shifted(x, by):
    return x if by == 0 else pltpu.roll(x, (-by) % LANES, 1)


def as_tiles(x):
    n, feat = x.shape
    return x.reshape(n // 8, 8, feat // LANES, LANES).transpose(0, 2, 1, 3).reshape(n * feat // LANES, LANES)


def from_tiles(x, feat):
    n = x.shape[0] * LANES // feat
    return x.reshape(n // 8, feat // LANES, 8, LANES).transpose(0, 2, 1, 3).reshape(n, feat)


def pair_rows(r, k, tile, half, tiles):
    first = ((r * RUNS * (half // 8) + k // 8) * tiles + tile) * 8 + k % 8
    return pl.ds(first, RUNS, stride=half // 8 * tiles * 8)


def prep_kernel(embed_ref, taps_ref, bias_ref, scorer_ref, split_ref, table_ref):
    embed = embed_ref[...]
    high = embed.astype(jnp.bfloat16)
    split_ref[0] = high
    split_ref[1] = (embed - high.astype(f32)).astype(jnp.bfloat16)
    taps = taps_ref[...]
    rows = jnp.concatenate([taps * scorer_ref[...], taps * bias_ref[...]], axis=0)
    table_ref[0:8, :] = lax.dot_general(rows, embed, NT, precision=HIGH, preferred_element_type=f32)
    table_ref[8:16, :] = lax.dot_general(
        jnp.ones_like(rows), embed * embed, NT, precision=HIGH, preferred_element_type=f32
    )


def stats_kernel(
    sizes, own_ref, left_ref, right_ref, len_ref, split_ref, table_ref, taps_ref, bias_ref, grad_ref,
    emb_ref, conv_ref, ids_ref, dots_ref, sums_ref,
):
    rows, width, run, feat, vocab, kernel = sizes
    tiles = feat // LANES
    start = lax.axis_index("seq") * width
    lane = iota((RUNS, LANES), 1)
    sub = iota((RUNS, LANES), 0)
    base = start + run * sub
    back = (OFF - run) % LANES

    for r in range(rows):
        own = own_ref[r * RUNS : (r + 1) * RUNS, :]
        before = pltpu.roll(pltpu.roll(own, 1, 0), back, 1)
        edge = pltpu.roll(jnp.broadcast_to(left_ref[r : r + 1, width - LANES : width], (RUNS, LANES)), OFF, 1)
        before = jnp.where(sub == 0, edge, before)
        after = pltpu.roll(pltpu.roll(own, RUNS - 1, 0), OFF + run, 1)
        edge = pltpu.roll(jnp.broadcast_to(right_ref[r : r + 1, 0:LANES], (RUNS, LANES)), OFF + run, 1)
        after = jnp.where(sub == RUNS - 1, edge, after)
        ids = jnp.where(lane < OFF, before, jnp.where(lane < OFF + run, pltpu.roll(own, OFF, 1), after))
        place = base + lane - OFF
        real = (place >= 0) & (place < len_ref[r])
        real = real & (lane >= OFF - LEFT) & (lane < OFF + run + RIGHT)
        ids_ref[r * RUNS : (r + 1) * RUNS, :] = jnp.where(real, ids, -1)

    group = 8
    vr = rows * RUNS
    for first in range(0, emb_ref.shape[0], group):
        marks = []
        for i in range(first, first + group):
            column = ids_ref[:, i + OFF - LEFT : i + OFF - LEFT + 1]
            marks.append((column == iota((vr, vocab), 1)).astype(f32))
        onehot = jnp.concatenate(marks, axis=0).astype(jnp.bfloat16)
        total = jnp.dot(onehot, split_ref[0], preferred_element_type=f32)
        total = total + jnp.dot(onehot, split_ref[1], preferred_element_type=f32)
        emb_ref[first : first + group] = total.reshape(group, vr, feat)

    def convolve(step, carry):
        r, tile = step // tiles, step % tiles
        at = (pl.ds(pl.multiple_of(r * RUNS, RUNS), RUNS), pl.ds(pl.multiple_of(tile * LANES, LANES), LANES))
        length = len_ref[r]
        taps = [jnp.broadcast_to(taps_ref[k : k + 1, at[1]], (RUNS, LANES)) for k in range(kernel)]
        window = [emb_ref[k, at[0], at[1]] for k in range(kernel - 1)]
        for j in range(-2, run + 2):
            window.append(emb_ref[j + LEFT, at[0], at[1]])
            total = taps[0] * window[0]
            for k in range(1, kernel):
                total = total + taps[k] * window[k]
            window = window[1:]
            real = base < length - j
            if j < 0:
                real = real & (base >= -j)
            conv_ref[j + 2, at[0], at[1]] = jnp.where(real, total, 0.0)
        return carry

    lax.fori_loop(0, rows * tiles, convolve, 0)

    dots_ref[...] = jnp.zeros_like(dots_ref)
    block = 4
    slices = run + 4

    def lagged(step, carry):
        r, first = step // (slices // block), step % (slices // block) * block
        at = pl.ds(pl.multiple_of(r * RUNS, RUNS), RUNS)
        acc = {}
        for tile in range(tiles):
            cols = slice(tile * LANES, (tile + 1) * LANES)
            u = [conv_ref[first + i, at, cols] for i in range(block + 5)]
            for i in range(block):
                for lag in range(6):
                    term = u[i] * u[i + lag]
                    acc[i, lag] = term if tile == 0 else acc[i, lag] + term
        for lag in range(6):
            value = dots_ref[lag, at, :]
            for i in range(block):
                here = lane == first + (i + OFF - 2)
                value = jnp.where(here, jnp.sum(acc[i, lag], axis=1, keepdims=True), value)
            dots_ref[lag, at, :] = value
        return carry

    for i in range(slices, slices + 8):
        conv_ref[i] = jnp.zeros_like(conv_ref[i])
    lax.fori_loop(0, rows * (slices // block), lagged, 0)

    half = run // 2

    def crossed(step, carry):
        r, first = step // (half // block), step % (half // block) * block
        at = pl.ds(pl.multiple_of(r * RUNS, RUNS), RUNS)
        acc = {}
        for tile in range(tiles):
            cols = slice(tile * LANES, (tile + 1) * LANES)
            u = [conv_ref[2 * first + i, at, cols] for i in range(2 * block + 4)]
            bias = jnp.broadcast_to(bias_ref[:, cols], (RUNS, LANES))
            for i in range(block):
                g = grad_ref[pair_rows(r, first + i, tile, half, tiles), :]
                terms = [g * u[2 * i + d] for d in range(6)] + [g * bias]
                for d in range(7):
                    acc[i, d] = terms[d] if tile == 0 else acc[i, d] + terms[d]
        for d in range(7):
            value = dots_ref[6 + d, at, :]
            for i in range(block):
                here = lane == 2 * first + (2 * i + OFF)
                value = jnp.where(here, jnp.sum(acc[i, d], axis=1, keepdims=True), value)
            dots_ref[6 + d, at, :] = value
        return carry

    lax.fori_loop(0, rows * (half // block), crossed, 0)

    def total_of(x):
        return jnp.sum(jnp.sum(x, axis=1, keepdims=True), axis=0, keepdims=True)

    sums = [jnp.zeros((1, 1), f32) for _ in range(5)]
    for r in range(rows):
        at = slice(r * RUNS, (r + 1) * RUNS)
        ids = ids_ref[at, :]
        real = ids >= 0
        low = jnp.where(real, ids, 0)

        def look(row):
            value = jnp.zeros((RUNS, LANES), f32)
            for part in range(vocab // LANES):
                entry = jnp.broadcast_to(
                    table_ref[row : row + 1, part * LANES : (part + 1) * LANES], (RUNS, LANES)
                )
                picked = jnp.take_along_axis(entry, low % LANES, axis=1)
                value = jnp.where(low // LANES == part, picked, value)
            return jnp.where(real, value, 0.0)

        scored = jnp.zeros((RUNS, LANES), f32)
        biased = jnp.zeros((RUNS, LANES), f32)
        for k in range(kernel):
            scored = scored + shifted(look(k), k - (kernel - 1))
            biased = biased + shifted(look(4 + k), k - (kernel - 1))
        inner = real & (lane >= OFF - 2)
        scored = jnp.where(inner, scored, 0.0)
        biased = jnp.where(inner, biased, 0.0)
        dots_ref[13, at, :] = scored
        dots_ref[14, at, :] = biased
        own = (real & (lane >= OFF) & (lane < OFF + run)).astype(f32)
        for i, x in enumerate((
            own * look(8), own, own * biased, own * dots_ref[0, at, :], own * (1 - lane % 2).astype(f32)
        )):
            sums[i] = sums[i] + total_of(x)
    sums_ref[...] = spread(sums, sums_ref.shape[0])


def spread(sums, count):
    lane = iota((1, LANES), 1)
    row = jnp.zeros((1, LANES), f32)
    for i, x in enumerate(sums):
        row = jnp.where(lane == i, x, row)
    return jnp.broadcast_to(row[None], (count, 1, LANES))


def picked(ref, number):
    row = jnp.sum(ref[...], axis=0)
    return [row[:, i : i + 1] for i in range(number)]


def scales(first_ref, bias, feat):
    emb_sum, count, cross, square, count4 = picked(first_ref, 5)
    one = jnp.sqrt(emb_sum / (count * feat) + EPS)
    bias_sum = jnp.sum(bias * bias, axis=1, keepdims=True)
    conv_sum = jnp.maximum(count * bias_sum + 2.0 * cross / one + square / (one * one), 0.0)
    two = jnp.sqrt(conv_sum / (count * feat) + EPS)
    return one, two, count, count4, bias_sum, cross


class Places:
    def __init__(self, ids, start, run):
        shape = ids.shape
        self.j = iota(shape, 1) - OFF
        sub = iota(shape, 0) % RUNS
        self.inside = (self.j >= 0) & (self.j < run)
        self.real = ((ids >= 0) & (self.j >= -2)).astype(f32)
        self.own = jnp.where(self.inside, self.real, 0.0)
        shown = self.j + OFF
        self.two, self.four = shown % 2, shown % 4
        self.three = (start + run * sub + shown + (3 * OFF - OFF)) % 3

    def holds(self, size, by):
        if size == 1:
            return jnp.ones_like(self.real) if by == 0 else None
        if abs(by) >= size:
            return None
        phase = {2: self.two, 3: self.three, 4: self.four}[size]
        return ((phase + by >= 0) & (phase + by < size)).astype(f32)

    def pooled(self, size, x):
        if size == 1:
            return x
        pair = x + jnp.where(self.two == 0, shifted(x, 1), shifted(x, -1))
        if size == 2:
            return pair
        if size == 4:
            return pair + jnp.where(self.four < 2, shifted(pair, 2), shifted(pair, -2))
        left, right = shifted(x, -1), shifted(x, 1)
        side = jnp.where(self.three == 0, shifted(x, 2), left)
        far = jnp.where(self.three == 2, shifted(x, -2), right)
        return x + side + far

    def both(self, x):
        return x + shifted(x, -1)


SIZES = (1, 2, 3, 4)
REACH = range(-3, 4)


def score_kernel(sizes, first_ref, ids_ref, dots_ref, bias_ref, scorer_ref, state_ref, sums_ref):
    rows, width, run, feat, vocab, kernel = sizes
    start = lax.axis_index("seq") * width
    bias = bias_ref[...]
    one, two, count, count4, bias_sum, cross = scales(first_ref, bias, feat)
    at = Places(ids_ref[...], start, run)
    real, own = at.real, at.own
    rate = 1.0 / (one * two)
    bias_score = jnp.sum(bias * scorer_ref[...], axis=1, keepdims=True) / two

    normed_score = real * bias_score + rate * dots_ref[13]
    counts = [jnp.maximum(at.pooled(b, real), 1.0) for b in SIZES]
    scores = [at.pooled(b, normed_score) / n for b, n in zip(SIZES, counts)]
    top = functools.reduce(jnp.maximum, scores)
    parts = [jnp.exp(s - top) for s in scores]
    whole = sum(parts)
    probs = [p / whole for p in parts]
    weights = [own * p / n for p, n in zip(probs, counts)]

    holds = {(b, d): at.holds(b, d) for b in SIZES for d in REACH}

    def blend(values):
        out = {}
        for d in REACH:
            terms = [v * holds[b, d] for b, v in zip(SIZES, values) if holds[b, d] is not None]
            out[d] = sum(terms)
        return out

    mixer = blend(weights)
    pair_count = jnp.maximum(at.pooled(2, real), 1.0)
    halver = {}
    even = at.two == 0
    for d in REACH:
        zero = jnp.zeros_like(real)
        ahead = shifted(mixer[d - 1], 1) if d - 1 >= -3 else zero
        behind = shifted(mixer[d + 1], -1) if d + 1 <= 3 else zero
        other = jnp.where(even, ahead, behind)
        halver[d] = jnp.where(at.inside, (mixer[d] + other) / pair_count, 0.0)

    bias_dot = dots_ref[14]
    normed_bias = real * (bias_sum / two) + rate * bias_dot
    lags = []
    for lag in range(6):
        later = shifted(real, lag)
        value = rate * rate * dots_ref[lag]
        value = value + (rate / two) * (bias_dot * later + real * shifted(bias_dot, lag))
        lags.append(value + (bias_sum / (two * two)) * (real * later))

    def gram(a, b):
        low, high = min(a, b), max(a, b)
        return shifted(lags[high - low], low) if high - low < 6 else None

    table = {(a, b): gram(a, b) for a in REACH for b in REACH if a <= b}

    def against(weighting):
        out = {}
        for a in REACH:
            out[a] = sum(
                weighting[b] * table[min(a, b), max(a, b)]
                for b in REACH if table[min(a, b), max(a, b)] is not None
            )
        return out

    with_mixed, with_half = against(mixer), against(halver)
    with_grad = {}
    grad_bias = dots_ref[12]
    cross_dots = {
        d: rate * dots_ref[6 + d + 2] + shifted(real, d) * (grad_bias / two) for d in range(-2, 4)
    }
    for d in REACH:
        here = cross_dots[d] if d >= -2 else jnp.zeros_like(real)
        before = shifted(cross_dots[d + 1], -1) if d + 1 <= 3 else jnp.zeros_like(real)
        with_grad[d] = jnp.where(even, here, before)

    def per_block(values, scale):
        out = []
        for b, n in zip(SIZES, counts):
            terms = [values[d] * holds[b, d] for d in REACH if holds[b, d] is not None]
            out.append(scale * sum(terms) / n)
        return out

    shared = own / pair_count
    bases = [per_block(with_grad, shared), per_block(with_half, shared), per_block(with_mixed, own)]

    def total_of(x):
        return jnp.sum(jnp.sum(x, axis=1, keepdims=True), axis=0, keepdims=True)

    first_of_pair = jnp.where(even & at.inside, 1.0, 0.0)
    mean_score = sum(p * s for p, s in zip(probs, scores))

    def bent(values):
        mean = sum(p * v for p, v in zip(probs, values))
        return total_of(own * (sum(p * s * v for p, s, v in zip(probs, scores, values)) - mean * mean_score))

    sums = [
        total_of(sum(own * mixer[d] * with_mixed[d] for d in REACH)),
        total_of(first_of_pair * sum(halver[d] * with_half[d] for d in REACH)),
        total_of(first_of_pair * sum(halver[d] * with_grad[d] for d in REACH)),
        bent(bases[0]), bent(bases[1]), bent(bases[2]),
        total_of(shared * at.both(grad_bias)),
        total_of(shared * sum(halver[d] * shifted(normed_bias, d) for d in REACH)),
        total_of(own * sum(mixer[d] * shifted(normed_bias, d) for d in REACH)),
    ]
    for i, b in enumerate(SIZES):
        state_ref[i] = weights[i]
        state_ref[4 + i] = probs[i]
        for f in range(3):
            state_ref[8 + 4 * f + i] = bases[f][i]
    sums_ref[...] = spread(sums, sums_ref.shape[0])


def back_kernel(
    sizes, first_ref, second_ref, ids_ref, state_ref, conv_ref, emb_ref, grad_ref, embed_ref, taps_ref, bias_ref,
    scorer_ref, out_ref, pay_ref, coef_ref, back_ref, acc_ref,
):
    rows, width, run, feat, vocab, kernel = sizes
    tiles = feat // LANES
    half = run // 2
    vr = rows * RUNS
    start = lax.axis_index("seq") * width
    bias = bias_ref[...]
    one, two, count, count4, bias_sum, cross = scales(first_ref, bias, feat)
    mixed_sum, half_sum, inner, bent_g, bent_h, bent_m, bias_g, bias_h, bias_m = picked(second_ref, 9)
    size, size4 = count * feat, count4 * feat
    three = jnp.sqrt(mixed_sum / size + EPS)
    four = jnp.sqrt(half_sum / (three * three) / size4 + EPS)
    fourth = (inner / three) / (four * four * four * size4)
    alpha = 1.0 / (three * four)
    beta = -fourth / (three * three)
    gamma = -(inner / four - fourth / three * half_sum) / (three * three * three * size)
    joint = alpha * (inner + bent_g) + beta * (half_sum + bent_h) + gamma * (mixed_sum + bent_m)
    rate = 1.0 / (one * two)
    normed_bias = count * bias_sum / two + rate * cross
    bias_back = (alpha * bias_g + beta * bias_h + gamma * bias_m - joint / size * normed_bias) / two
    inner_one = one * (joint * EPS / (two * two) - bias_back)
    first_coef = inner_one / (one * one * one * size)

    at = Places(ids_ref[...], start, run)
    probs = [state_ref[4 + i] for i in range(4)]
    weights = [state_ref[i] for i in range(4)]
    grads = [
        alpha * state_ref[8 + i] + beta * state_ref[12 + i] + gamma * state_ref[16 + i] for i in range(4)
    ]
    mean = sum(p * g for p, g in zip(probs, grads))
    spreading = jnp.zeros_like(probs[0])
    for i, b in enumerate(SIZES):
        bent = probs[i] * (grads[i] - mean)
        n = jnp.maximum(at.pooled(b, at.real), 1.0)
        spreading = spreading + at.pooled(b, jnp.where(at.inside, bent / n, 0.0))
    pair_real = at.pooled(2, at.real)
    pair_count = jnp.maximum(pair_real, 1.0)
    filled = (pair_real > 0).astype(f32)
    narrow = [rate * w for w in weights] + [rate * spreading, at.real]
    paired = [
        alpha / pair_count, alpha * filled, beta / (pair_count * pair_count), beta * filled / pair_count + gamma
    ]
    leak = jnp.sum(jnp.sum(spreading * at.real, axis=1, keepdims=True), axis=0, keepdims=True)

    for r in range(rows):
        sub = slice(r * RUNS, (r + 1) * RUNS)
        for j in range(-2, run + 2):
            which = range(6) if 0 <= j < run else (4, 5)
            for i in which:
                coef_ref[i, j + 2, sub, :] = jnp.broadcast_to(narrow[i][sub, j + OFF : j + OFF + 1], (RUNS, LANES))
        for k in range(half):
            for i in range(4):
                coef_ref[6 + i // 2, 2 * k + i % 2, sub, :] = jnp.broadcast_to(
                    paired[i][sub, 2 * k + OFF : 2 * k + OFF + 1], (RUNS, LANES)
                )

    acc_ref[...] = jnp.zeros_like(acc_ref)
    phase = (start + run * iota((RUNS, LANES), 0)) % 3
    at_phase = [phase == p for p in range(3)]

    def chosen(j, a, b, c):
        return jnp.where(at_phase[(0 - j) % 3], a, jnp.where(at_phase[(1 - j) % 3], b, c))

    full = (RUNS, LANES)
    alpha_all = jnp.broadcast_to(alpha, full)
    gamma_all = jnp.broadcast_to(gamma, full)
    fall = jnp.broadcast_to(rate * rate * joint / size, full)
    fall_bias = rate * joint / size / two

    def column(step, carry):
        r, tile = step // tiles, step % tiles
        sub = pl.ds(pl.multiple_of(r * RUNS, RUNS), RUNS)
        cols = pl.ds(pl.multiple_of(tile * LANES, LANES), LANES)
        taps = [jnp.broadcast_to(taps_ref[k : k + 1, cols], full) for k in range(kernel)]
        bias_row = bias_ref[:, cols]
        normed_row = jnp.broadcast_to(bias_row / two, full)
        fall_row = jnp.broadcast_to(bias_row * fall_bias, full)
        scorer = jnp.broadcast_to(scorer_ref[:, cols], full)
        zero = jnp.zeros(full, f32)

        def coef(i, j):
            return coef_ref[i, j, sub, :]

        u, triple, third, pairs, g_m, y3, gc = {}, {}, {}, {}, {}, {}, {}
        sums = [zero] * (kernel + 2)
        block = {}
        for j in range(-2, 2):
            u[j] = conv_ref[j + 2, sub, cols]
        triple[-2] = u[-2] + u[-1] + u[0]
        triple[-1] = u[-1] + u[0] + u[1]

        def window(j):
            near = [y3[i] for i in (j, j + 1, j + 2) if 0 <= i < run]
            return functools.reduce(lambda a, b: a + b, near) if near else zero

        def settle(s):
            nonlocal sums
            for j in (s, s - 1, s - 2):
                if j not in block:
                    block[j] = window(j)
            g = chosen(s, block[s], block[s - 1], block[s - 2])
            sigma = coef(4, s + 2)
            g = g + sigma * scorer
            if 0 <= s < run:
                g = g + lone[s]
                g = g - fall * u[s] - fall_row
            g = g * coef(5, s + 2)
            gc[s] = g
            for k in range(kernel):
                sums[k] = sums[k] + g * emb_ref[s - kernel + 1 + k + LEFT, sub, cols]
            sums[kernel] = sums[kernel] + g
            sums[kernel + 1] = sums[kernel + 1] + sigma * u[s]

        def finish(s):
            terms = [taps[k] * gc[s + kernel - 1 - k] for k in range(kernel) if s + kernel - 1 - k in gc]
            back_ref[s + LEFT, sub, cols] = functools.reduce(lambda a, b: a + b, terms)

        lone = {}
        settled = -2
        finished = -LEFT
        for quad in range(0, run, 4):
            for j in range(quad + 2, quad + 6):
                u[j] = conv_ref[j + 2, sub, cols]
            two_sums = [u[quad + 2 * p] + u[quad + 2 * p + 1] for p in range(2)]
            four_sum = two_sums[0] + two_sums[1]
            wide = zero
            for p in range(2):
                y = None
                xs = []
                for j in (quad + 2 * p, quad + 2 * p + 1):
                    triple[j] = u[j] + u[j + 1] + u[j + 2] if j % 2 else two_sums[p] + u[j + 2]
                    x = coef(0, j + 2) * u[j] + coef(1, j + 2) * two_sums[p]
                    x = x + coef(2, j + 2) * chosen(j, triple[j], triple[j - 1], triple[j - 2])
                    x = x + coef(3, j + 2) * four_sum
                    xs.append(x)
                y = xs[0] + xs[1]
                k = quad // 2 + p
                rowk = pair_rows(r, k, tile, half, tiles)
                scale_y = coef(6, 2 * k)
                out_ref[rowk, :] = scale_y * y + coef(6, 2 * k + 1) * normed_row
                q = scale_y * grad_ref[rowk, :] + coef(7, 2 * k) * y + coef(7, 2 * k + 1) * normed_row
                pair = zero
                for i, j in enumerate((quad + 2 * p, quad + 2 * p + 1)):
                    g = q + gamma_all * xs[i]
                    lone[j] = coef(0, j + 2) * g
                    y3[j] = coef(2, j + 2) * g
                    pair = coef(1, j + 2) * g if i == 0 else pair + coef(1, j + 2) * g
                    wide = coef(3, j + 2) * g if i + p == 0 else wide + coef(3, j + 2) * g
                for j in (quad + 2 * p, quad + 2 * p + 1):
                    lone[j] = lone[j] + pair
            for j in range(quad, quad + 4):
                lone[j] = lone[j] + wide
            last = quad + 3 - 2 if quad + 4 < run else run + 1
            while settled <= last:
                settle(settled)
                settled += 1
            done = settled - kernel if quad + 4 < run else run + RIGHT - 1
            while finished <= done:
                finish(finished)
                finished += 1
        for i in range(kernel + 2):
            acc_ref[i, :, cols] = acc_ref[i, :, cols] + sums[i]
        return carry

    lax.fori_loop(0, rows * tiles, column, 0)

    group = 8
    table = jnp.zeros((vocab, feat), f32)
    seen = jnp.zeros((vocab, LANES), f32)
    span = run + LEFT + RIGHT
    for first in range(0, emb_ref.shape[0], group):
        marks, inside = [], []
        for i in range(first, first + group):
            column_ids = ids_ref[:, i + OFF - LEFT : i + OFF - LEFT + 1]
            marks.append((column_ids == iota((vr, vocab), 1)).astype(f32))
            inside.append(jnp.full((vr, LANES), 1.0 if LEFT <= i < LEFT + run else 0.0, f32))
        onehot = jnp.concatenate(marks, axis=0).astype(jnp.bfloat16)
        if first + group > span:
            back_ref[span : first + group] = jnp.zeros((first + group - span, vr, feat), f32)
        value = back_ref[first : first + group].reshape(group * vr, feat)
        high = value.astype(jnp.bfloat16)
        low = (value - high.astype(f32)).astype(jnp.bfloat16)
        table = table + lax.dot_general(onehot, high, TN, preferred_element_type=f32)
        table = table + lax.dot_general(onehot, low, TN, preferred_element_type=f32)
        ones = jnp.concatenate(inside, axis=0).astype(jnp.bfloat16)
        seen = seen + lax.dot_general(onehot, ones, TN, preferred_element_type=f32)
    for tile in range(tiles):
        cols = slice(tile * LANES, (tile + 1) * LANES)
        pay_ref[:, cols] = table[:, cols] - first_coef * seen * embed_ref[:, cols]

    pay_ref[:, feat : feat + LANES] = jnp.zeros((vocab, LANES), f32)
    for i in range(kernel + 2):
        row = jnp.sum(acc_ref[i], axis=0, keepdims=True)
        if i == kernel:
            row = row * one
        if i == kernel + 1:
            row = row + bias * (leak / two)
        for tile in range(tiles):
            place = i * tiles + tile
            pay_ref[place : place + 1, feat : feat + LANES] = row[:, tile * LANES : (tile + 1) * LANES]


def exchanged(x, n):
    return lax.all_to_all(x, AXES, 0, 0, tiled=True)


def partner(x, axis, step):
    n = lax.axis_size(axis)
    return lax.ppermute(x, axis, [(i, i ^ step) for i in range(n)])


def summed_over_devices(x):
    steps = []
    step = 1
    while step < lax.axis_size("seq"):
        steps.append(step)
        step *= 2
    here = lax.axis_index("seq")
    for step in steps:
        side = (here // step) % 2
        parts = x.reshape(2, x.shape[0] // 2, x.shape[1])
        send = lax.dynamic_index_in_dim(parts, 1 - side, 0, False)
        keep = lax.dynamic_index_in_dim(parts, side, 0, False)
        x = keep + partner(send, "seq", step)
    n = lax.axis_size("rows")
    part = x.reshape(n, x.shape[0] // n, x.shape[1])
    part = jnp.sum(lax.all_to_all(part, "rows", 0, 0, tiled=True), axis=0)
    part = jnp.broadcast_to(part[None], (n,) + part.shape)
    x = lax.all_to_all(part, "rows", 0, 0, tiled=True).reshape(x.shape)
    for step in steps[::-1]:
        side = (here // step) % 2
        other = partner(x, "seq", step)
        x = jnp.where(side == 0, jnp.concatenate([x, other]), jnp.concatenate([other, x]))
    return x


def on_device(byte_ids, lengths, embed, conv_weight, conv_bias, score_weight, out_grad):
    rows, width = byte_ids.shape
    vocab, feat = embed.shape
    kernel = conv_weight.shape[0]
    run = width // RUNS
    half = width // 2
    vr = rows * RUNS
    sizes = (rows, width, run, feat, vocab, kernel)
    count = lax.axis_size("seq")
    devices = count * lax.axis_size("rows")
    span = -(-(run + LEFT + RIGHT) // 8) * 8
    struct = jax.ShapeDtypeStruct
    params = pltpu.CompilerParams(vmem_limit_bytes=60 * 1024 * 1024)

    up = [(i, i + 1) for i in range(count - 1)]
    left = lax.ppermute(byte_ids, "seq", up)
    right = lax.ppermute(byte_ids, "seq", [(j, i) for i, j in up])
    own = jnp.pad(byte_ids.reshape(vr, run), ((0, 0), (0, LANES - run)))
    bias = conv_bias.reshape(1, feat)
    scorer = score_weight.reshape(1, feat)
    grad = as_tiles(out_grad.reshape(rows * half, feat))

    split, table = pl.pallas_call(
        prep_kernel,
        out_shape=(struct((2, vocab, feat), jnp.bfloat16), struct((16, vocab), f32)),
        in_specs=[VMEM] * 4, out_specs=(VMEM, VMEM), compiler_params=params, name="prep",
    )(embed, conv_weight, bias, scorer)

    emb, conv, ids, dots, first = pl.pallas_call(
        functools.partial(stats_kernel, sizes),
        out_shape=(
            struct((span, vr, feat), f32), struct((run + 12, vr, feat), f32), struct((vr, LANES), jnp.int32),
            struct((15, vr, LANES), f32), struct((devices, 1, LANES), f32),
        ),
        in_specs=[VMEM, VMEM, VMEM, SMEM] + [VMEM] * 5, out_specs=(VMEM,) * 5, compiler_params=params, name="stats",
    )(own, left, right, lengths, split, table, conv_weight, bias, grad)
    first = exchanged(first, devices)

    state, second = pl.pallas_call(
        functools.partial(score_kernel, sizes),
        out_shape=(struct((20, vr, LANES), f32), struct((devices, 1, LANES), f32)),
        in_specs=[VMEM] * 5, out_specs=(VMEM, VMEM), compiler_params=params, name="score",
    )(first, ids, dots, bias, scorer)
    second = exchanged(second, devices)

    blocks, pay = pl.pallas_call(
        functools.partial(back_kernel, sizes),
        out_shape=(struct((rows * half * feat // LANES, LANES), f32), struct((vocab, feat + LANES), f32)),
        in_specs=[VMEM] * 11, out_specs=(VMEM, VMEM), compiler_params=params, name="back",
        scratch_shapes=[
            pltpu.VMEM((8, run + 4, vr, LANES), f32), pltpu.VMEM((span, vr, feat), f32),
            pltpu.VMEM((kernel + 2, RUNS, feat), f32),
        ],
    )(first, second, ids, state, conv, emb, grad, embed, conv_weight, bias, scorer)

    pay = summed_over_devices(pay)
    tiles = feat // LANES
    extra = pay[: (kernel + 2) * tiles, feat:].reshape(kernel + 2, feat)
    return (
        from_tiles(blocks, feat).reshape(rows, half, feat), pay[:, :feat], extra[:kernel], extra[kernel], extra[kernel + 1]
    )


def solution(mesh):
    placed = (P("rows", "seq"), P("rows"), P(), P(), P(), P(), P("rows", "seq", None))
    return jax.shard_map(
        on_device,
        mesh=mesh,
        in_specs=placed,
        out_specs=(P("rows", "seq", None), P(), P(), P(), P()),
        check_vma=False,
    )
```

time: 866 us -> 142 us (0.16); the launches traced: 855 us -> 141 us
  other arithmetic: 253 us -> 1.2 us
  blocking collectives: 288 us -> 38.1 us
  waiting for transfers between devices: 129 us -> 23.3 us
  local copies, waits for them, and re-layouts: 112 us -> 8.34 us
  Pallas kernels: 0 us -> 62.2 us
  matrix products: 44.1 us -> 0 us
  between operations: 24.8 us -> 0.8 us
    psum x7 -> x0, blocking collectives: 288 us -> none  [the longest x4 166 us: stream_scale(): lax.psum((jnp.sum(element_numbers * element_numbers), jnp.sum(mask)), ('r...]
    psum x1 -> x0, waiting for transfers between devices: 129 us -> none  [on_device(): summed = lax.psum((g_table, g_taps, g_bias, g_score), ('rows', 'seq'))]
    reduce_sum x16 -> x1, other arithmetic: 113 us -> 0.02 us  [summed_over_devices(): part = jnp.sum(lax.all_to_all(part, 'rows', 0, 0, tiled=True), axis=0)]
    pallas_call x0 -> x4, Pallas kernels: none -> 62.2 us  [the longest x1 30.6 us: on_device(): pl.pallas_call(functools.partial(back_kernel, sizes), out_shape=(struct((...]
    reshape x7 -> x3, local copies, waits for them, and re-layouts: 57.8 us -> 3.31 us  [the longest x1 1.27 us: on_device(): bias = conv_bias.reshape(1, feat)]
    div x8 -> x0, other arithmetic: 49.2 us -> none  [the longest x3 27.9 us: pool_blocks(): pooled.append(total / jnp.maximum(count, 1.0)[:, :, None])]
    dot_general x4 -> x0, matrix products: 44.1 us -> none  [the longest x2 31.8 us: mix_blocks(): jnp.einsum('brwd,d->brw', pooled, score_weight, precision=high_precision)]
    all_to_all x0 -> x3, blocking collectives: none -> 38.1 us  [the longest x1 16.3 us: exchanged(): return lax.all_to_all(x, AXES, 0, 0, tiled=True)]
  transfers between devices with their start and end apart: 3 -> 7, of which waited for: 1 -> 5; matrix products, arithmetic and copies ran while one was open for 1% -> 3% of each run, Pallas kernels for 0% -> 2%
where the time goes in v1:
time: 142 us; the launch traced here: 141 us
  Pallas kernels  62.2 us (44%)
  blocking collectives  38.1 us (27%)
  waiting for transfers between devices  23.3 us (16%)
  local copies, waits for them, and re-layouts  8.34 us (6%)
  starting transfers between devices  7.49 us (5%)
    pallas_call x1, Pallas kernels, on_device(): pl.pallas_call(functools.partial(back_kernel, sizes), out_shape=(struct((...  30.6 us
    pallas_call x1, Pallas kernels, on_device(): pl.pallas_call(functools.partial(stats_kernel, sizes), out_shape=(struct(...  25.9 us
    all_to_all x1, blocking collectives, exchanged(): return lax.all_to_all(x, AXES, 0, 0, tiled=True)  16.3 us
    ppermute x4, waiting for transfers between devices, partner(): return lax.ppermute(x, axis, [(i, i ^ step) for i in range(n)])  16.1 us
    all_to_all x1, blocking collectives, summed_over_devices(): x = lax.all_to_all(part, 'rows', 0, 0, tiled=True).reshape(x.shape)  11.2 us
    all_to_all x1, blocking collectives, summed_over_devices(): part = jnp.sum(lax.all_to_all(part, 'rows', 0, 0, tiled=True), axis=0)  10.6 us
    all_to_all x1, waiting for transfers between devices, exchanged(): return lax.all_to_all(x, AXES, 0, 0, tiled=True)  7.13 us
    pallas_call x1, Pallas kernels, on_device(): pl.pallas_call(prep_kernel, out_shape=(struct((2, vocab, feat), jnp.bfloa...  3.11 us
  transfers between devices with their start and end apart: 7, of which 5 were waited for; matrix products, arithmetic and copies ran while one was open for 3% of the time, Pallas kernels for 2%

profile of v1, /device:TPU:0, one launch (start us, length us, event | category | flops | bytes accessed | tf_op | source)
XLA Modules:
  0.0 141.4 jit_solution(10034707594728581255)
XLA Ops:
  0.6 2.4 %collective-permute-start = (s32[4,512]{1,0:T(4,128)}, s32[4,512]{1,0:T(4,128)S(1)}, u32[]{:S(2)}, u32[]{:S(2)}) collective-permute-start(s32[4,512]{1,0:T(4,128)} %param.7), channel_id=1, source_target_pairs={{0,1},{1,2},{2,3},{4,5},{5,6},{6,7},{8,9},{9,10},{10,11},{12,13},{... | collective-permute-start | bytes 24584 | tf_op jit(solution)/shard_map/ppermute | solution.py:636
  3.0 1.3 collective-permute-start.1
  4.3 0.8 reshape.44
  5.1 1.3 reshape.45.bias_ref
  6.3 1.3 reshape.46.scorer_ref
  7.6 0.6 pad.4.own_ref
  8.2 3.1 %prep.1 = (bf16[2,256,768]{2,1,0:T(8,128)(2,1)}, f32[16,256]{1,0:T(8,128)}) custom-call(f32[256,768]{1,0:T(8,128)} %embed_ref.3, f32[4,768]{1,0:T(4,128)} %taps_ref.5, f32[1,768]{1,0:T(1,128)} %reshape.45.bias_ref, f32[1,768]{1,0:T(1,128)} %reshape.46.scorer_ref), custom_call_target="tpu_custom_call" | custom-call | tf_op jit(solution)/shard_map/prep/pallas_call | solution.py:643
  11.3 0.0 collective-permute-done.left_ref
  11.3 0.6 copy-done.1
  11.9 25.9 %stats.1 = (f32[72,32,768]{2,1,0:T(8,128)}, f32[76,32,768]{2,1,0:T(8,128)}, s32[32,128]{1,0:T(8,128)}, f32[15,32,128]{2,1,0:T(8,128)}, f32[32,1,128]{2,1,0:T(1,128)}) custom-call(s32[32,128]{1,0:T(8,128)} %pad.4.own_ref, s32[4,512]{1,0:T(4,128)} %copy-done.1, s32[4,512]{1,0:T(4,128)} %copy-done.2, s32[4]{0:T(128)} %len_ref.1, ...), custom_call_target="tpu_custom_call" | custom-call | tf_op jit(solution)/shard_map/stats/pallas_call | solution.py:649
  37.8 16.3 %all_to_all.20.first_ref = f32[32,1,128]{2,1,0:T(1,128)} all-to-all(f32[32,1,128]{2,1,0:T(1,128)} %get-tuple-element.18), channel_id=1, replica_groups=mesh['rows'=8,'seq'=4] {'rows','seq'}, dimensions={0} | all-to-all | bytes 32768 | tf_op jit(solution)/shard_map/all_to_all | solution.py:588
  54.1 2.6 %score.1 = (f32[20,32,128]{2,1,0:T(8,128)}, f32[32,1,128]{2,1,0:T(1,128)}) custom-call(f32[32,1,128]{2,1,0:T(1,128)} %all_to_all.20.first_ref, s32[32,128]{1,0:T(8,128)} %get-tuple-element.19.ids_ref, f32[15,32,128]{2,1,0:T(8,128)} %get-tuple-element.20.dots_ref, f32[1,768]{1,0:T(1,128)} %reshape.45.bias_ref, f32[1,768]{1,0:T(1,128)} %reshape.46.scorer_ref), custom_call_target="tpu_custom_call" | custom-call | tf_op jit(solution)/shard_map/score/pallas_call | solution.py:659
  56.8 2.6 %all-to-all-start.1 = ((f32[32,1,128]{2,1,0:T(1,128)}), f32[32,1,128]{2,1,0:T(1,128)S(1)}, u32[]{:S(2)}, u32[]{:S(2)}) async-start(f32[32,1,128]{2,1,0:T(1,128)} %get-tuple-element.21), calls=%async_computation.1 | async-start | bytes 32768 | tf_op jit(solution)/shard_map/all_to_all | solution.py:588
  59.4 7.1 %all-to-all-done.1.second_ref = f32[32,1,128]{2,1,0:T(1,128)S(1)} async-done(((f32[32,1,128]{2,1,0:T(1,128)}), f32[32,1,128]{2,1,0:T(1,128)S(1)}, u32[]{:S(2)}, u32[]{:S(2)}) %all-to-all-start.1) | async-done | bytes 16416 | tf_op jit(solution)/shard_map/all_to_all | solution.py:588
  66.5 0.6 copy-done
  67.1 30.6 %back.1 = (f32[6144,128]{1,0:T(8,128)}, f32[256,896]{1,0:T(8,128)}) custom-call(f32[32,1,128]{2,1,0:T(1,128)} %all_to_all.20.first_ref, f32[32,1,128]{2,1,0:T(1,128)} %copy-done, s32[32,128]{1,0:T(8,128)} %get-tuple-element.19.ids_ref, f32[20,32,128]{2,1,0:T(8,128)} %get-tuple-element.22.state_ref, f32[76,32,768]{2,1,0:T(8,128)} %get-tuple-element.23.conv_ref, ...), custom_call_target="tpu_custom_call" | custom-call | tf_op jit(solution)/shard_map/back/pallas_call | solution.py:666
  97.7 1.0 dynamic-slice_bitcast_fusion
  98.7 0.1 collective-permute-start.2
  98.8 1.8 %collective-permute-done.2 = f32[128,896]{1,0:T(8,128)S(1)} collective-permute-done((f32[128,896]{1,0:T(8,128)S(1)}, f32[128,896]{1,0:T(8,128)S(1)}, u32[]{:S(2)}, u32[]{:S(2)}) %collective-permute-start.2) | collective-permute-done | bytes 458784 | tf_op jit(solution)/shard_map/ppermute | solution.py:593
  100.6 1.1 bitcast_add_fusion
  101.7 0.6 collective-permute-start.3
  102.3 7.1 %collective-permute-done.3 = f32[64,896]{1,0:T(8,128)S(1)} collective-permute-done((f32[64,896]{1,0:T(8,128)S(1)}, f32[64,896]{1,0:T(8,128)S(1)}, u32[]{:S(2)}, u32[]{:S(2)}) %collective-permute-start.3) | collective-permute-done | bytes 229408 | tf_op jit(solution)/shard_map/ppermute | solution.py:593
  109.4 10.6 %all_to_all.21 = f32[8,8,896]{2,1,0:T(8,128)S(1)} all-to-all(f32[8,8,896]{2,1,0:T(8,128)S(1)} %fusion), channel_id=1, replica_groups=mesh['rows'=8,'seq'=4] {'rows'}, dimensions={0} | all-to-all | bytes 458752 | tf_op jit(solution)/shard_map/all_to_all | solution.py:611
  120.1 11.2 %all_to_all.22 = f32[8,8,896]{2,1,0:T(8,128)S(1)} all-to-all(f32[8,8,896]{2,1,0:T(8,128)S(1)} %broadcast_in_dim.2), channel_id=1, replica_groups=mesh['rows'=8,'seq'=4] {'rows'}, dimensions={0} | all-to-all | bytes 458752 | tf_op jit(solution)/shard_map/all_to_all | solution.py:613
  131.3 0.5 collective-permute-start.4
  131.8 5.5 %collective-permute-done.4 = f32[64,896]{1,0:T(8,128)S(1)} collective-permute-done((f32[64,896]{1,0:T(8,128)S(1)}, f32[64,896]{1,0:T(8,128)S(1)}, u32[]{:S(2)}, u32[]{:S(2)}) %collective-permute-start.4) | collective-permute-done | bytes 229408 | tf_op jit(solution)/shard_map/ppermute | solution.py:593
  137.3 0.1 collective-permute-start.5
  137.4 1.8 %collective-permute-done.5 = f32[128,896]{1,0:T(8,128)S(1)} collective-permute-done((f32[128,896]{1,0:T(8,128)S(1)}, f32[128,896]{1,0:T(8,128)S(1)}, u32[]{:S(2)}, u32[]{:S(2)}) %collective-permute-start.5) | collective-permute-done | bytes 458784 | tf_op jit(solution)/shard_map/ppermute | solution.py:593
  139.2 0.1 maximum_select_fusion
  139.3 0.9 slice.26
  140.2 0.6 slice_bitcast_fusion
  140.8 0.6 slice.23
  (11 shorter events, 0.1 us)
Async XLA Ops:
  0.6 10.7 %collective-permute-start = (s32[4,512]{1,0:T(4,128)}, s32[4,512]{1,0:T(4,128)S(1)}, u32[]{:S(2)}, u32[]{:S(2)}) collective-permute-start(s32[4,512]{1,0:T(4,128)} %param.7), channel_id=1, source_target_pairs={{0,1},{1,2},{2,3},{4,5},{5,6},{6,7},{8,9},{9,10},{10,11},{12,13},{... | collective-permute-start | bytes 24584 | tf_op jit(solution)/shard_map/ppermute | solution.py:636
  3.0 8.3 %collective-permute-start.1 = (s32[4,512]{1,0:T(4,128)}, s32[4,512]{1,0:T(4,128)S(1)}, u32[]{:S(2)}, u32[]{:S(2)}) collective-permute-start(s32[4,512]{1,0:T(4,128)} %param.7), channel_id=1, source_target_pairs={{1,0},{2,1},{3,2},{5,4},{6,5},{7,6},{9,8},{10,9},{11,10},{13,12},{... | collective-permute-start | bytes 24584 | tf_op jit(solution)/shard_map/ppermute | solution.py:637
  11.3 0.6 copy-start.1
  11.3 0.6 copy-start.2
  56.8 9.7 %all-to-all-start.1 = ((f32[32,1,128]{2,1,0:T(1,128)}), f32[32,1,128]{2,1,0:T(1,128)S(1)}, u32[]{:S(2)}, u32[]{:S(2)}) async-start(f32[32,1,128]{2,1,0:T(1,128)} %get-tuple-element.21), calls=%async_computation.1 | async-start | bytes 32768 | tf_op jit(solution)/shard_map/all_to_all | solution.py:588
  66.5 0.6 copy-start
  98.7 1.9 %collective-permute-start.2 = (f32[128,896]{1,0:T(8,128)S(1)}, f32[128,896]{1,0:T(8,128)S(1)}, u32[]{:S(2)}, u32[]{:S(2)}) collective-permute-start(f32[128,896]{1,0:T(8,128)S(1)} %dynamic-slice_bitcast_fusion), channel_id=1, source_target_pairs={{0,1},{1,0},{2,3},{3,2},{4,5},{5,4},{6,7},{7,6},{8,9},{9,8},{10,11... | collective-permute-start | bytes 1376264 | tf_op jit(solution)/shard_map/ppermute | solution.py:593
  101.7 7.7 %collective-permute-start.3 = (f32[64,896]{1,0:T(8,128)S(1)}, f32[64,896]{1,0:T(8,128)S(1)}, u32[]{:S(2)}, u32[]{:S(2)}) collective-permute-start(f32[64,896]{1,0:T(8,128)S(1)} %dynamic-slice_bitcast_fusion.1), channel_id=1, source_target_pairs={{0,2},{1,3},{2,0},{3,1},{4,6},{5,7},{6,4},{7,5},{8,10},{9,11},{10,... | collective-permute-start | bytes 688136 | tf_op jit(solution)/shard_map/ppermute | solution.py:593
  131.3 6.0 %collective-permute-start.4 = (f32[64,896]{1,0:T(8,128)S(1)}, f32[64,896]{1,0:T(8,128)S(1)}, u32[]{:S(2)}, u32[]{:S(2)}) collective-permute-start(f32[64,896]{1,0:T(8,128)S(1)} %bitcast.35), channel_id=1, source_target_pairs={{0,2},{1,3},{2,0},{3,1},{4,6},{5,7},{6,4},{7,5},{8,10},{9,11},{10,... | collective-permute-start | bytes 688136 | tf_op jit(solution)/shard_map/ppermute | solution.py:593
  137.3 1.9 %collective-permute-start.5 = (f32[128,896]{1,0:T(8,128)S(1)}, f32[128,896]{1,0:T(8,128)S(1)}, u32[]{:S(2)}, u32[]{:S(2)}) collective-permute-start(f32[128,896]{1,0:T(8,128)S(1)} %maximum_select_fusion.1), channel_id=1, source_target_pairs={{0,1},{1,0},{2,3},{3,2},{4,5},{5,4},{6,7},{7,6},{8,9},{9,8},{10,11... | collective-permute-start | bytes 1376264 | tf_op jit(solution)/shard_map/ppermute | solution.py:593

commit v2 on v1

v2 whole, which is shorter than its diff:
```python
import functools

import jax
import jax.numpy as jnp
from jax import lax
from jax.experimental import pallas as pl
from jax.experimental.pallas import tpu as pltpu
from jax.sharding import PartitionSpec as P

f32 = jnp.float32
EPS = 1e-06
LANES = 128
WIDE = 256
RUNS = 8
OFF = 8
LEFT, RIGHT = 5, 2
NT = (((1,), (1,)), ((), ()))
AXES = ("rows", "seq")
VMEM = pl.BlockSpec(memory_space=pltpu.VMEM)
HBM = pl.BlockSpec(memory_space=pltpu.HBM)


def iota(shape, dim):
    return lax.broadcasted_iota(jnp.int32, shape, dim)


def shifted(x, by):
    return x if by == 0 else pltpu.roll(x, (-by) % LANES, 1)


BIAS, SCORER = 4, 5
IDS, WEIGHTS, SEEN = 15, 16, 18


def stats_kernel(
    sizes, own_hbm, left_hbm, right_hbm, len_hbm, embed_hbm, taps_hbm, bias_hbm, scorer_hbm, grad_hbm,
    emb_hbm, conv_hbm, cot_hbm, mark_hbm, pack_ref, sums_ref,
    own_ref, left_ref, right_ref, len_ref, embed_ref, taps_ref, bias_ref, scorer_ref, grad_ref,
    split_ref, table_ref, rows_ref, mark_ref, turn_ref, spot_ref, line_ref, seen_ref, order_ref, run_ref, *rest,
):
    rows, width, run, feat, vocab, kernel = sizes
    pairs = feat // WIDE
    emb_ref, conv_ref = rest[:pairs], rest[pairs : 2 * pairs]
    cot_ref, sems = rest[2 * pairs :]
    half = run // 2
    vr = rows * RUNS
    span = mark_ref.shape[0] // vr
    sources = (own_hbm, left_hbm, right_hbm, len_hbm, embed_hbm, taps_hbm, bias_hbm, scorer_hbm, grad_hbm)
    targets = (own_ref, left_ref, right_ref, len_ref, embed_ref, taps_ref, bias_ref, scorer_ref, grad_ref)
    fetch = [pltpu.make_async_copy(a, b, sems.at[0, i]) for i, (a, b) in enumerate(zip(sources, targets))]
    for copy in fetch:
        copy.start()
    start = lax.axis_index("seq") * width
    lane = iota((RUNS, LANES), 1)
    sub = iota((RUNS, LANES), 0)
    base = start + run * sub
    back = (OFF - run) % LANES

    for copy in fetch[:4]:
        copy.wait()
    for r in range(rows):
        for s in range(RUNS):
            line = own_ref[r : r + 1, s * run // LANES * LANES : (s * run // LANES + 1) * LANES]
            shift = -(s * run % LANES) % LANES
            line = jnp.broadcast_to(line, (RUNS, LANES))
            line = pltpu.roll(line, shift, 1) if shift else line
            run_ref[r * RUNS + s : r * RUNS + s + 1, :] = line[0:1]
    for r in range(rows):
        own = run_ref[r * RUNS : (r + 1) * RUNS, :]
        before = pltpu.roll(pltpu.roll(own, 1, 0), back, 1)
        edge = pltpu.roll(jnp.broadcast_to(left_ref[r : r + 1, width - LANES : width], (RUNS, LANES)), OFF, 1)
        before = jnp.where(sub == 0, edge, before)
        after = pltpu.roll(pltpu.roll(own, RUNS - 1, 0), OFF + run, 1)
        edge = pltpu.roll(jnp.broadcast_to(right_ref[r : r + 1, 0:LANES], (RUNS, LANES)), OFF + run, 1)
        after = jnp.where(sub == RUNS - 1, edge, after)
        ids = jnp.where(lane < OFF, before, jnp.where(lane < OFF + run, pltpu.roll(own, OFF, 1), after))
        place = base + lane - OFF
        real = (place >= 0) & (place < len_ref[r])
        real = real & (lane >= OFF - LEFT) & (lane < OFF + run + RIGHT)
        pack_ref[IDS, r * RUNS : (r + 1) * RUNS, :] = jnp.where(real, ids, -1).astype(f32)

    group = LANES // (rows * RUNS)
    ids = pack_ref[IDS].astype(jnp.bfloat16)
    eye = (iota((LANES, LANES), 0) == iota((LANES, LANES), 1)).astype(f32).astype(jnp.bfloat16)
    turned = lax.dot_general(eye, ids, NT, preferred_element_type=f32).astype(jnp.bfloat16)
    lined = jnp.zeros((line_ref.shape[0], LANES), f32)
    for i in range(group):
        shape = (line_ref.shape[0], LANES)
        take = (iota(shape, 1) == iota(shape, 0) * group + (i + OFF - LEFT)).astype(f32).astype(jnp.bfloat16)
        put = (iota((vr, LANES), 1) == iota((vr, LANES), 0) + i * vr).astype(f32).astype(jnp.bfloat16)
        some = jnp.dot(take, turned, preferred_element_type=f32).astype(jnp.bfloat16)
        lined = lined + jnp.dot(some, put, preferred_element_type=f32)
    line_ref[...] = lined

    def mark(step, carry):
        for r in range(rows):
            ids = pack_ref[IDS, r * RUNS : (r + 1) * RUNS, :].astype(jnp.int32)
            for i in range(group):
                where = jnp.full((RUNS, LANES), step * group + (i + OFF - LEFT), jnp.int32)
                byte = jnp.take_along_axis(ids, where, axis=1)
                for part in range(vocab // LANES):
                    spot_ref[i, r * RUNS : (r + 1) * RUNS, part * LANES : (part + 1) * LANES] = jnp.where(
                        byte == lane + part * LANES, 1.0, 0.0
                    )
        at = pl.ds(pl.multiple_of(step * LANES, LANES), LANES)
        mark_ref[at, :] = spot_ref[...].reshape(LANES, vocab).astype(jnp.bfloat16)
        bytes_here = jnp.broadcast_to(line_ref[pl.ds(step, 1), :], (vocab, LANES))
        column = jnp.where(bytes_here == iota((vocab, LANES), 0).astype(f32), 1.0, 0.0)
        turn_ref[:, at] = column.astype(jnp.bfloat16)
        line = step * group + iota((1, LANES), 1) // vr
        inside = ((line >= LEFT) & (line < LEFT + run)).astype(f32)
        seen_ref[...] = seen_ref[...] + column * inside
        return carry

    seen_ref[...] = jnp.zeros_like(seen_ref)
    lax.fori_loop(0, span // group, mark, 0)
    for i in range(vocab // vr):
        seen = jnp.sum(seen_ref[i * vr : (i + 1) * vr, :], axis=1, keepdims=True)
        pack_ref[SEEN + i] = jnp.broadcast_to(seen, (vr, LANES))
    keep_mark = pltpu.make_async_copy(turn_ref, mark_hbm, sems.at[1, 0])
    keep_mark.start()
    for copy in fetch[4:8]:
        copy.wait()
    embed = embed_ref[...]
    high, low = in_two(embed)
    split_ref[0] = high
    split_ref[1] = low

    taps = taps_ref[...]
    bias = bias_ref[...].reshape(1, feat)
    scorer = scorer_ref[...].reshape(1, feat)
    rows_ref[0:kernel, :] = taps
    rows_ref[BIAS : BIAS + 1, :] = bias
    rows_ref[SCORER : SCORER + 1, :] = scorer
    rows_ref[SCORER + 1 : 8, :] = jnp.zeros((7 - SCORER, feat), f32)
    for tile in range(feat // LANES):
        at = slice(tile % 4 * 8, tile % 4 * 8 + 8)
        pack_ref[WEIGHTS + tile // 4, at, :] = rows_ref[:, tile * LANES : (tile + 1) * LANES]

    def inner(a, b):
        return lax.dot_general(a, b, NT, preferred_element_type=f32)

    scaled = in_two(jnp.concatenate([taps * scorer, taps * bias], axis=0))
    ones = jnp.ones((8, feat), jnp.bfloat16)
    squares = in_two(embed * embed)
    table_ref[0:8, :] = inner(scaled[0], high) + (inner(scaled[0], low) + inner(scaled[1], high))
    table_ref[8:16, :] = inner(ones, squares[0]) + inner(ones, squares[1])

    steps = rows * (WIDE // LANES)
    lines = span // steps

    def embedding(pair, step):
        at = pl.ds(pl.multiple_of(step * (lines * vr), 16), lines * vr)
        cols = slice(pair * WIDE, (pair + 1) * WIDE)
        total = jnp.dot(mark_ref[at, :], split_ref[0, :, cols], preferred_element_type=f32)
        total = total + jnp.dot(mark_ref[at, :], split_ref[1, :, cols], preferred_element_type=f32)
        emb_ref[pair][pl.ds(step * lines, lines)] = total.reshape(lines, vr, WIDE)

    def convolution(pair, step):
        r, tile = step // (WIDE // LANES), step % (WIDE // LANES)
        at = (pl.ds(pl.multiple_of(r * RUNS, RUNS), RUNS), pl.ds(pl.multiple_of(tile * LANES, LANES), LANES))
        cols = pl.ds(pl.multiple_of(pair * WIDE + tile * LANES, LANES), LANES)
        length = len_ref[r]
        taps = [jnp.broadcast_to(rows_ref[k : k + 1, cols], (RUNS, LANES)) for k in range(kernel)]
        window = [emb_ref[pair][k, at[0], at[1]] for k in range(kernel - 1)]
        for j in range(-2, run + 2):
            window.append(emb_ref[pair][j + LEFT, at[0], at[1]])
            total = taps[0] * window[0]
            for k in range(1, kernel):
                total = total + taps[k] * window[k]
            window = window[1:]
            real = base < length - j
            if j < 0:
                real = real & (base >= -j)
            conv_ref[pair][j + 2, at[0], at[1]] = jnp.where(real, total, 0.0)

    size = RUNS * half
    order = iota((size, size), 0)
    order = (iota((size, size), 1) == order % RUNS * half + order // RUNS).astype(f32)
    order_ref[...] = order.astype(jnp.bfloat16)

    def reorder(r):
        order = order_ref[...]
        at = pl.ds(pl.multiple_of(r * RUNS, RUNS), RUNS)
        for pair in range(pairs):
            cols = slice(pair * WIDE, (pair + 1) * WIDE)
            parts = in_two(grad_ref[pl.ds(pl.multiple_of(r * size, 8), size), cols])
            moved = jnp.dot(order, parts[0], preferred_element_type=f32)
            moved = moved + jnp.dot(order, parts[1], preferred_element_type=f32)
            cot_ref[:, at, cols] = moved.reshape(half, RUNS, WIDE)

    keeps = [keep_mark]
    for stage in range(pairs + 1):

        def both(step, carry):
            if stage < pairs:
                embedding(stage, step)
            if stage > 0:
                convolution(stage - 1, step)
            return carry

        lax.fori_loop(0, steps, both, 0)
        if stage < pairs:
            cols = pl.ds(stage * WIDE, WIDE)
            keeps.append(pltpu.make_async_copy(emb_ref[stage], emb_hbm.at[:, :, cols], sems.at[1, 1 + stage]))
            keeps[-1].start()
        if stage > 0:
            cols = pl.ds((stage - 1) * WIDE, WIDE)
            keeps.append(
                pltpu.make_async_copy(conv_ref[stage - 1], conv_hbm.at[:, :, cols], sems.at[2, stage - 1])
            )
            keeps[-1].start()

    block = 4
    slices = run + 4
    zero = jnp.zeros((RUNS, LANES), f32)
    tile_at = [(t * LANES // WIDE, slice(t * LANES % WIDE, t * LANES % WIDE + LANES)) for t in range(feat // LANES)]

    def lagged(r, carry):
        at = pl.ds(pl.multiple_of(r * RUNS, RUNS), RUNS)
        values = [zero] * 6
        for first in range(0, slices, block):
            acc = {}
            for tile, (pair, cols) in enumerate(tile_at):
                u = [conv_ref[pair][first + i, at, cols] for i in range(min(block + 5, slices - first))]
                for i in range(block):
                    for lag in range(min(6, slices - first - i)):
                        term = u[i] * u[i + lag]
                        acc[i, lag] = term if tile == 0 else acc[i, lag] + term
            for i, lag in acc:
                here = lane == first + (i + OFF - 2)
                values[lag] = jnp.where(here, jnp.sum(acc[i, lag], axis=1, keepdims=True), values[lag])
        for lag in range(6):
            pack_ref[lag, at, :] = values[lag]
        reorder(r)
        return carry

    fetch[8].wait()
    lax.fori_loop(0, rows, lagged, 0)
    keeps.append(pltpu.make_async_copy(cot_ref, cot_hbm, sems.at[3, 0]))
    keeps[-1].start()
    def crossed(r, carry):
        at = pl.ds(pl.multiple_of(r * RUNS, RUNS), RUNS)
        values = [zero] * 7
        for first in range(0, half, block):
            acc = {}
            for tile, (pair, cols) in enumerate(tile_at):
                u = [conv_ref[pair][2 * first + i, at, cols] for i in range(2 * block + 4)]
                bias = jnp.broadcast_to(rows_ref[BIAS : BIAS + 1, tile * LANES : (tile + 1) * LANES], (RUNS, LANES))
                for i in range(block):
                    g = cot_ref[first + i, at, tile * LANES : (tile + 1) * LANES]
                    terms = [g * u[2 * i + d] for d in range(6)] + [g * bias]
                    for d in range(7):
                        acc[i, d] = terms[d] if tile == 0 else acc[i, d] + terms[d]
            for i, d in acc:
                here = lane == 2 * first + (2 * i + OFF)
                values[d] = jnp.where(here, jnp.sum(acc[i, d], axis=1, keepdims=True), values[d])
        for d in range(7):
            pack_ref[6 + d, at, :] = values[d]
        return carry

    lax.fori_loop(0, rows, crossed, 0)

    def total_of(x):
        return jnp.sum(jnp.sum(x, axis=1, keepdims=True), axis=0, keepdims=True)

    def lookups(r, sums):
        at = pl.ds(pl.multiple_of(r * RUNS, RUNS), RUNS)
        ids = pack_ref[IDS, at, :].astype(jnp.int32)
        real = ids >= 0
        low = jnp.where(real, ids, 0)

        def look(row):
            value = jnp.zeros((RUNS, LANES), f32)
            for part in range(vocab // LANES):
                entry = jnp.broadcast_to(
                    table_ref[row : row + 1, part * LANES : (part + 1) * LANES], (RUNS, LANES)
                )
                taken = jnp.take_along_axis(entry, low % LANES, axis=1)
                value = jnp.where(low // LANES == part, taken, value)
            return jnp.where(real, value, 0.0)

        scored = jnp.zeros((RUNS, LANES), f32)
        biased = jnp.zeros((RUNS, LANES), f32)
        for k in range(kernel):
            scored = scored + shifted(look(k), k - (kernel - 1))
            biased = biased + shifted(look(4 + k), k - (kernel - 1))
        inner_real = real & (lane >= OFF - 2)
        scored = jnp.where(inner_real, scored, 0.0)
        biased = jnp.where(inner_real, biased, 0.0)
        pack_ref[13, at, :] = scored
        pack_ref[14, at, :] = biased
        own = (real & (lane >= OFF) & (lane < OFF + run)).astype(f32)
        new = (own * look(8), own, own * biased, own * pack_ref[0, at, :], own * (1 - lane % 2).astype(f32))
        return tuple(a + b for a, b in zip(sums, new))

    sums = lax.fori_loop(0, rows, lookups, (zero,) * 5)
    sums_ref[...] = spread([total_of(x) for x in sums], sums_ref.shape[0])
    for copy in keeps:
        copy.wait()


def in_two(x):
    high = x.astype(jnp.bfloat16)
    return high, (x - high.astype(f32)).astype(jnp.bfloat16)


def unpack_rows(pack_ref, rows_ref):
    for tile in range(rows_ref.shape[1] // LANES):
        at = slice(tile % 4 * 8, tile % 4 * 8 + 8)
        rows_ref[:, tile * LANES : (tile + 1) * LANES] = pack_ref[WEIGHTS + tile // 4, at, :]


def spread(sums, count):
    lane = iota((1, LANES), 1)
    row = jnp.zeros((1, LANES), f32)
    for i, x in enumerate(sums):
        row = jnp.where(lane == i, x, row)
    return jnp.broadcast_to(row[None], (count, 1, LANES))


def picked(ref, number):
    row = jnp.sum(ref[...], axis=0)
    return [row[:, i : i + 1] for i in range(number)]


def scales(first_ref, bias, feat):
    emb_sum, count, cross, square, count4 = picked(first_ref, 5)
    one = jnp.sqrt(emb_sum / (count * feat) + EPS)
    bias_sum = jnp.sum(bias * bias, axis=1, keepdims=True)
    conv_sum = jnp.maximum(count * bias_sum + 2.0 * cross / one + square / (one * one), 0.0)
    two = jnp.sqrt(conv_sum / (count * feat) + EPS)
    return one, two, count, count4, bias_sum, cross


class Places:
    def __init__(self, ids, start, run):
        shape = ids.shape
        self.j = iota(shape, 1) - OFF
        sub = iota(shape, 0) % RUNS
        self.inside = (self.j >= 0) & (self.j < run)
        self.real = ((ids >= 0) & (self.j >= -2)).astype(f32)
        self.own = jnp.where(self.inside, self.real, 0.0)
        shown = self.j + OFF
        self.two, self.four = shown % 2, shown % 4
        self.three = (start + run * sub + shown + (3 * OFF - OFF)) % 3

    def holds(self, size, by):
        if size == 1:
            return jnp.ones_like(self.real) if by == 0 else None
        if abs(by) >= size:
            return None
        phase = {2: self.two, 3: self.three, 4: self.four}[size]
        return ((phase + by >= 0) & (phase + by < size)).astype(f32)

    def pooled(self, size, x):
        if size == 1:
            return x
        pair = x + jnp.where(self.two == 0, shifted(x, 1), shifted(x, -1))
        if size == 2:
            return pair
        if size == 4:
            return pair + jnp.where(self.four < 2, shifted(pair, 2), shifted(pair, -2))
        left, right = shifted(x, -1), shifted(x, 1)
        side = jnp.where(self.three == 0, shifted(x, 2), left)
        far = jnp.where(self.three == 2, shifted(x, -2), right)
        return x + side + far

    def both(self, x):
        return x + shifted(x, -1)


SIZES = (1, 2, 3, 4)
REACH = range(-3, 4)


def score_kernel(sizes, first_ref, dots_ref, state_ref, sums_ref, rows_ref):
    rows, width, run, feat, vocab, kernel = sizes
    start = lax.axis_index("seq") * width
    unpack_rows(dots_ref, rows_ref)
    bias = rows_ref[BIAS : BIAS + 1, :]
    one, two, count, count4, bias_sum, cross = scales(first_ref, bias, feat)
    at = Places(dots_ref[IDS], start, run)
    real, own = at.real, at.own
    rate = 1.0 / (one * two)
    bias_score = jnp.sum(bias * rows_ref[SCORER : SCORER + 1, :], axis=1, keepdims=True) / two

    normed_score = real * bias_score + rate * dots_ref[13]
    counts = [jnp.maximum(at.pooled(b, real), 1.0) for b in SIZES]
    scores = [at.pooled(b, normed_score) / n for b, n in zip(SIZES, counts)]
    top = functools.reduce(jnp.maximum, scores)
    parts = [jnp.exp(s - top) for s in scores]
    whole = sum(parts)
    probs = [p / whole for p in parts]
    weights = [own * p / n for p, n in zip(probs, counts)]

    holds = {(b, d): at.holds(b, d) for b in SIZES for d in REACH}

    def blend(values):
        out = {}
        for d in REACH:
            terms = [v * holds[b, d] for b, v in zip(SIZES, values) if holds[b, d] is not None]
            out[d] = sum(terms)
        return out

    mixer = blend(weights)
    pair_count = jnp.maximum(at.pooled(2, real), 1.0)
    halver = {}
    even = at.two == 0
    for d in REACH:
        zero = jnp.zeros_like(real)
        ahead = shifted(mixer[d - 1], 1) if d - 1 >= -3 else zero
        behind = shifted(mixer[d + 1], -1) if d + 1 <= 3 else zero
        other = jnp.where(even, ahead, behind)
        halver[d] = jnp.where(at.inside, (mixer[d] + other) / pair_count, 0.0)

    bias_dot = dots_ref[14]
    normed_bias = real * (bias_sum / two) + rate * bias_dot
    lags = []
    for lag in range(6):
        later = shifted(real, lag)
        value = rate * rate * dots_ref[lag]
        value = value + (rate / two) * (bias_dot * later + real * shifted(bias_dot, lag))
        lags.append(value + (bias_sum / (two * two)) * (real * later))

    def gram(a, b):
        low, high = min(a, b), max(a, b)
        return shifted(lags[high - low], low) if high - low < 6 else None

    table = {(a, b): gram(a, b) for a in REACH for b in REACH if a <= b}

    def against(weighting):
        out = {}
        for a in REACH:
            out[a] = sum(
                weighting[b] * table[min(a, b), max(a, b)]
                for b in REACH if table[min(a, b), max(a, b)] is not None
            )
        return out

    with_mixed, with_half = against(mixer), against(halver)
    with_grad = {}
    grad_bias = dots_ref[12]
    cross_dots = {
        d: rate * dots_ref[6 + d + 2] + shifted(real, d) * (grad_bias / two) for d in range(-2, 4)
    }
    for d in REACH:
        here = cross_dots[d] if d >= -2 else jnp.zeros_like(real)
        before = shifted(cross_dots[d + 1], -1) if d + 1 <= 3 else jnp.zeros_like(real)
        with_grad[d] = jnp.where(even, here, before)

    def per_block(values, scale):
        out = []
        for b, n in zip(SIZES, counts):
            terms = [values[d] * holds[b, d] for d in REACH if holds[b, d] is not None]
            out.append(scale * sum(terms) / n)
        return out

    shared = own / pair_count
    bases = [per_block(with_grad, shared), per_block(with_half, shared), per_block(with_mixed, own)]

    def total_of(x):
        return jnp.sum(jnp.sum(x, axis=1, keepdims=True), axis=0, keepdims=True)

    first_of_pair = jnp.where(even & at.inside, 1.0, 0.0)
    mean_score = sum(p * s for p, s in zip(probs, scores))

    def bent(values):
        mean = sum(p * v for p, v in zip(probs, values))
        return total_of(own * (sum(p * s * v for p, s, v in zip(probs, scores, values)) - mean * mean_score))

    sums = [
        total_of(sum(own * mixer[d] * with_mixed[d] for d in REACH)),
        total_of(first_of_pair * sum(halver[d] * with_half[d] for d in REACH)),
        total_of(first_of_pair * sum(halver[d] * with_grad[d] for d in REACH)),
        bent(bases[0]), bent(bases[1]), bent(bases[2]),
        total_of(shared * at.both(grad_bias)),
        total_of(shared * sum(halver[d] * shifted(normed_bias, d) for d in REACH)),
        total_of(own * sum(mixer[d] * shifted(normed_bias, d) for d in REACH)),
    ]
    for i, b in enumerate(SIZES):
        state_ref[i] = weights[i]
        state_ref[4 + i] = probs[i]
        for f in range(3):
            state_ref[8 + 4 * f + i] = bases[f][i]
    sums_ref[...] = spread(sums, sums_ref.shape[0])


def back_kernel(
    sizes, first_hbm, second_hbm, pack_hbm, state_hbm, mark_hbm, embed_hbm, conv_hbm, emb_hbm, cot_hbm,
    out_hbm, keep_hbm, send_hbm,
    first_ref, second_ref, pack_ref, state_ref, mark_ref, embed_ref, rows_ref, turn_ref, out_ref, order_ref,
    narrow_ref, acc_ref, pay_ref, conv_ref, emb_ref, cot_ref, back_ref, sems,
):
    rows, width, run, feat, vocab, kernel = sizes
    tiles = feat // LANES
    per = WIDE // LANES
    units = rows * (feat // WIDE)
    half = run // 2
    vr = rows * RUNS

    def fetches(unit):
        sub = pl.ds(pl.multiple_of(unit % rows * RUNS, RUNS), RUNS)
        cols = pl.ds(pl.multiple_of(unit // rows * WIDE, LANES), WIDE)
        return [
            pltpu.make_async_copy(a.at[:, sub, cols], b.at[:, sub, cols], sems.at[i, unit])
            for i, (a, b) in enumerate(((conv_hbm, conv_ref), (cot_hbm, cot_ref), (emb_hbm, emb_ref)))
        ]

    size = RUNS * half

    def stored(unit):
        some = pl.ds(pl.multiple_of(unit % rows * size, 8), size)
        cols = pl.ds(pl.multiple_of(unit // rows * WIDE, LANES), WIDE)
        return pltpu.make_async_copy(out_ref.at[some, cols], out_hbm.at[some, cols], sems.at[3, unit])

    def restore(unit):
        some = pl.ds(pl.multiple_of(unit % rows * size, 8), size)
        cols = pl.ds(pl.multiple_of(unit // rows * WIDE, LANES), WIDE)
        high, low = in_two(turn_ref[...].reshape(size, WIDE))
        moved = jnp.dot(order_ref[...], high, preferred_element_type=f32)
        out_ref[some, cols] = moved + jnp.dot(order_ref[...], low, preferred_element_type=f32)

    sources = (first_hbm, second_hbm, pack_hbm, state_hbm, mark_hbm, embed_hbm)
    targets = (first_ref, second_ref, pack_ref, state_ref, mark_ref, embed_ref)
    small = [pltpu.make_async_copy(a, b, sems.at[4, i]) for i, (a, b) in enumerate(zip(sources, targets))]
    ahead = 3
    for copy in small[:4]:
        copy.start()
    for unit in range(ahead):
        for copy in fetches(unit):
            copy.start()
    for copy in small[4:]:
        copy.start()
    for copy in small[:4]:
        copy.wait()

    start = lax.axis_index("seq") * width
    unpack_rows(pack_ref, rows_ref)
    bias = rows_ref[BIAS : BIAS + 1, :]
    one, two, count, count4, bias_sum, cross = scales(first_ref, bias, feat)
    mixed_sum, half_sum, inner, bent_g, bent_h, bent_m, bias_g, bias_h, bias_m = picked(second_ref, 9)
    volume, volume4 = count * feat, count4 * feat
    three = jnp.sqrt(mixed_sum / volume + EPS)
    four = jnp.sqrt(half_sum / (three * three) / volume4 + EPS)
    fourth = (inner / three) / (four * four * four * volume4)
    alpha = 1.0 / (three * four)
    beta = -fourth / (three * three)
    gamma = -(inner / four - fourth / three * half_sum) / (three * three * three * volume)
    joint = alpha * (inner + bent_g) + beta * (half_sum + bent_h) + gamma * (mixed_sum + bent_m)
    rate = 1.0 / (one * two)
    normed_bias = count * bias_sum / two + rate * cross
    bias_back = (alpha * bias_g + beta * bias_h + gamma * bias_m - joint / volume * normed_bias) / two
    inner_one = one * (joint * EPS / (two * two) - bias_back)
    first_coef = inner_one / (one * one * one * volume)

    at = Places(pack_ref[IDS], start, run)
    probs = [state_ref[4 + i] for i in range(4)]
    weights = [state_ref[i] for i in range(4)]
    grads = [
        alpha * state_ref[8 + i] + beta * state_ref[12 + i] + gamma * state_ref[16 + i] for i in range(4)
    ]
    mean = sum(p * g for p, g in zip(probs, grads))
    spreading = jnp.zeros_like(probs[0])
    for i, b in enumerate(SIZES):
        bent = probs[i] * (grads[i] - mean)
        n = jnp.maximum(at.pooled(b, at.real), 1.0)
        spreading = spreading + at.pooled(b, jnp.where(at.inside, bent / n, 0.0))
    pair_real = at.pooled(2, at.real)
    pair_count = jnp.maximum(pair_real, 1.0)
    filled = (pair_real > 0).astype(f32)
    narrow = [rate * w for w in weights] + [rate * spreading, at.real]
    paired = [
        alpha / pair_count, alpha * filled, beta / (pair_count * pair_count), beta * filled / pair_count + gamma
    ]
    leak = jnp.sum(jnp.sum(spreading * at.real, axis=1, keepdims=True), axis=0, keepdims=True)

    for i, x in enumerate(narrow + paired):
        narrow_ref[i] = x
    order = iota((size, size), 0)
    order = (iota((size, size), 1) == order % half * RUNS + order // half).astype(f32)
    order_ref[...] = order.astype(jnp.bfloat16)
    turn_ref[...] = jnp.zeros_like(turn_ref)
    acc_ref[...] = jnp.zeros_like(acc_ref)
    phase = (start + run * iota((RUNS, LANES), 0)) % 3
    at_phase = [phase == p for p in range(3)]

    def chosen(j, a, b, c):
        return jnp.where(at_phase[(0 - j) % 3], a, jnp.where(at_phase[(1 - j) % 3], b, c))

    full = (RUNS, LANES)
    alpha_all = jnp.broadcast_to(alpha, full)
    gamma_all = jnp.broadcast_to(gamma, full)
    fall = jnp.broadcast_to(rate * rate * joint / volume, full)
    fall_bias = rate * joint / volume / two

    def column(r, tile, near, factor):
        sub = pl.ds(pl.multiple_of(r * RUNS, RUNS), RUNS)
        cols = pl.ds(pl.multiple_of(tile * LANES, LANES), LANES)
        taps = [jnp.broadcast_to(rows_ref[k : k + 1, cols], full) for k in range(kernel)]
        bias_row = rows_ref[BIAS : BIAS + 1, cols]
        normed_row = jnp.broadcast_to(bias_row / two, full)
        fall_row = jnp.broadcast_to(bias_row * fall_bias, full)
        scorer = jnp.broadcast_to(rows_ref[SCORER : SCORER + 1, cols], full)
        zero = jnp.zeros(full, f32)

        u, triple, y3, gc = {}, {}, {}, {}
        sums = [zero] * (kernel + 2)
        block = {}
        for j in range(-2, 2):
            u[j] = conv_ref[j + 2, sub, cols]
        triple[-2] = u[-2] + u[-1] + u[0]
        triple[-1] = u[-1] + u[0] + u[1]

        def window(j):
            near = [y3[i] for i in (j, j + 1, j + 2) if 0 <= i < run]
            return functools.reduce(lambda a, b: a + b, near) if near else zero

        def settle(s):
            nonlocal sums
            for j in (s, s - 1, s - 2):
                if j not in block:
                    block[j] = window(j)
            g = chosen(s, block[s], block[s - 1], block[s - 2])
            sigma = factor(4, s)
            g = g + sigma * scorer
            if 0 <= s < run:
                g = g + lone[s]
                g = g - fall * u[s] - fall_row
            g = g * factor(5, s)
            gc[s] = g
            for k in range(kernel):
                sums[k] = sums[k] + g * emb_ref[s - kernel + 1 + k + LEFT, sub, cols]
            sums[kernel] = sums[kernel] + g
            sums[kernel + 1] = sums[kernel + 1] + sigma * u[s]

        def finish(s):
            terms = [taps[k] * gc[s + kernel - 1 - k] for k in range(kernel) if s + kernel - 1 - k in gc]
            back_ref[s + LEFT, sub, cols] = functools.reduce(lambda a, b: a + b, terms)

        lone = {}
        settled = -2
        finished = -LEFT
        for quad in range(0, run, 4):
            for j in range(quad + 2, quad + 6):
                u[j] = conv_ref[j + 2, sub, cols]
            two_sums = [u[quad + 2 * p] + u[quad + 2 * p + 1] for p in range(2)]
            four_sum = two_sums[0] + two_sums[1]
            wide = zero
            for p in range(2):
                y = None
                xs = []
                for j in (quad + 2 * p, quad + 2 * p + 1):
                    triple[j] = u[j] + u[j + 1] + u[j + 2] if j % 2 else two_sums[p] + u[j + 2]
                    x = factor(0, j) * u[j] + factor(1, j) * two_sums[p]
                    x = x + factor(2, j) * chosen(j, triple[j], triple[j - 1], triple[j - 2])
                    x = x + factor(3, j) * four_sum
                    xs.append(x)
                y = xs[0] + xs[1]
                k = quad // 2 + p
                scale_y = factor(6, 2 * k)
                turn_ref[k, :, near] = scale_y * y + factor(7, 2 * k) * normed_row
                q = scale_y * cot_ref[k, sub, cols] + factor(8, 2 * k) * y + factor(9, 2 * k) * normed_row
                pair = zero
                for i, j in enumerate((quad + 2 * p, quad + 2 * p + 1)):
                    g = q + gamma_all * xs[i]
                    lone[j] = factor(0, j) * g
                    y3[j] = factor(2, j) * g
                    pair = factor(1, j) * g if i == 0 else pair + factor(1, j) * g
                    wide = factor(3, j) * g if i + p == 0 else wide + factor(3, j) * g
                for j in (quad + 2 * p, quad + 2 * p + 1):
                    lone[j] = lone[j] + pair
            for j in range(quad, quad + 4):
                lone[j] = lone[j] + wide
            last = quad + 3 - 2 if quad + 4 < run else run + 1
            while settled <= last:
                settle(settled)
                settled += 1
            done = settled - kernel if quad + 4 < run else run + RIGHT - 1
            while finished <= done:
                finish(finished)
                finished += 1
            yield
        for i in range(kernel + 2):
            acc_ref[i, :, cols] = acc_ref[i, :, cols] + sums[i]

    def some_columns(unit, carry):
        for copy in fetches(unit):
            copy.wait()

        @pl.when(unit + ahead < units)
        def _():
            for copy in fetches(unit + ahead):
                copy.start()

        r = unit % rows
        made = {}

        def factor(i, j):
            if (i, j) not in made:
                sub = pl.ds(pl.multiple_of(r * RUNS, RUNS), RUNS)
                made[i, j] = jnp.broadcast_to(narrow_ref[i, sub, j + OFF : j + OFF + 1], full)
            return made[i, j]

        last = jnp.maximum(unit - 1, 0)
        restore(last)
        parts = []
        for i in range(per):
            near = slice(i * LANES, (i + 1) * LANES)
            parts.append(column(r, unit // rows * per + i, near, factor))
        for _ in zip(*parts, strict=True):
            pass

        @pl.when(unit > 0)
        def _():
            stored(last).start()

        return carry

    lax.fori_loop(0, units, some_columns, 0)
    restore(units - 1)
    stored(units - 1).start()

    positions = mark_ref.shape[1]
    edge = run + LEFT + RIGHT
    back_ref[edge:] = jnp.zeros((back_ref.shape[0] - edge, vr, feat), f32)
    for copy in small[4:]:
        copy.wait()
    total_tiles = pay_ref.shape[0]

    def gather(pair, carry):
        cols = pl.ds(pl.multiple_of(pair * WIDE, LANES), WIDE)
        high, low = in_two(back_ref[:, :, cols].reshape(positions, WIDE))
        total = jnp.dot(mark_ref[...], high, preferred_element_type=f32)
        total = total + jnp.dot(mark_ref[...], low, preferred_element_type=f32)
        for v in range(vocab // 8):
            seen = first_coef * pack_ref[SEEN + v * 8 // vr, v * 8 % vr : v * 8 % vr + 8, :]
            for i in range(per):
                wide = pl.ds(pl.multiple_of(pair * WIDE + i * LANES, LANES), LANES)
                part = total[v * 8 : v * 8 + 8, i * LANES : (i + 1) * LANES]
                pay_ref[v * tiles + pair * per + i] = part - seen * embed_ref[v * 8 : v * 8 + 8, wide]
        return carry

    lax.fori_loop(0, feat // WIDE, gather, 0)

    end = vocab // 8 * tiles
    pay_ref[end:] = jnp.zeros((total_tiles - end, 8, LANES), f32)
    for i in range(kernel + 2):
        row = jnp.sum(acc_ref[i], axis=0, keepdims=True)
        if i == kernel:
            row = row * one
        if i == kernel + 1:
            row = row + bias * (leak / two)
        for tile in range(tiles):
            place = i * tiles + tile
            pay_ref[end + place // 8, place % 8 : place % 8 + 1, :] = row[:, tile * LANES : (tile + 1) * LANES]
    core = lax.axis_index("seq") % 2
    part = total_tiles // 2
    halves = [
        pltpu.make_async_copy(pay_ref.at[pl.ds(core * part, part)], keep_hbm, sems.at[0, 0]),
        pltpu.make_async_copy(pay_ref.at[pl.ds((1 - core) * part, part)], send_hbm, sems.at[1, 0]),
    ]
    for copy in halves:
        copy.start()
    for unit in range(units):
        stored(unit).wait()
    for copy in halves:
        copy.wait()


def exchanged(x):
    return lax.all_to_all(x, AXES, 0, 0, tiled=True)


def partner(x, axis, step):
    n = lax.axis_size(axis)
    return lax.ppermute(x, axis, [(i, i ^ step) for i in range(n)])


def summed_over_devices(keep, send):
    n = lax.axis_size("seq")
    others = lax.axis_size("rows") * n // 2
    groups = [[2 * i + side for i in range(others)] for side in range(2)]

    def traded(x):
        return lax.all_to_all(x, AXES, 0, 0, tiled=True, axis_index_groups=groups)

    x = keep + partner(send, "seq", 1)
    chunk = (others, x.shape[0] * x.shape[1] // others, 1, LANES)
    part = jnp.sum(traded(x.reshape(chunk)), axis=0)
    x = traded(jnp.broadcast_to(part[None], chunk)).reshape(x.shape)
    return x, partner(x, "seq", 1), lax.axis_index("seq") % 2 == 1


def on_device(byte_ids, lengths, embed, conv_weight, conv_bias, score_weight, out_grad):
    rows, width = byte_ids.shape
    vocab, feat = embed.shape
    kernel = conv_weight.shape[0]
    run = width // RUNS
    half = width // 2
    vr = rows * RUNS
    sizes = (rows, width, run, feat, vocab, kernel)
    count = lax.axis_size("seq")
    devices = count * lax.axis_size("rows")
    span = -(-(run + LEFT + RIGHT) // 8) * 8
    tiles = feat // LANES
    struct = jax.ShapeDtypeStruct
    sem = pltpu.SemaphoreType.DMA

    params = pltpu.CompilerParams(vmem_limit_bytes=63 * 1024 * 1024)

    up = [(i, i + 1) for i in range(count - 1)]
    left = lax.ppermute(byte_ids, "seq", up)
    right = lax.ppermute(byte_ids, "seq", [(j, i) for i, j in up])

    pairs = feat // WIDE
    bf16 = jnp.bfloat16
    wide_emb = struct((span, vr, feat), f32)
    wide_conv = struct((run + 4, vr, feat), f32)
    wide_cot = struct((half // RUNS, vr, feat), f32)
    marks = struct((vocab, span * vr), bf16)
    pack = struct((SEEN + vocab // vr, vr, LANES), f32)
    sums = struct((devices, 1, LANES), f32)
    state = struct((20, vr, LANES), f32)

    def scratch(like):
        return pltpu.VMEM(like.shape, like.dtype)

    def per_pair(like):
        return [pltpu.VMEM((*like.shape[:-1], WIDE), like.dtype)] * pairs

    emb, conv, cot, mark, packed, first = pl.pallas_call(
        functools.partial(stats_kernel, sizes),
        out_shape=(wide_emb, wide_conv, wide_cot, marks, pack, sums),
        in_specs=[HBM] * 9, out_specs=(HBM,) * 4 + (VMEM,) * 2,
        scratch_shapes=[
            scratch(byte_ids), scratch(byte_ids), scratch(byte_ids), pltpu.SMEM((rows,), jnp.int32), scratch(embed),
            scratch(conv_weight), scratch(conv_bias), scratch(score_weight), pltpu.VMEM((rows * half, feat), f32),
            pltpu.VMEM((2, vocab, feat), bf16), pltpu.VMEM((16, vocab), f32), pltpu.VMEM((8, feat), f32),
            pltpu.VMEM((span * vr, vocab), bf16), scratch(marks), pltpu.VMEM((LANES // vr, vr, vocab), f32),
            pltpu.VMEM((-(-span * vr // LANES // 8) * 8, LANES), f32), pltpu.VMEM((vocab, LANES), f32),
            pltpu.VMEM((half, half), bf16), pltpu.VMEM((vr, LANES), jnp.int32),
            *per_pair(wide_emb), *per_pair(wide_conv), scratch(wide_cot), sem((4, 9)),
        ],
        compiler_params=params, name="stats",
    )(
        byte_ids, left, right, lengths, embed, conv_weight, conv_bias, score_weight,
        out_grad.reshape(rows * half, feat),
    )
    first = exchanged(first)

    states, second = pl.pallas_call(
        functools.partial(score_kernel, sizes),
        out_shape=(state, sums),
        in_specs=[VMEM] * 2, out_specs=(VMEM, VMEM), scratch_shapes=[pltpu.VMEM((8, feat), f32)],
        compiler_params=params, name="score",
    )(first, packed)
    second = exchanged(second)

    lines = vocab * tiles
    lines = -(-(lines + (kernel + 2) * tiles) // devices) * devices
    parts = struct((lines // 16, 8, LANES), f32)
    blocks, keep, send = pl.pallas_call(
        functools.partial(back_kernel, sizes),
        out_shape=(struct((rows * half, feat), f32), parts, parts),
        in_specs=[HBM] * 9, out_specs=(HBM, HBM, HBM),
        scratch_shapes=[
            scratch(sums), scratch(sums), scratch(pack), scratch(state), scratch(marks), scratch(embed),
            pltpu.VMEM((8, feat), f32), pltpu.VMEM((half // RUNS, RUNS, WIDE), f32),
            pltpu.VMEM((rows * half, feat), f32), pltpu.VMEM((half, half), bf16), pltpu.VMEM((10, vr, LANES), f32),
            pltpu.VMEM((kernel + 2, RUNS, feat), f32), pltpu.VMEM((lines // 8, 8, LANES), f32),
            scratch(wide_conv), scratch(wide_emb), scratch(wide_cot), scratch(wide_emb),
            sem((5, max(6, rows * pairs))),
        ],
        compiler_params=params, name="back",
    )(first, second, packed, states, mark, embed, conv, emb, cot)

    mine, other, swapped = summed_over_devices(keep, send)
    whole = jnp.where(swapped, jnp.concatenate([other, mine]), jnp.concatenate([mine, other]))
    table = whole[: vocab * tiles // 8].reshape(vocab // 8, tiles, 8, LANES).transpose(0, 2, 1, 3).reshape(vocab, feat)
    extra = whole[vocab * tiles // 8 :].reshape(-1, LANES)[: (kernel + 2) * tiles].reshape(kernel + 2, feat)
    return blocks.reshape(rows, half, feat), table, extra[:kernel], extra[kernel], extra[kernel + 1]


def solution(mesh):
    placed = (P("rows", "seq"), P("rows"), P(), P(), P(), P(), P("rows", "seq", None))
    return jax.shard_map(
        on_device,
        mesh=mesh,
        in_specs=placed,
        out_specs=(P("rows", "seq", None), P(), P(), P(), P()),
        check_vma=False,
    )
```

time: 142 us -> 117 us (0.82)
  Pallas kernels: 62.2 us -> 44.2 us
  blocking collectives: 38.1 us -> 56 us
  waiting for transfers between devices: 23.3 us -> 7.75 us
  local copies, waits for them, and re-layouts: 8.34 us -> 2.96 us
  starting transfers between devices: 7.49 us -> 3.72 us
    ppermute x4 -> x2, waiting for transfers between devices: 16.1 us -> 3.69 us  [partner(): return lax.ppermute(x, axis, [(i, i ^ step) for i in range(n)])]
    pallas_call x3 -> x2, Pallas kernels: 31.6 us -> 21.6 us  [the longest x1 18.9 us: on_device(): pl.pallas_call(functools.partial(stats_kernel, sizes), out_shape=(wide_em...]
    all_to_all x2, blocking collectives: 21.8 us -> 31.8 us  [traded(): return lax.all_to_all(x, AXES, 0, 0, tiled=True, axis_index_groups=groups)]
    pallas_call x1, Pallas kernels: 30.6 us -> 22.6 us  [on_device(): pl.pallas_call(functools.partial(back_kernel, sizes), out_shape=(struct((...]
    all_to_all x1 -> x2, blocking collectives: 16.3 us -> 24.2 us  [exchanged(): return lax.all_to_all(x, AXES, 0, 0, tiled=True)]
    all_to_all x1 -> x0, waiting for transfers between devices: 7.13 us -> none  [exchanged(): return lax.all_to_all(x, AXES, 0, 0, tiled=True)]
    ppermute x1, waiting for transfers between devices: 0.01 us -> 4.06 us  [on_device(): right = lax.ppermute(byte_ids, 'seq', [(j, i) for i, j in up])]
    reshape x3 -> x1, local copies, waits for them, and re-layouts: 3.31 us -> 0.01 us  [on_device(): whole[vocab * tiles // 8:].reshape(-1, LANES)[:(kernel + 2) * tiles]]
  transfers between devices with their start and end apart: 7 -> 4, of which waited for: 5 -> 3; matrix products, arithmetic and copies ran while one was open for 3% -> 0% of each run, Pallas kernels for 2% -> 0%
where the time goes in v2:
time: 117 us
  blocking collectives  56 us (48%)
  Pallas kernels  44.2 us (38%)
  waiting for transfers between devices  7.75 us (7%)
  starting transfers between devices  3.72 us (3%)
  local copies, waits for them, and re-layouts  2.96 us (3%)
  other arithmetic  1.38 us (1%)
    all_to_all x2, blocking collectives, traded(): return lax.all_to_all(x, AXES, 0, 0, tiled=True, axis_index_groups=groups)  31.8 us
    all_to_all x2, blocking collectives, exchanged(): return lax.all_to_all(x, AXES, 0, 0, tiled=True)  24.2 us
    pallas_call x1, Pallas kernels, on_device(): pl.pallas_call(functools.partial(back_kernel, sizes), out_shape=(struct((...  22.6 us
    pallas_call x1, Pallas kernels, on_device(): pl.pallas_call(functools.partial(stats_kernel, sizes), out_shape=(wide_em...  18.9 us
    ppermute x1, waiting for transfers between devices, on_device(): right = lax.ppermute(byte_ids, 'seq', [(j, i) for i, j in up])  4.06 us
    ppermute x2, waiting for transfers between devices, partner(): return lax.ppermute(x, axis, [(i, i ^ step) for i in range(n)])  3.69 us
    pallas_call x1, Pallas kernels, on_device(): pl.pallas_call(functools.partial(score_kernel, sizes), out_shape=(state,...  2.65 us
    ppermute x1, starting transfers between devices, on_device(): left = lax.ppermute(byte_ids, 'seq', up)  2.36 us
  transfers between devices with their start and end apart: 4, of which 3 were waited for; matrix products, arithmetic and copies ran while one was open for 0% of the time, Pallas kernels for 0%

profile of v2, /device:TPU:0, one launch (start us, length us, event | category | flops | bytes accessed | tf_op | source)
XLA Modules:
  0.0 116.7 jit_solution(17764811350675559100)
XLA Ops:
  0.6 2.4 %collective-permute-start = (s32[4,512]{1,0:T(4,128)}, s32[4,512]{1,0:T(4,128)S(1)}, u32[]{:S(2)}, u32[]{:S(2)}) collective-permute-start(s32[4,512]{1,0:T(4,128)} %own_hbm.1), channel_id=1, source_target_pairs={{0,1},{1,2},{2,3},{4,5},{5,6},{6,7},{8,9},{9,10},{10,11},{12,13},{... | collective-permute-start | bytes 24584 | tf_op jit(solution)/shard_map/ppermute | solution.py:813
  3.0 1.3 %collective-permute-start.1 = (s32[4,512]{1,0:T(4,128)}, s32[4,512]{1,0:T(4,128)S(1)}, u32[]{:S(2)}, u32[]{:S(2)}) collective-permute-start(s32[4,512]{1,0:T(4,128)} %own_hbm.1), channel_id=1, source_target_pairs={{1,0},{2,1},{3,2},{5,4},{6,5},{7,6},{9,8},{10,9},{11,10},{13,12},{... | collective-permute-start | bytes 24584 | tf_op jit(solution)/shard_map/ppermute | solution.py:814
  4.3 0.0 collective-permute-done.left_hbm
  4.3 0.0 copy-start
  4.3 4.1 %collective-permute-done.1.right_hbm = s32[4,512]{1,0:T(4,128)S(1)} collective-permute-done((s32[4,512]{1,0:T(4,128)}, s32[4,512]{1,0:T(4,128)S(1)}, u32[]{:S(2)}, u32[]{:S(2)}) %collective-permute-start.1) | collective-permute-done | bytes 8224 | tf_op jit(solution)/shard_map/ppermute | solution.py:814
  8.4 0.0 copy-start.1
  8.4 0.0 copy-done
  8.4 0.6 copy-done.1
  9.0 18.9 %stats.1 = (f32[72,32,768]{2,1,0:T(8,128)}, f32[68,32,768]{2,1,0:T(8,128)}, f32[32,32,768]{2,1,0:T(8,128)}, bf16[256,2304]{1,0:T(8,128)(2,1)}, f32[26,32,128]{2,1,0:T(8,128)}, /*index=5*/f32[32,1,128]{2,1,0:T(1,128)}) custom-call(s32[4,512]{1,0:T(4,128)} %own_hbm.1, s32[4,512]{1,0:T(4,128)} %copy-done, s32[4,512]{1,0:T(4,128)} %copy-done.1, s32[4]{0:T(128)} %len_hbm.1, ...), custom_call_target="tpu_custom_call" | custom-call | tf_op jit(solution)/shard_map/stats/pallas_call | solution.py:832
  27.9 14.0 %all_to_all.20.first_ref.first_hbm = f32[32,1,128]{2,1,0:T(1,128)} all-to-all(f32[32,1,128]{2,1,0:T(1,128)} %get-tuple-element.16), channel_id=1, replica_groups=mesh['rows'=8,'seq'=4] {'rows','seq'}, dimensions={0} | all-to-all | bytes 32768 | tf_op jit(solution)/shard_map/all_to_all | solution.py:772
  41.9 2.6 %score.1 = (f32[20,32,128]{2,1,0:T(8,128)}, f32[32,1,128]{2,1,0:T(1,128)}) custom-call(f32[32,1,128]{2,1,0:T(1,128)} %all_to_all.20.first_ref.first_hbm, f32[26,32,128]{2,1,0:T(8,128)} %get-tuple-element.17.dots_ref.pack_hbm), custom_call_target="tpu_custom_call" | custom-call | tf_op jit(solution)/shard_map/score/pallas_call | solution.py:852
  44.6 10.2 %all_to_all.21.second_hbm = f32[32,1,128]{2,1,0:T(1,128)} all-to-all(f32[32,1,128]{2,1,0:T(1,128)} %get-tuple-element.18), channel_id=1, replica_groups=mesh['rows'=8,'seq'=4] {'rows','seq'}, dimensions={0} | all-to-all | bytes 32768 | tf_op jit(solution)/shard_map/all_to_all | solution.py:772
  54.8 22.6 %back.1 = (f32[1024,768]{1,0:T(8,128)}, f32[100,8,128]{2,1,0:T(8,128)}, f32[100,8,128]{2,1,0:T(8,128)}) custom-call(f32[32,1,128]{2,1,0:T(1,128)} %all_to_all.20.first_ref.first_hbm, f32[32,1,128]{2,1,0:T(1,128)} %all_to_all.21.second_hbm, f32[26,32,128]{2,1,0:T(8,128)} %get-tuple-element.17.dots_ref.pack_hbm, f32[20,32,128]{2,1,0:T(8,128)} %get-tuple-element.19.state_hbm, ...), custom_call_target="tpu_custom_call" | custom-call | tf_op jit(solution)/shard_map/back/pallas_call | solution.py:863
  77.4 0.1 collective-permute-start.2
  77.5 1.9 %collective-permute-done.2 = f32[100,8,128]{2,1,0:T(8,128)S(1)} collective-permute-done((f32[100,8,128]{2,1,0:T(8,128)}, f32[100,8,128]{2,1,0:T(8,128)S(1)}, u32[]{:S(2)}, u32[]{:S(2)}) %collective-permute-start.2) | collective-permute-done | bytes 409632 | tf_op jit(solution)/shard_map/ppermute | solution.py:777
  79.4 1.1 add.8
  80.5 16.1 %all_to_all.22 = f32[16,50,1,128]{3,2,1,0:T(1,128)S(1)} all-to-all(f32[16,50,1,128]{3,2,1,0:T(1,128)S(1)} %bitcast.18), channel_id=1, replica_groups={{0,2,4,6,8,10,12,14,16,18,20,22,24,26,28,30},{1,3,5,7,9,11,13,15,17,19,..., dimensions={0} | all-to-all | bytes 819200 | tf_op jit(solution)/shard_map/all_to_all | solution.py:786
  96.5 0.3 reduce_sum.9
  96.8 0.2 broadcast_in_dim.2
  97.0 15.7 %all_to_all.23 = f32[16,50,1,128]{3,2,1,0:T(1,128)S(1)} all-to-all(f32[16,50,1,128]{3,2,1,0:T(1,128)S(1)} %broadcast_in_dim.2), channel_id=1, replica_groups={{0,2,4,6,8,10,12,14,16,18,20,22,24,26,28,30},{1,3,5,7,9,11,13,15,17,19,..., dimensions={0} | all-to-all | bytes 819200 | tf_op jit(solution)/shard_map/all_to_all | solution.py:786
  112.8 0.0 collective-permute-start.3
  112.8 1.7 %collective-permute-done.3 = f32[100,8,128]{2,1,0:T(8,128)S(1)} collective-permute-done((f32[100,8,128]{2,1,0:T(8,128)S(1)}, f32[100,8,128]{2,1,0:T(8,128)S(1)}, u32[]{:S(2)}, u32[]{:S(2)}) %collective-permute-start.3) | collective-permute-done | bytes 409632 | tf_op jit(solution)/shard_map/ppermute | solution.py:777
  114.5 0.1 maximum_select_fusion
  114.6 0.9 slice.32
  115.5 0.6 slice_bitcast_fusion.1
  116.1 0.6 slice.28
  (2 shorter events, 0.0 us)
Async XLA Ops:
  0.6 3.7 %collective-permute-start = (s32[4,512]{1,0:T(4,128)}, s32[4,512]{1,0:T(4,128)S(1)}, u32[]{:S(2)}, u32[]{:S(2)}) collective-permute-start(s32[4,512]{1,0:T(4,128)} %own_hbm.1), channel_id=1, source_target_pairs={{0,1},{1,2},{2,3},{4,5},{5,6},{6,7},{8,9},{9,10},{10,11},{12,13},{... | collective-permute-start | bytes 24584 | tf_op jit(solution)/shard_map/ppermute | solution.py:813
  3.0 5.4 %collective-permute-start.1 = (s32[4,512]{1,0:T(4,128)}, s32[4,512]{1,0:T(4,128)S(1)}, u32[]{:S(2)}, u32[]{:S(2)}) collective-permute-start(s32[4,512]{1,0:T(4,128)} %own_hbm.1), channel_id=1, source_target_pairs={{1,0},{2,1},{3,2},{5,4},{6,5},{7,6},{9,8},{10,9},{11,10},{13,12},{... | collective-permute-start | bytes 24584 | tf_op jit(solution)/shard_map/ppermute | solution.py:814
  4.3 4.1 %copy-start = (s32[4,512]{1,0:T(4,128)}, s32[4,512]{1,0:T(4,128)S(1)}, u32[]{:S(2)}) copy-start(s32[4,512]{1,0:T(4,128)S(1)} %collective-permute-done.left_hbm) | copy-start | bytes 24580
  8.4 0.6 copy-start.1
  77.4 2.0 %collective-permute-start.2 = (f32[100,8,128]{2,1,0:T(8,128)}, f32[100,8,128]{2,1,0:T(8,128)S(1)}, u32[]{:S(2)}, u32[]{:S(2)}) collective-permute-start(f32[100,8,128]{2,1,0:T(8,128)} %get-tuple-element.26), channel_id=1, source_target_pairs={{0,1},{1,0},{2,3},{3,2},{4,5},{5,4},{6,7},{7,6},{8,9},{9,8},{10,11... | collective-permute-start | bytes 1228808 | tf_op jit(solution)/shard_map/ppermute | solution.py:777
  112.8 1.7 %collective-permute-start.3 = (f32[100,8,128]{2,1,0:T(8,128)S(1)}, f32[100,8,128]{2,1,0:T(8,128)S(1)}, u32[]{:S(2)}, u32[]{:S(2)}) collective-permute-start(f32[100,8,128]{2,1,0:T(8,128)S(1)} %bitcast.16), channel_id=1, source_target_pairs={{0,1},{1,0},{2,3},{3,2},{4,5},{5,4},{6,7},{7,6},{8,9},{9,8},{10,11... | collective-permute-start | bytes 1228808 | tf_op jit(solution)/shard_map/ppermute | solution.py:777

commit v3 on v2

--- a/solution.py
+++ b/solution.py
@@ -15,6 +15,7 @@
 OFF = 8
 LEFT, RIGHT = 5, 2
 NT = (((1,), (1,)), ((), ()))
+TN = (((0,), (0,)), ((), ()))
 AXES = ("rows", "seq")
 VMEM = pl.BlockSpec(memory_space=pltpu.VMEM)
 HBM = pl.BlockSpec(memory_space=pltpu.HBM)
@@ -33,20 +34,17 @@
 
 
 def stats_kernel(
-    sizes, own_hbm, left_hbm, right_hbm, len_hbm, embed_hbm, taps_hbm, bias_hbm, scorer_hbm, grad_hbm,
+    sizes, own_hbm, left_ref, right_ref, len_hbm, embed_hbm, taps_hbm, bias_hbm, scorer_hbm, grad_hbm,
     emb_hbm, conv_hbm, cot_hbm, mark_hbm, pack_ref, sums_ref,
-    own_ref, left_ref, right_ref, len_ref, embed_ref, taps_ref, bias_ref, scorer_ref, grad_ref,
-    split_ref, table_ref, rows_ref, mark_ref, turn_ref, spot_ref, line_ref, seen_ref, order_ref, run_ref, *rest,
+    own_ref, len_ref, embed_ref, taps_ref, bias_ref, scorer_ref, grad_ref,
+    split_ref, table_ref, rows_ref, turn_ref, line_ref, seen_ref, order_ref, run_ref, emb_ref, conv_ref, cot_ref, sems,
 ):
     rows, width, run, feat, vocab, kernel = sizes
-    pairs = feat // WIDE
-    emb_ref, conv_ref = rest[:pairs], rest[pairs : 2 * pairs]
-    cot_ref, sems = rest[2 * pairs :]
     half = run // 2
     vr = rows * RUNS
-    span = mark_ref.shape[0] // vr
-    sources = (own_hbm, left_hbm, right_hbm, len_hbm, embed_hbm, taps_hbm, bias_hbm, scorer_hbm, grad_hbm)
-    targets = (own_ref, left_ref, right_ref, len_ref, embed_ref, taps_ref, bias_ref, scorer_ref, grad_ref)
+    span = emb_ref.shape[0]
+    sources = (own_hbm, len_hbm, embed_hbm, taps_hbm, bias_hbm, scorer_hbm, grad_hbm)
+    targets = (own_ref, len_ref, embed_ref, taps_ref, bias_ref, scorer_ref, grad_ref)
     fetch = [pltpu.make_async_copy(a, b, sems.at[0, i]) for i, (a, b) in enumerate(zip(sources, targets))]
     for copy in fetch:
         copy.start()
@@ -56,7 +54,7 @@
     base = start + run * sub
     back = (OFF - run) % LANES
 
-    for copy in fetch[:4]:
+    for copy in fetch[:2]:
         copy.wait()
     for r in range(rows):
         for s in range(RUNS):
@@ -92,34 +90,8 @@
         lined = lined + jnp.dot(some, put, preferred_element_type=f32)
     line_ref[...] = lined
 
-    def mark(step, carry):
-        for r in range(rows):
-            ids = pack_ref[IDS, r * RUNS : (r + 1) * RUNS, :].astype(jnp.int32)
-            for i in range(group):
-                where = jnp.full((RUNS, LANES), step * group + (i + OFF - LEFT), jnp.int32)
-                byte = jnp.take_along_axis(ids, where, axis=1)
-                for part in range(vocab // LANES):
-                    spot_ref[i, r * RUNS : (r + 1) * RUNS, part * LANES : (part + 1) * LANES] = jnp.where(
-                        byte == lane + part * LANES, 1.0, 0.0
-                    )
-        at = pl.ds(pl.multiple_of(step * LANES, LANES), LANES)
-        mark_ref[at, :] = spot_ref[...].reshape(LANES, vocab).astype(jnp.bfloat16)
-        bytes_here = jnp.broadcast_to(line_ref[pl.ds(step, 1), :], (vocab, LANES))
-        column = jnp.where(bytes_here == iota((vocab, LANES), 0).astype(f32), 1.0, 0.0)
-        turn_ref[:, at] = column.astype(jnp.bfloat16)
-        line = step * group + iota((1, LANES), 1) // vr
-        inside = ((line >= LEFT) & (line < LEFT + run)).astype(f32)
-        seen_ref[...] = seen_ref[...] + column * inside
-        return carry
-
     seen_ref[...] = jnp.zeros_like(seen_ref)
-    lax.fori_loop(0, span // group, mark, 0)
-    for i in range(vocab // vr):
-        seen = jnp.sum(seen_ref[i * vr : (i + 1) * vr, :], axis=1, keepdims=True)
-        pack_ref[SEEN + i] = jnp.broadcast_to(seen, (vr, LANES))
-    keep_mark = pltpu.make_async_copy(turn_ref, mark_hbm, sems.at[1, 0])
-    keep_mark.start()
-    for copy in fetch[4:8]:
+    for copy in fetch[2:6]:
         copy.wait()
     embed = embed_ref[...]
     high, low = in_two(embed)
@@ -146,109 +118,115 @@
     table_ref[0:8, :] = inner(scaled[0], high) + (inner(scaled[0], low) + inner(scaled[1], high))
     table_ref[8:16, :] = inner(ones, squares[0]) + inner(ones, squares[1])
 
-    steps = rows * (WIDE // LANES)
-    lines = span // steps
-
-    def embedding(pair, step):
-        at = pl.ds(pl.multiple_of(step * (lines * vr), 16), lines * vr)
-        cols = slice(pair * WIDE, (pair + 1) * WIDE)
-        total = jnp.dot(mark_ref[at, :], split_ref[0, :, cols], preferred_element_type=f32)
-        total = total + jnp.dot(mark_ref[at, :], split_ref[1, :, cols], preferred_element_type=f32)
-        emb_ref[pair][pl.ds(step * lines, lines)] = total.reshape(lines, vr, WIDE)
-
-    def convolution(pair, step):
-        r, tile = step // (WIDE // LANES), step % (WIDE // LANES)
-        at = (pl.ds(pl.multiple_of(r * RUNS, RUNS), RUNS), pl.ds(pl.multiple_of(tile * LANES, LANES), LANES))
-        cols = pl.ds(pl.multiple_of(pair * WIDE + tile * LANES, LANES), LANES)
-        length = len_ref[r]
-        taps = [jnp.broadcast_to(rows_ref[k : k + 1, cols], (RUNS, LANES)) for k in range(kernel)]
-        window = [emb_ref[pair][k, at[0], at[1]] for k in range(kernel - 1)]
-        for j in range(-2, run + 2):
-            window.append(emb_ref[pair][j + LEFT, at[0], at[1]])
-            total = taps[0] * window[0]
-            for k in range(1, kernel):
-                total = total + taps[k] * window[k]
-            window = window[1:]
-            real = base < length - j
-            if j < 0:
-                real = real & (base >= -j)
-            conv_ref[pair][j + 2, at[0], at[1]] = jnp.where(real, total, 0.0)
+    chunk = 2 * LANES
+    lines = chunk // vr
+
+    def embedding(step, carry):
+        marks = []
+        for i in range(chunk // LANES):
+            column = step * (chunk // LANES) + i
+            bytes_here = jnp.broadcast_to(line_ref[pl.ds(column, 1), :], (vocab, LANES))
+            marks.append(jnp.where(bytes_here == iota((vocab, LANES), 0).astype(f32), 1.0, 0.0))
+            line = column * group + iota((1, LANES), 1) // vr
+            inside = ((line >= LEFT) & (line < LEFT + run)).astype(f32)
+            seen_ref[...] = seen_ref[...] + marks[i] * inside
+        marks = jnp.concatenate(marks, axis=1).astype(jnp.bfloat16)
+        turn_ref[:, pl.ds(pl.multiple_of(step * chunk, chunk), chunk)] = marks
+        total = lax.dot_general(marks, split_ref[0], TN, preferred_element_type=f32)
+        total = total + lax.dot_general(marks, split_ref[1], TN, preferred_element_type=f32)
+        emb_ref[pl.ds(step * lines, lines)] = total.reshape(lines, vr, feat)
+        return carry
+
+    lax.fori_loop(0, span // lines, embedding, 0)
+    for i in range(vocab // vr):
+        seen = jnp.sum(seen_ref[i * vr : (i + 1) * vr, :], axis=1, keepdims=True)
+        pack_ref[SEEN + i] = jnp.broadcast_to(seen, (vr, LANES))
+    keeps = [
+        pltpu.make_async_copy(turn_ref, mark_hbm, sems.at[1, 0]), pltpu.make_async_copy(emb_ref, emb_hbm, sems.at[1, 1])
+    ]
+    for copy in keeps:
+        copy.start()
 
     size = RUNS * half
     order = iota((size, size), 0)
     order = (iota((size, size), 1) == order % RUNS * half + order // RUNS).astype(f32)
     order_ref[...] = order.astype(jnp.bfloat16)
 
-    def reorder(r):
-        order = order_ref[...]
-        at = pl.ds(pl.multiple_of(r * RUNS, RUNS), RUNS)
-        for pair in range(pairs):
-            cols = slice(pair * WIDE, (pair + 1) * WIDE)
-            parts = in_two(grad_ref[pl.ds(pl.multiple_of(r * size, 8), size), cols])
-            moved = jnp.dot(order, parts[0], preferred_element_type=f32)
-            moved = moved + jnp.dot(order, parts[1], preferred_element_type=f32)
-            cot_ref[:, at, cols] = moved.reshape(half, RUNS, WIDE)
-
-    keeps = [keep_mark]
-    for stage in range(pairs + 1):
-
-        def both(step, carry):
-            if stage < pairs:
-                embedding(stage, step)
-            if stage > 0:
-                convolution(stage - 1, step)
-            return carry
-
-        lax.fori_loop(0, steps, both, 0)
-        if stage < pairs:
-            cols = pl.ds(stage * WIDE, WIDE)
-            keeps.append(pltpu.make_async_copy(emb_ref[stage], emb_hbm.at[:, :, cols], sems.at[1, 1 + stage]))
-            keeps[-1].start()
-        if stage > 0:
-            cols = pl.ds((stage - 1) * WIDE, WIDE)
-            keeps.append(
-                pltpu.make_async_copy(conv_ref[stage - 1], conv_hbm.at[:, :, cols], sems.at[2, stage - 1])
-            )
-            keeps[-1].start()
+    def convolution(step, carry):
+        r, pair = step % rows, step // rows
+        sub = pl.ds(pl.multiple_of(r * RUNS, RUNS), RUNS)
+        length = len_ref[r]
+        for tile in range(WIDE // LANES):
+            cols = pl.ds(pl.multiple_of(pair * WIDE + tile * LANES, LANES), LANES)
+            taps = [jnp.broadcast_to(rows_ref[k : k + 1, cols], (RUNS, LANES)) for k in range(kernel)]
+            window = [emb_ref[k, sub, cols] for k in range(kernel - 1)]
+            for j in range(-2, run + 2):
+                window.append(emb_ref[j + LEFT, sub, cols])
+                total = taps[0] * window[0]
+                for k in range(1, kernel):
+                    total = total + taps[k] * window[k]
+                window = window[1:]
+                real = base < length - j
+                if j < 0:
+                    real = real & (base >= -j)
+                conv_ref[j + 2, sub, cols] = jnp.where(real, total, 0.0)
+        return carry
+
+    lax.fori_loop(0, rows * (feat // WIDE), convolution, 0)
+    keeps.append(pltpu.make_async_copy(conv_ref.at[0 : run + 4], conv_hbm, sems.at[2, 0]))
+    keeps[-1].start()
 
     block = 4
     slices = run + 4
     zero = jnp.zeros((RUNS, LANES), f32)
-    tile_at = [(t * LANES // WIDE, slice(t * LANES % WIDE, t * LANES % WIDE + LANES)) for t in range(feat // LANES)]
-
-    def lagged(r, carry):
-        at = pl.ds(pl.multiple_of(r * RUNS, RUNS), RUNS)
-        values = [zero] * 6
-        for first in range(0, slices, block):
+    parts = 4
+    portion = slices // parts
+
+    def lagged(step, carry):
+        at = pl.ds(pl.multiple_of(step // parts * RUNS, RUNS), RUNS)
+        begin = step % parts * portion
+        values = [jnp.where(begin == 0, 0.0, pack_ref[lag, at, :]) for lag in range(6)]
+        for first in range(0, portion, block):
+            some = min(block, portion - first)
             acc = {}
-            for tile, (pair, cols) in enumerate(tile_at):
-                u = [conv_ref[pair][first + i, at, cols] for i in range(min(block + 5, slices - first))]
-                for i in range(block):
-                    for lag in range(min(6, slices - first - i)):
+            for tile in range(feat // LANES):
+                cols = slice(tile * LANES, (tile + 1) * LANES)
+                u = [conv_ref[begin + (first + i), at, cols] for i in range(some + 5)]
+                for i in range(some):
+                    for lag in range(6):
                         term = u[i] * u[i + lag]
                         acc[i, lag] = term if tile == 0 else acc[i, lag] + term
             for i, lag in acc:
-                here = lane == first + (i + OFF - 2)
+                here = lane == begin + (first + i + OFF - 2)
                 values[lag] = jnp.where(here, jnp.sum(acc[i, lag], axis=1, keepdims=True), values[lag])
         for lag in range(6):
             pack_ref[lag, at, :] = values[lag]
-        reorder(r)
+
+        pair = jnp.minimum(step % parts, feat // WIDE - 1)
+        wide = pl.ds(pl.multiple_of(pair * WIDE, LANES), WIDE)
+        high, low = in_two(grad_ref[pl.ds(pl.multiple_of(step // parts * size, 8), size), wide])
+        moved = jnp.dot(order_ref[...], high, preferred_element_type=f32)
+        moved = moved + jnp.dot(order_ref[...], low, preferred_element_type=f32)
+        cot_ref[:, at, wide] = moved.reshape(half, RUNS, WIDE)
         return carry
 
-    fetch[8].wait()
-    lax.fori_loop(0, rows, lagged, 0)
+    conv_ref[slices:] = jnp.zeros((conv_ref.shape[0] - slices, vr, feat), f32)
+    fetch[6].wait()
+    lax.fori_loop(0, rows * parts, lagged, 0)
     keeps.append(pltpu.make_async_copy(cot_ref, cot_hbm, sems.at[3, 0]))
     keeps[-1].start()
+
     def crossed(r, carry):
         at = pl.ds(pl.multiple_of(r * RUNS, RUNS), RUNS)
         values = [zero] * 7
         for first in range(0, half, block):
             acc = {}
-            for tile, (pair, cols) in enumerate(tile_at):
-                u = [conv_ref[pair][2 * first + i, at, cols] for i in range(2 * block + 4)]
+            for tile in range(feat // LANES):
+                cols = slice(tile * LANES, (tile + 1) * LANES)
+                u = [conv_ref[2 * first + i, at, cols] for i in range(2 * block + 4)]
                 bias = jnp.broadcast_to(rows_ref[BIAS : BIAS + 1, tile * LANES : (tile + 1) * LANES], (RUNS, LANES))
                 for i in range(block):
-                    g = cot_ref[first + i, at, tile * LANES : (tile + 1) * LANES]
+                    g = cot_ref[first + i, at, cols]
                     terms = [g * u[2 * i + d] for d in range(6)] + [g * bias]
                     for d in range(7):
                         acc[i, d] = terms[d] if tile == 0 else acc[i, d] + terms[d]
@@ -265,7 +243,7 @@
         return jnp.sum(jnp.sum(x, axis=1, keepdims=True), axis=0, keepdims=True)
 
     def lookups(r, sums):
-        at = pl.ds(pl.multiple_of(r * RUNS, RUNS), RUNS)
+        at = slice(r * RUNS, (r + 1) * RUNS)
         ids = pack_ref[IDS, at, :].astype(jnp.int32)
         real = ids >= 0
         low = jnp.where(real, ids, 0)
@@ -294,7 +272,9 @@
         new = (own * look(8), own, own * biased, own * pack_ref[0, at, :], own * (1 - lane % 2).astype(f32))
         return tuple(a + b for a, b in zip(sums, new))
 
-    sums = lax.fori_loop(0, rows, lookups, (zero,) * 5)
+    sums = (zero,) * 5
+    for r in range(rows):
+        sums = lookups(r, sums)
     sums_ref[...] = spread([total_of(x) for x in sums], sums_ref.shape[0])
     for copy in keeps:
         copy.wait()
@@ -488,7 +468,7 @@
 
 def back_kernel(
     sizes, first_hbm, second_hbm, pack_hbm, state_hbm, mark_hbm, embed_hbm, conv_hbm, emb_hbm, cot_hbm,
-    out_hbm, keep_hbm, send_hbm,
+    out_hbm, keep_ref, send_ref,
     first_ref, second_ref, pack_ref, state_ref, mark_ref, embed_ref, rows_ref, turn_ref, out_ref, order_ref,
     narrow_ref, acc_ref, pay_ref, conv_ref, emb_ref, cot_ref, back_ref, sems,
 ):
@@ -756,16 +736,38 @@
             pay_ref[end + place // 8, place % 8 : place % 8 + 1, :] = row[:, tile * LANES : (tile + 1) * LANES]
     core = lax.axis_index("seq") % 2
     part = total_tiles // 2
-    halves = [
-        pltpu.make_async_copy(pay_ref.at[pl.ds(core * part, part)], keep_hbm, sems.at[0, 0]),
-        pltpu.make_async_copy(pay_ref.at[pl.ds((1 - core) * part, part)], send_hbm, sems.at[1, 0]),
-    ]
-    for copy in halves:
-        copy.start()
+    keep_ref[...] = pay_ref[pl.ds(core * part, part)]
+    send_ref[...] = pay_ref[pl.ds((1 - core) * part, part)]
     for unit in range(units):
         stored(unit).wait()
-    for copy in halves:
-        copy.wait()
+
+
+def finish_kernel(feat, mine_ref, other_ref, table_hbm, taps_ref, bias_ref, scorer_ref, sems):
+    core = lax.axis_index("seq") % 2
+    tiles = feat // LANES
+    part = mine_ref.shape[0]
+    rest = table_hbm.shape[0] - part
+    for side in range(2):
+
+        @pl.when(core == side)
+        def _():
+            first, second = (mine_ref, other_ref) if side == 0 else (other_ref, mine_ref)
+            copies = (
+                pltpu.make_async_copy(first, table_hbm.at[0:part], sems.at[0]),
+                pltpu.make_async_copy(second.at[0:rest], table_hbm.at[part : part + rest], sems.at[1]),
+            )
+            for copy in copies:
+                copy.start()
+            lines = []
+            for i in range(taps_ref.shape[0] + 2):
+                places = [i * tiles + tile for tile in range(tiles)]
+                lines.append([second[rest + p // 8, p % 8 : p % 8 + 1, :] for p in places])
+            for i in range(taps_ref.shape[0]):
+                taps_ref[i : i + 1, :] = jnp.concatenate(lines[i], axis=1)
+            bias_ref[...] = jnp.concatenate(lines[-2], axis=1).reshape(feat)
+            scorer_ref[...] = jnp.concatenate(lines[-1], axis=1).reshape(feat)
+            for copy in copies:
+                copy.wait()
 
 
 def exchanged(x):
@@ -789,7 +791,7 @@
     chunk = (others, x.shape[0] * x.shape[1] // others, 1, LANES)
     part = jnp.sum(traded(x.reshape(chunk)), axis=0)
     x = traded(jnp.broadcast_to(part[None], chunk)).reshape(x.shape)
-    return x, partner(x, "seq", 1), lax.axis_index("seq") % 2 == 1
+    return x, partner(x, "seq", 1)
 
 
 def on_device(byte_ids, lengths, embed, conv_weight, conv_bias, score_weight, out_grad):
@@ -807,11 +809,11 @@
     struct = jax.ShapeDtypeStruct
     sem = pltpu.SemaphoreType.DMA
 
-    params = pltpu.CompilerParams(vmem_limit_bytes=63 * 1024 * 1024)
+    params = pltpu.CompilerParams(vmem_limit_bytes=60 * 1024 * 1024)
 
     up = [(i, i + 1) for i in range(count - 1)]
-    left = lax.ppermute(byte_ids, "seq", up)
-    right = lax.ppermute(byte_ids, "seq", [(j, i) for i, j in up])
+    left = pltpu.with_memory_space_constraint(lax.ppermute(byte_ids, "seq", up), pltpu.VMEM)
+    right = pltpu.with_memory_space_constraint(lax.ppermute(byte_ids, "seq", [(j, i) for i, j in up]), pltpu.VMEM)
 
     pairs = feat // WIDE
     bf16 = jnp.bfloat16
@@ -826,21 +828,17 @@
     def scratch(like):
         return pltpu.VMEM(like.shape, like.dtype)
 
-    def per_pair(like):
-        return [pltpu.VMEM((*like.shape[:-1], WIDE), like.dtype)] * pairs
-
     emb, conv, cot, mark, packed, first = pl.pallas_call(
         functools.partial(stats_kernel, sizes),
-        out_shape=(wide_emb, wide_conv, wide_cot, marks, pack, sums),
-        in_specs=[HBM] * 9, out_specs=(HBM,) * 4 + (VMEM,) * 2,
+        out_shape=(*(pltpu.HBM(x.shape, x.dtype) for x in (wide_emb, wide_conv, wide_cot, marks, pack)), pltpu.VMEM(sums.shape, f32)),
+        in_specs=[HBM, VMEM, VMEM] + [HBM] * 6, out_specs=(HBM,) * 4 + (VMEM,) * 2,
         scratch_shapes=[
-            scratch(byte_ids), scratch(byte_ids), scratch(byte_ids), pltpu.SMEM((rows,), jnp.int32), scratch(embed),
+            scratch(byte_ids), pltpu.SMEM((rows,), jnp.int32), scratch(embed),
             scratch(conv_weight), scratch(conv_bias), scratch(score_weight), pltpu.VMEM((rows * half, feat), f32),
             pltpu.VMEM((2, vocab, feat), bf16), pltpu.VMEM((16, vocab), f32), pltpu.VMEM((8, feat), f32),
-            pltpu.VMEM((span * vr, vocab), bf16), scratch(marks), pltpu.VMEM((LANES // vr, vr, vocab), f32),
-            pltpu.VMEM((-(-span * vr // LANES // 8) * 8, LANES), f32), pltpu.VMEM((vocab, LANES), f32),
-            pltpu.VMEM((half, half), bf16), pltpu.VMEM((vr, LANES), jnp.int32),
-            *per_pair(wide_emb), *per_pair(wide_conv), scratch(wide_cot), sem((4, 9)),
+            scratch(marks), pltpu.VMEM((-(-span * vr // LANES // 8) * 8, LANES), f32), pltpu.VMEM((vocab, LANES), f32),
+            pltpu.VMEM((half, half), bf16), pltpu.VMEM((vr, LANES), jnp.int32), scratch(wide_emb),
+            pltpu.VMEM((run + 12, vr, feat), f32), scratch(wide_cot), sem((4, 9)),
         ],
         compiler_params=params, name="stats",
     )(
@@ -851,7 +849,7 @@
 
     states, second = pl.pallas_call(
         functools.partial(score_kernel, sizes),
-        out_shape=(state, sums),
+        out_shape=(pltpu.HBM(state.shape, f32), pltpu.VMEM(sums.shape, f32)),
         in_specs=[VMEM] * 2, out_specs=(VMEM, VMEM), scratch_shapes=[pltpu.VMEM((8, feat), f32)],
         compiler_params=params, name="score",
     )(first, packed)
@@ -862,8 +860,8 @@
     parts = struct((lines // 16, 8, LANES), f32)
     blocks, keep, send = pl.pallas_call(
         functools.partial(back_kernel, sizes),
-        out_shape=(struct((rows * half, feat), f32), parts, parts),
-        in_specs=[HBM] * 9, out_specs=(HBM, HBM, HBM),
+        out_shape=(pltpu.HBM((rows * half, feat), f32), pltpu.VMEM(parts.shape, f32), pltpu.VMEM(parts.shape, f32)),
+        in_specs=[HBM] * 9, out_specs=(HBM, VMEM, VMEM),
         scratch_shapes=[
             scratch(sums), scratch(sums), scratch(pack), scratch(state), scratch(marks), scratch(embed),
             pltpu.VMEM((8, feat), f32), pltpu.VMEM((half // RUNS, RUNS, WIDE), f32),
@@ -875,11 +873,18 @@
         compiler_params=params, name="back",
     )(first, second, packed, states, mark, embed, conv, emb, cot)
 
-    mine, other, swapped = summed_over_devices(keep, send)
-    whole = jnp.where(swapped, jnp.concatenate([other, mine]), jnp.concatenate([mine, other]))
-    table = whole[: vocab * tiles // 8].reshape(vocab // 8, tiles, 8, LANES).transpose(0, 2, 1, 3).reshape(vocab, feat)
-    extra = whole[vocab * tiles // 8 :].reshape(-1, LANES)[: (kernel + 2) * tiles].reshape(kernel + 2, feat)
-    return blocks.reshape(rows, half, feat), table, extra[:kernel], extra[kernel], extra[kernel + 1]
+    mine, other = summed_over_devices(keep, send)
+    table, taps_grad, bias_grad, scorer_grad = pl.pallas_call(
+        functools.partial(finish_kernel, feat),
+        out_shape=(
+            pltpu.HBM((vocab * tiles // 8, 8, LANES), f32), struct((kernel, feat), f32), struct((feat,), f32),
+            struct((feat,), f32),
+        ),
+        in_specs=[VMEM, VMEM], out_specs=(HBM, VMEM, VMEM, VMEM), scratch_shapes=[sem((2,))],
+        compiler_params=pltpu.CompilerParams(vmem_limit_bytes=8 * 1024 * 1024), name="finish",
+    )(mine, other)
+    table = table.reshape(vocab // 8, tiles, 8, LANES).transpose(0, 2, 1, 3).reshape(vocab, feat)
+    return blocks.reshape(rows, half, feat), table, taps_grad, bias_grad, scorer_grad
 
 
 def solution(mesh):

time: 117 us -> 110 us (0.940)
  local copies, waits for them, and re-layouts: 2.96 us -> 0.21 us
  Pallas kernels: 44.2 us -> 42.5 us
    pallas_call x3 -> x4, Pallas kernels: 44.2 us -> 42.5 us  [the longest x1 21.7 us: on_device(): pl.pallas_call(functools.partial(back_kernel, sizes), out_shape=(pltpu.HB...]
    slice x3 -> x0, local copies, waits for them, and re-layouts: 1.54 us -> none  [the longest x1 0.93 us: on_device(): whole[:vocab * tiles // 8].reshape(vocab // 8, tiles, 8, LANES)]
where the time goes in v3:
time: 110 us
  blocking collectives  55 us (50%)
  Pallas kernels  42.5 us (39%)
  waiting for transfers between devices  7.52 us (7%)
  starting transfers between devices  3.76 us (3%)
    all_to_all x2, blocking collectives, traded(): return lax.all_to_all(x, AXES, 0, 0, tiled=True, axis_index_groups=groups)  31.8 us
    all_to_all x2, blocking collectives, exchanged(): return lax.all_to_all(x, AXES, 0, 0, tiled=True)  23.2 us
    pallas_call x1, Pallas kernels, on_device(): pl.pallas_call(functools.partial(back_kernel, sizes), out_shape=(pltpu.HB...  21.7 us
    pallas_call x1, Pallas kernels, on_device(): pl.pallas_call(functools.partial(stats_kernel, sizes), out_shape=(*(pltpu...  16.6 us
    ppermute x1, waiting for transfers between devices, on_device(): lax.ppermute(byte_ids, 'seq', [(j, i) for i, j in up])  4.07 us
    ppermute x2, waiting for transfers between devices, partner(): return lax.ppermute(x, axis, [(i, i ^ step) for i in range(n)])  3.44 us
    pallas_call x1, Pallas kernels, on_device(): pl.pallas_call(functools.partial(score_kernel, sizes), out_shape=(pltpu.H...  2.66 us
    ppermute x1, starting transfers between devices, on_device(): lax.ppermute(byte_ids, 'seq', up)  2.36 us
  transfers between devices with their start and end apart: 4, of which 3 were waited for; matrix products, arithmetic and copies ran while one was open for 0% of the time, Pallas kernels for 0%

profile of v3, /device:TPU:0, one launch (start us, length us, event | category | flops | bytes accessed | tf_op | source)
XLA Modules:
  0.0 110.0 jit_solution(8831800669937774000)
XLA Ops:
  0.6 2.4 %collective-permute-start = (s32[4,512]{1,0:T(4,128)}, s32[4,512]{1,0:T(4,128)S(1)}, u32[]{:S(2)}, u32[]{:S(2)}) collective-permute-start(s32[4,512]{1,0:T(4,128)} %own_hbm.1), channel_id=1, source_target_pairs={{0,1},{1,2},{2,3},{4,5},{5,6},{6,7},{8,9},{9,10},{10,11},{12,13},{... | collective-permute-start | bytes 24584 | tf_op jit(solution)/shard_map/ppermute | solution.py:815
  3.0 1.3 %collective-permute-start.1 = (s32[4,512]{1,0:T(4,128)}, s32[4,512]{1,0:T(4,128)S(1)}, u32[]{:S(2)}, u32[]{:S(2)}) collective-permute-start(s32[4,512]{1,0:T(4,128)} %own_hbm.1), channel_id=1, source_target_pairs={{1,0},{2,1},{3,2},{5,4},{6,5},{7,6},{9,8},{10,9},{11,10},{13,12},{... | collective-permute-start | bytes 24584 | tf_op jit(solution)/shard_map/ppermute | solution.py:816
  4.3 0.0 collective-permute-done.left_ref
  4.3 4.1 %collective-permute-done.1.right_ref = s32[4,512]{1,0:T(4,128)S(1)} collective-permute-done((s32[4,512]{1,0:T(4,128)}, s32[4,512]{1,0:T(4,128)S(1)}, u32[]{:S(2)}, u32[]{:S(2)}) %collective-permute-start.1) | collective-permute-done | bytes 8224 | tf_op jit(solution)/shard_map/ppermute | solution.py:816
  8.4 16.6 %stats.1 = (f32[72,32,768]{2,1,0:T(8,128)}, f32[68,32,768]{2,1,0:T(8,128)}, f32[32,32,768]{2,1,0:T(8,128)}, bf16[256,2304]{1,0:T(8,128)(2,1)}, f32[26,32,128]{2,1,0:T(8,128)}, /*index=5*/f32[32,1,128]{2,1,0:T(1,128)S(1)}) custom-call(s32[4,512]{1,0:T(4,128)} %own_hbm.1, s32[4,512]{1,0:T(4,128)S(1)} %collective-permute-done.left_ref, ...), custom_call_target="tpu_custom_call" | custom-call | tf_op jit(solution)/shard_map/stats/pallas_call | solution.py:831
  25.0 13.8 %all_to_all.20.first_ref.first_hbm = f32[32,1,128]{2,1,0:T(1,128)} all-to-all(f32[32,1,128]{2,1,0:T(1,128)S(1)} %get-tuple-element.20), channel_id=1, replica_groups=mesh['rows'=8,'seq'=4] {'rows','seq'}, dimensions={0} | all-to-all | bytes 32768 | tf_op jit(solution)/shard_map/all_to_all | solution.py:774
  38.8 2.7 %score.1 = (f32[20,32,128]{2,1,0:T(8,128)}, f32[32,1,128]{2,1,0:T(1,128)S(1)}) custom-call(f32[32,1,128]{2,1,0:T(1,128)} %all_to_all.20.first_ref.first_hbm, f32[26,32,128]{2,1,0:T(8,128)} %get-tuple-element.21.dots_ref.pack_hbm), custom_call_target="tpu_custom_call" | custom-call | tf_op jit(solution)/shard_map/score/pallas_call | solution.py:850
  41.5 9.4 %all_to_all.21.second_hbm = f32[32,1,128]{2,1,0:T(1,128)} all-to-all(f32[32,1,128]{2,1,0:T(1,128)S(1)} %get-tuple-element.22), channel_id=1, replica_groups=mesh['rows'=8,'seq'=4] {'rows','seq'}, dimensions={0} | all-to-all | bytes 32768 | tf_op jit(solution)/shard_map/all_to_all | solution.py:774
  50.8 21.7 %back.1 = (f32[1024,768]{1,0:T(8,128)}, f32[100,8,128]{2,1,0:T(8,128)S(1)}, f32[100,8,128]{2,1,0:T(8,128)S(1)}) custom-call(f32[32,1,128]{2,1,0:T(1,128)} %all_to_all.20.first_ref.first_hbm, f32[32,1,128]{2,1,0:T(1,128)} %all_to_all.21.second_hbm, f32[26,32,128]{2,1,0:T(8,128)} %get-tuple-element.21.dots_ref.pack_hbm, ...), custom_call_target="tpu_custom_call" | custom-call | tf_op jit(solution)/shard_map/back/pallas_call | solution.py:861
  72.6 0.1 collective-permute-start.2
  72.7 1.7 %collective-permute-done.2 = f32[100,8,128]{2,1,0:T(8,128)S(1)} collective-permute-done((f32[100,8,128]{2,1,0:T(8,128)S(1)}, f32[100,8,128]{2,1,0:T(8,128)S(1)}, u32[]{:S(2)}, u32[]{:S(2)}) %collective-permute-start.2) | collective-permute-done | bytes 409632 | tf_op jit(solution)/shard_map/ppermute | solution.py:779
  74.4 0.1 add.3
  74.4 16.1 %all_to_all.22 = f32[16,50,1,128]{3,2,1,0:T(1,128)S(1)} all-to-all(f32[16,50,1,128]{3,2,1,0:T(1,128)S(1)} %bitcast.12), channel_id=1, replica_groups={{0,2,4,6,8,10,12,14,16,18,20,22,24,26,28,30},{1,3,5,7,9,11,13,15,17,19,..., dimensions={0} | all-to-all | bytes 819200 | tf_op jit(solution)/shard_map/all_to_all | solution.py:788
  90.5 0.3 reduce_sum.9
  90.7 0.2 broadcast_in_dim.2
  91.0 15.7 %all_to_all.23 = f32[16,50,1,128]{3,2,1,0:T(1,128)S(1)} all-to-all(f32[16,50,1,128]{3,2,1,0:T(1,128)S(1)} %broadcast_in_dim.2), channel_id=1, replica_groups={{0,2,4,6,8,10,12,14,16,18,20,22,24,26,28,30},{1,3,5,7,9,11,13,15,17,19,..., dimensions={0} | all-to-all | bytes 819200 | tf_op jit(solution)/shard_map/all_to_all | solution.py:788
  106.7 0.0 collective-permute-start.3
  106.7 1.7 %collective-permute-done.3.other_ref = f32[100,8,128]{2,1,0:T(8,128)S(1)} collective-permute-done((f32[100,8,128]{2,1,0:T(8,128)S(1)}, f32[100,8,128]{2,1,0:T(8,128)S(1)}, u32[]{:S(2)}, u32[]{:S(2)}) %collective-permute-start.3) | collective-permute-done | bytes 409632 | tf_op jit(solution)/shard_map/ppermute | solution.py:779
  108.5 1.5 %finish.1 = (f32[192,8,128]{2,1,0:T(8,128)}, f32[4,768]{1,0:T(4,128)}, f32[768]{0:T(1024)}, f32[768]{0:T(1024)}) custom-call(f32[100,8,128]{2,1,0:T(8,128)S(1)} %bitcast.10, f32[100,8,128]{2,1,0:T(8,128)S(1)} %collective-permute-done.3.other_ref), custom_call_target="tpu_custom_call" | custom-call | tf_op jit(solution)/shard_map/finish/pallas_call | solution.py:877
Async XLA Ops:
  0.6 3.7 %collective-permute-start = (s32[4,512]{1,0:T(4,128)}, s32[4,512]{1,0:T(4,128)S(1)}, u32[]{:S(2)}, u32[]{:S(2)}) collective-permute-start(s32[4,512]{1,0:T(4,128)} %own_hbm.1), channel_id=1, source_target_pairs={{0,1},{1,2},{2,3},{4,5},{5,6},{6,7},{8,9},{9,10},{10,11},{12,13},{... | collective-permute-start | bytes 24584 | tf_op jit(solution)/shard_map/ppermute | solution.py:815
  3.0 5.4 %collective-permute-start.1 = (s32[4,512]{1,0:T(4,128)}, s32[4,512]{1,0:T(4,128)S(1)}, u32[]{:S(2)}, u32[]{:S(2)}) collective-permute-start(s32[4,512]{1,0:T(4,128)} %own_hbm.1), channel_id=1, source_target_pairs={{1,0},{2,1},{3,2},{5,4},{6,5},{7,6},{9,8},{10,9},{11,10},{13,12},{... | collective-permute-start | bytes 24584 | tf_op jit(solution)/shard_map/ppermute | solution.py:816
  72.6 1.8 %collective-permute-start.2 = (f32[100,8,128]{2,1,0:T(8,128)S(1)}, f32[100,8,128]{2,1,0:T(8,128)S(1)}, u32[]{:S(2)}, u32[]{:S(2)}) collective-permute-start(f32[100,8,128]{2,1,0:T(8,128)S(1)} %get-tuple-element.30), channel_id=1, source_target_pairs={{0,1},{1,0},{2,3},{3,2},{4,5},{5,4},{6,7},{7,6},{8,9},{9,8},{10,11... | collective-permute-start | bytes 1228808 | tf_op jit(solution)/shard_map/ppermute | solution.py:779
  106.7 1.7 %collective-permute-start.3 = (f32[100,8,128]{2,1,0:T(8,128)S(1)}, f32[100,8,128]{2,1,0:T(8,128)S(1)}, u32[]{:S(2)}, u32[]{:S(2)}) collective-permute-start(f32[100,8,128]{2,1,0:T(8,128)S(1)} %bitcast.9), channel_id=1, source_target_pairs={{0,1},{1,0},{2,3},{3,2},{4,5},{5,4},{6,7},{7,6},{8,9},{9,8},{10,11... | collective-permute-start | bytes 1228808 | tf_op jit(solution)/shard_map/ppermute | solution.py:779

commit v4 on v3

--- a/solution.py
+++ b/solution.py
@@ -108,20 +108,31 @@
     for tile in range(feat // LANES):
         at = slice(tile % 4 * 8, tile % 4 * 8 + 8)
         pack_ref[WEIGHTS + tile // 4, at, :] = rows_ref[:, tile * LANES : (tile + 1) * LANES]
+    table_ref[...] = jnp.zeros_like(table_ref)
 
     def inner(a, b):
         return lax.dot_general(a, b, NT, preferred_element_type=f32)
 
-    scaled = in_two(jnp.concatenate([taps * scorer, taps * bias], axis=0))
-    ones = jnp.ones((8, feat), jnp.bfloat16)
-    squares = in_two(embed * embed)
-    table_ref[0:8, :] = inner(scaled[0], high) + (inner(scaled[0], low) + inner(scaled[1], high))
-    table_ref[8:16, :] = inner(ones, squares[0]) + inner(ones, squares[1])
+    def products(tile):
+        cols = pl.ds(pl.multiple_of(tile * LANES, LANES), LANES)
+        taps = rows_ref[0:kernel, cols]
+        scaled = jnp.concatenate(
+            [taps * rows_ref[SCORER : SCORER + 1, cols], taps * rows_ref[BIAS : BIAS + 1, cols]], axis=0
+        )
+        scaled = in_two(scaled)
+        high, low = split_ref[0, :, cols], split_ref[1, :, cols]
+        ones = jnp.ones((8, LANES), jnp.bfloat16)
+        some = embed_ref[:, cols]
+        squares = in_two(some * some)
+        table_ref[0:8, :] = table_ref[0:8, :] + (
+            inner(scaled[0], high) + (inner(scaled[0], low) + inner(scaled[1], high))
+        )
+        table_ref[8:16, :] = table_ref[8:16, :] + (inner(ones, squares[0]) + inner(ones, squares[1]))
 
     chunk = 2 * LANES
     lines = chunk // vr
 
-    def embedding(step, carry):
+    def embedding(step):
         marks = []
         for i in range(chunk // LANES):
             column = step * (chunk // LANES) + i
@@ -135,9 +146,18 @@
         total = lax.dot_general(marks, split_ref[0], TN, preferred_element_type=f32)
         total = total + lax.dot_general(marks, split_ref[1], TN, preferred_element_type=f32)
         emb_ref[pl.ds(step * lines, lines)] = total.reshape(lines, vr, feat)
+
+    chunks, tiles = span // lines, feat // LANES
+    trips = next(n for n in (3, 1) if chunks % n == 0 and tiles % n == 0)
+
+    def some_chunks(trip, carry):
+        for i in range(chunks // trips):
+            embedding(trip * (chunks // trips) + i)
+        for i in range(tiles // trips):
+            products(trip * (tiles // trips) + i)
         return carry
 
-    lax.fori_loop(0, span // lines, embedding, 0)
+    lax.fori_loop(0, trips, some_chunks, 0)
     for i in range(vocab // vr):
         seen = jnp.sum(seen_ref[i * vr : (i + 1) * vr, :], axis=1, keepdims=True)
         pack_ref[SEEN + i] = jnp.broadcast_to(seen, (vr, LANES))
@@ -173,51 +193,79 @@
         return carry
 
     lax.fori_loop(0, rows * (feat // WIDE), convolution, 0)
-    keeps.append(pltpu.make_async_copy(conv_ref.at[0 : run + 4], conv_hbm, sems.at[2, 0]))
+    keeps.append(pltpu.make_async_copy(conv_ref, conv_hbm, sems.at[2, 0]))
     keeps[-1].start()
 
     block = 4
     slices = run + 4
     zero = jnp.zeros((RUNS, LANES), f32)
-    parts = 4
-    portion = slices // parts
-
-    def lagged(step, carry):
-        at = pl.ds(pl.multiple_of(step // parts * RUNS, RUNS), RUNS)
-        begin = step % parts * portion
-        values = [jnp.where(begin == 0, 0.0, pack_ref[lag, at, :]) for lag in range(6)]
-        for first in range(0, portion, block):
-            some = min(block, portion - first)
+    def lagged(r, carry):
+        at = pl.ds(pl.multiple_of(r * RUNS, RUNS), RUNS)
+        some = grad_ref.at[pl.ds(pl.multiple_of(r * size, 8), size), :]
+        for pair in range(feat // WIDE):
+            wide = slice(pair * WIDE, (pair + 1) * WIDE)
+            high, low = in_two(some[:, wide])
+            moved = jnp.dot(order_ref[...], high, preferred_element_type=f32)
+            moved = moved + jnp.dot(order_ref[...], low, preferred_element_type=f32)
+            cot_ref[:, at, wide] = moved.reshape(half, RUNS, WIDE)
+        values = [zero] * 6
+        for first in range(0, slices, block):
             acc = {}
             for tile in range(feat // LANES):
                 cols = slice(tile * LANES, (tile + 1) * LANES)
-                u = [conv_ref[begin + (first + i), at, cols] for i in range(some + 5)]
-                for i in range(some):
-                    for lag in range(6):
+                u = [conv_ref[first + i, at, cols] for i in range(min(block + 5, slices - first))]
+                for i in range(block):
+                    for lag in range(min(6, slices - first - i)):
                         term = u[i] * u[i + lag]
                         acc[i, lag] = term if tile == 0 else acc[i, lag] + term
             for i, lag in acc:
-                here = lane == begin + (first + i + OFF - 2)
+                here = lane == first + (i + OFF - 2)
                 values[lag] = jnp.where(here, jnp.sum(acc[i, lag], axis=1, keepdims=True), values[lag])
         for lag in range(6):
             pack_ref[lag, at, :] = values[lag]
-
-        pair = jnp.minimum(step % parts, feat // WIDE - 1)
-        wide = pl.ds(pl.multiple_of(pair * WIDE, LANES), WIDE)
-        high, low = in_two(grad_ref[pl.ds(pl.multiple_of(step // parts * size, 8), size), wide])
-        moved = jnp.dot(order_ref[...], high, preferred_element_type=f32)
-        moved = moved + jnp.dot(order_ref[...], low, preferred_element_type=f32)
-        cot_ref[:, at, wide] = moved.reshape(half, RUNS, WIDE)
         return carry
 
-    conv_ref[slices:] = jnp.zeros((conv_ref.shape[0] - slices, vr, feat), f32)
     fetch[6].wait()
-    lax.fori_loop(0, rows * parts, lagged, 0)
+    lax.fori_loop(0, rows, lagged, 0)
     keeps.append(pltpu.make_async_copy(cot_ref, cot_hbm, sems.at[3, 0]))
     keeps[-1].start()
 
-    def crossed(r, carry):
+    def total_of(x):
+        return jnp.sum(jnp.sum(x, axis=1, keepdims=True), axis=0, keepdims=True)
+
+    def lookups(r, sums):
         at = pl.ds(pl.multiple_of(r * RUNS, RUNS), RUNS)
+        ids = pack_ref[IDS, at, :].astype(jnp.int32)
+        real = ids >= 0
+        low = jnp.where(real, ids, 0)
+
+        def look(row):
+            value = jnp.zeros((RUNS, LANES), f32)
+            for part in range(vocab // LANES):
+                entry = jnp.broadcast_to(
+                    table_ref[row : row + 1, part * LANES : (part + 1) * LANES], (RUNS, LANES)
+                )
+                taken = jnp.take_along_axis(entry, low % LANES, axis=1)
+                value = jnp.where(low // LANES == part, taken, value)
+            return jnp.where(real, value, 0.0)
+
+        scored = jnp.zeros((RUNS, LANES), f32)
+        biased = jnp.zeros((RUNS, LANES), f32)
+        for k in range(kernel):
+            scored = scored + shifted(look(k), k - (kernel - 1))
+            biased = biased + shifted(look(4 + k), k - (kernel - 1))
+        inner_real = real & (lane >= OFF - 2)
+        scored = jnp.where(inner_real, scored, 0.0)
+        biased = jnp.where(inner_real, biased, 0.0)
+        pack_ref[13, at, :] = scored
+        pack_ref[14, at, :] = biased
+        own = (real & (lane >= OFF) & (lane < OFF + run)).astype(f32)
+        new = (own * look(8), own, own * biased, own * pack_ref[0, at, :], own * (1 - lane % 2).astype(f32))
+        return tuple(a + b for a, b in zip(sums, new))
+
+    def crossed(r, sums):
+        at = pl.ds(pl.multiple_of(r * RUNS, RUNS), RUNS)
+        sums = lookups(r, sums)
         values = [zero] * 7
         for first in range(0, half, block):
             acc = {}
@@ -235,46 +283,9 @@
                 values[d] = jnp.where(here, jnp.sum(acc[i, d], axis=1, keepdims=True), values[d])
         for d in range(7):
             pack_ref[6 + d, at, :] = values[d]
-        return carry
-
-    lax.fori_loop(0, rows, crossed, 0)
-
-    def total_of(x):
-        return jnp.sum(jnp.sum(x, axis=1, keepdims=True), axis=0, keepdims=True)
-
-    def lookups(r, sums):
-        at = slice(r * RUNS, (r + 1) * RUNS)
-        ids = pack_ref[IDS, at, :].astype(jnp.int32)
-        real = ids >= 0
-        low = jnp.where(real, ids, 0)
-
-        def look(row):
-            value = jnp.zeros((RUNS, LANES), f32)
-            for part in range(vocab // LANES):
-                entry = jnp.broadcast_to(
-                    table_ref[row : row + 1, part * LANES : (part + 1) * LANES], (RUNS, LANES)
-                )
-                taken = jnp.take_along_axis(entry, low % LANES, axis=1)
-                value = jnp.where(low // LANES == part, taken, value)
-            return jnp.where(real, value, 0.0)
-
-        scored = jnp.zeros((RUNS, LANES), f32)
-        biased = jnp.zeros((RUNS, LANES), f32)
-        for k in range(kernel):
-            scored = scored + shifted(look(k), k - (kernel - 1))
-            biased = biased + shifted(look(4 + k), k - (kernel - 1))
-        inner_real = real & (lane >= OFF - 2)
-        scored = jnp.where(inner_real, scored, 0.0)
-        biased = jnp.where(inner_real, biased, 0.0)
-        pack_ref[13, at, :] = scored
-        pack_ref[14, at, :] = biased
-        own = (real & (lane >= OFF) & (lane < OFF + run)).astype(f32)
-        new = (own * look(8), own, own * biased, own * pack_ref[0, at, :], own * (1 - lane % 2).astype(f32))
-        return tuple(a + b for a, b in zip(sums, new))
-
-    sums = (zero,) * 5
-    for r in range(rows):
-        sums = lookups(r, sums)
+        return sums
+
+    sums = lax.fori_loop(0, rows, crossed, (zero,) * 5)
     sums_ref[...] = spread([total_of(x) for x in sums], sums_ref.shape[0])
     for copy in keeps:
         copy.wait()
@@ -504,6 +515,7 @@
     sources = (first_hbm, second_hbm, pack_hbm, state_hbm, mark_hbm, embed_hbm)
     targets = (first_ref, second_ref, pack_ref, state_ref, mark_ref, embed_ref)
     small = [pltpu.make_async_copy(a, b, sems.at[4, i]) for i, (a, b) in enumerate(zip(sources, targets))]
+    small[2] = pltpu.make_async_copy(pack_hbm.at[IDS:], pack_ref.at[IDS:], sems.at[4, 2])
     ahead = 3
     for copy in small[:4]:
         copy.start()
@@ -587,12 +599,24 @@
         u, triple, y3, gc = {}, {}, {}, {}
         sums = [zero] * (kernel + 2)
         block = {}
+        twos, y_twos = {}, {}
         for j in range(-2, 2):
             u[j] = conv_ref[j + 2, sub, cols]
-        triple[-2] = u[-2] + u[-1] + u[0]
-        triple[-1] = u[-1] + u[0] + u[1]
+
+        def pair_of(j):
+            if j not in twos:
+                twos[j] = u[j] + u[j + 1]
+            return twos[j]
+
+        triple[-2] = pair_of(-2) + u[0]
+        triple[-1] = u[-1] + pair_of(0)
 
         def window(j):
+            if 0 <= j <= run - 3:
+                first = j if j % 2 == 0 else j + 1
+                if first not in y_twos:
+                    y_twos[first] = y3[first] + y3[first + 1]
+                return y_twos[first] + y3[j + 2 if j % 2 == 0 else j]
             near = [y3[i] for i in (j, j + 1, j + 2) if 0 <= i < run]
             return functools.reduce(lambda a, b: a + b, near) if near else zero
 
@@ -606,7 +630,7 @@
             g = g + sigma * scorer
             if 0 <= s < run:
                 g = g + lone[s]
-                g = g - fall * u[s] - fall_row
+                g = g - fall * u[s]
             g = g * factor(5, s)
             gc[s] = g
             for k in range(kernel):
@@ -624,14 +648,15 @@
         for quad in range(0, run, 4):
             for j in range(quad + 2, quad + 6):
                 u[j] = conv_ref[j + 2, sub, cols]
-            two_sums = [u[quad + 2 * p] + u[quad + 2 * p + 1] for p in range(2)]
+            two_sums = [pair_of(quad), pair_of(quad + 2)]
             four_sum = two_sums[0] + two_sums[1]
+            shares = []
             wide = zero
             for p in range(2):
                 y = None
                 xs = []
                 for j in (quad + 2 * p, quad + 2 * p + 1):
-                    triple[j] = u[j] + u[j + 1] + u[j + 2] if j % 2 else two_sums[p] + u[j + 2]
+                    triple[j] = u[j] + pair_of(j + 1) if j % 2 else two_sums[p] + u[j + 2]
                     x = factor(0, j) * u[j] + factor(1, j) * two_sums[p]
                     x = x + factor(2, j) * chosen(j, triple[j], triple[j - 1], triple[j - 2])
                     x = x + factor(3, j) * four_sum
@@ -648,10 +673,12 @@
                     y3[j] = factor(2, j) * g
                     pair = factor(1, j) * g if i == 0 else pair + factor(1, j) * g
                     wide = factor(3, j) * g if i + p == 0 else wide + factor(3, j) * g
+                shares.append(pair)
+            wide = wide - fall_row
+            for p in range(2):
+                share = shares[p] + wide
                 for j in (quad + 2 * p, quad + 2 * p + 1):
-                    lone[j] = lone[j] + pair
-            for j in range(quad, quad + 4):
-                lone[j] = lone[j] + wide
+                    lone[j] = lone[j] + share
             last = quad + 3 - 2 if quad + 4 < run else run + 1
             while settled <= last:
                 settle(settled)
@@ -838,7 +865,7 @@
             pltpu.VMEM((2, vocab, feat), bf16), pltpu.VMEM((16, vocab), f32), pltpu.VMEM((8, feat), f32),
             scratch(marks), pltpu.VMEM((-(-span * vr // LANES // 8) * 8, LANES), f32), pltpu.VMEM((vocab, LANES), f32),
             pltpu.VMEM((half, half), bf16), pltpu.VMEM((vr, LANES), jnp.int32), scratch(wide_emb),
-            pltpu.VMEM((run + 12, vr, feat), f32), scratch(wide_cot), sem((4, 9)),
+            scratch(wide_conv), scratch(wide_cot), sem((4, 9)),
         ],
         compiler_params=params, name="stats",
     )(

time: 110 us -> 107 us (0.973)
  Pallas kernels: 42.5 us -> 39 us
    pallas_call x1, Pallas kernels: 16.6 us -> 13.8 us  [on_device(): pl.pallas_call(functools.partial(stats_kernel, sizes), out_shape=(*(pltpu...]
where the time goes in v4:
time: 107 us; the launch traced here: 106 us
  blocking collectives  55 us (51%)
  Pallas kernels  39 us (36%)
  waiting for transfers between devices  7.52 us (7%)
  starting transfers between devices  3.76 us (4%)
    all_to_all x2, blocking collectives, traded(): return lax.all_to_all(x, AXES, 0, 0, tiled=True, axis_index_groups=groups)  31.8 us
    all_to_all x2, blocking collectives, exchanged(): return lax.all_to_all(x, AXES, 0, 0, tiled=True)  23.2 us
    pallas_call x1, Pallas kernels, on_device(): pl.pallas_call(functools.partial(back_kernel, sizes), out_shape=(pltpu.HB...  21 us
    pallas_call x1, Pallas kernels, on_device(): pl.pallas_call(functools.partial(stats_kernel, sizes), out_shape=(*(pltpu...  13.8 us
    ppermute x1, waiting for transfers between devices, on_device(): lax.ppermute(byte_ids, 'seq', [(j, i) for i, j in up])  4.07 us
    ppermute x2, waiting for transfers between devices, partner(): return lax.ppermute(x, axis, [(i, i ^ step) for i in range(n)])  3.44 us
    pallas_call x1, Pallas kernels, on_device(): pl.pallas_call(functools.partial(score_kernel, sizes), out_shape=(pltpu.H...  2.66 us
    ppermute x1, starting transfers between devices, on_device(): lax.ppermute(byte_ids, 'seq', up)  2.36 us
  transfers between devices with their start and end apart: 4, of which 3 were waited for; matrix products, arithmetic and copies ran while one was open for 0% of the time, Pallas kernels for 0%

profile of v4, /device:TPU:0, one launch (start us, length us, event | category | flops | bytes accessed | tf_op | source)
XLA Modules:
  0.0 106.5 jit_solution(6452267389621626332)
XLA Ops:
  0.6 2.4 %collective-permute-start = (s32[4,512]{1,0:T(4,128)}, s32[4,512]{1,0:T(4,128)S(1)}, u32[]{:S(2)}, u32[]{:S(2)}) collective-permute-start(s32[4,512]{1,0:T(4,128)} %own_hbm.1), channel_id=1, source_target_pairs={{0,1},{1,2},{2,3},{4,5},{5,6},{6,7},{8,9},{9,10},{10,11},{12,13},{... | collective-permute-start | bytes 24584 | tf_op jit(solution)/shard_map/ppermute | solution.py:842
  3.0 1.3 %collective-permute-start.1 = (s32[4,512]{1,0:T(4,128)}, s32[4,512]{1,0:T(4,128)S(1)}, u32[]{:S(2)}, u32[]{:S(2)}) collective-permute-start(s32[4,512]{1,0:T(4,128)} %own_hbm.1), channel_id=1, source_target_pairs={{1,0},{2,1},{3,2},{5,4},{6,5},{7,6},{9,8},{10,9},{11,10},{13,12},{... | collective-permute-start | bytes 24584 | tf_op jit(solution)/shard_map/ppermute | solution.py:843
  4.3 0.0 collective-permute-done.left_ref
  4.3 4.1 %collective-permute-done.1.right_ref = s32[4,512]{1,0:T(4,128)S(1)} collective-permute-done((s32[4,512]{1,0:T(4,128)}, s32[4,512]{1,0:T(4,128)S(1)}, u32[]{:S(2)}, u32[]{:S(2)}) %collective-permute-start.1) | collective-permute-done | bytes 8224 | tf_op jit(solution)/shard_map/ppermute | solution.py:843
  8.4 13.8 %stats.1 = (f32[72,32,768]{2,1,0:T(8,128)}, f32[68,32,768]{2,1,0:T(8,128)}, f32[32,32,768]{2,1,0:T(8,128)}, bf16[256,2304]{1,0:T(8,128)(2,1)}, f32[26,32,128]{2,1,0:T(8,128)}, /*index=5*/f32[32,1,128]{2,1,0:T(1,128)S(1)}) custom-call(s32[4,512]{1,0:T(4,128)} %own_hbm.1, s32[4,512]{1,0:T(4,128)S(1)} %collective-permute-done.left_ref, ...), custom_call_target="tpu_custom_call" | custom-call | tf_op jit(solution)/shard_map/stats/pallas_call | solution.py:858
  22.2 13.8 %all_to_all.20.first_ref.first_hbm = f32[32,1,128]{2,1,0:T(1,128)} all-to-all(f32[32,1,128]{2,1,0:T(1,128)S(1)} %get-tuple-element.20), channel_id=1, replica_groups=mesh['rows'=8,'seq'=4] {'rows','seq'}, dimensions={0} | all-to-all | bytes 32768 | tf_op jit(solution)/shard_map/all_to_all | solution.py:801
  36.0 2.7 %score.1 = (f32[20,32,128]{2,1,0:T(8,128)}, f32[32,1,128]{2,1,0:T(1,128)S(1)}) custom-call(f32[32,1,128]{2,1,0:T(1,128)} %all_to_all.20.first_ref.first_hbm, f32[26,32,128]{2,1,0:T(8,128)} %get-tuple-element.21.dots_ref.pack_hbm), custom_call_target="tpu_custom_call" | custom-call | tf_op jit(solution)/shard_map/score/pallas_call | solution.py:877
  38.7 9.4 %all_to_all.21.second_hbm = f32[32,1,128]{2,1,0:T(1,128)} all-to-all(f32[32,1,128]{2,1,0:T(1,128)S(1)} %get-tuple-element.22), channel_id=1, replica_groups=mesh['rows'=8,'seq'=4] {'rows','seq'}, dimensions={0} | all-to-all | bytes 32768 | tf_op jit(solution)/shard_map/all_to_all | solution.py:801
  48.1 21.0 %back.1 = (f32[1024,768]{1,0:T(8,128)}, f32[100,8,128]{2,1,0:T(8,128)S(1)}, f32[100,8,128]{2,1,0:T(8,128)S(1)}) custom-call(f32[32,1,128]{2,1,0:T(1,128)} %all_to_all.20.first_ref.first_hbm, f32[32,1,128]{2,1,0:T(1,128)} %all_to_all.21.second_hbm, f32[26,32,128]{2,1,0:T(8,128)} %get-tuple-element.21.dots_ref.pack_hbm, ...), custom_call_target="tpu_custom_call" | custom-call | tf_op jit(solution)/shard_map/back/pallas_call | solution.py:888
  69.1 0.1 collective-permute-start.2
  69.2 1.7 %collective-permute-done.2 = f32[100,8,128]{2,1,0:T(8,128)S(1)} collective-permute-done((f32[100,8,128]{2,1,0:T(8,128)S(1)}, f32[100,8,128]{2,1,0:T(8,128)S(1)}, u32[]{:S(2)}, u32[]{:S(2)}) %collective-permute-start.2) | collective-permute-done | bytes 409632 | tf_op jit(solution)/shard_map/ppermute | solution.py:806
  70.9 0.1 add.3
  71.0 16.1 %all_to_all.22 = f32[16,50,1,128]{3,2,1,0:T(1,128)S(1)} all-to-all(f32[16,50,1,128]{3,2,1,0:T(1,128)S(1)} %bitcast.12), channel_id=1, replica_groups={{0,2,4,6,8,10,12,14,16,18,20,22,24,26,28,30},{1,3,5,7,9,11,13,15,17,19,..., dimensions={0} | all-to-all | bytes 819200 | tf_op jit(solution)/shard_map/all_to_all | solution.py:815
  87.0 0.3 reduce_sum.9
  87.3 0.2 broadcast_in_dim.2
  87.5 15.7 %all_to_all.23 = f32[16,50,1,128]{3,2,1,0:T(1,128)S(1)} all-to-all(f32[16,50,1,128]{3,2,1,0:T(1,128)S(1)} %broadcast_in_dim.2), channel_id=1, replica_groups={{0,2,4,6,8,10,12,14,16,18,20,22,24,26,28,30},{1,3,5,7,9,11,13,15,17,19,..., dimensions={0} | all-to-all | bytes 819200 | tf_op jit(solution)/shard_map/all_to_all | solution.py:815
  103.2 0.0 collective-permute-start.3
  103.2 1.7 %collective-permute-done.3.other_ref = f32[100,8,128]{2,1,0:T(8,128)S(1)} collective-permute-done((f32[100,8,128]{2,1,0:T(8,128)S(1)}, f32[100,8,128]{2,1,0:T(8,128)S(1)}, u32[]{:S(2)}, u32[]{:S(2)}) %collective-permute-start.3) | collective-permute-done | bytes 409632 | tf_op jit(solution)/shard_map/ppermute | solution.py:806
  105.0 1.5 %finish.1 = (f32[192,8,128]{2,1,0:T(8,128)}, f32[4,768]{1,0:T(4,128)}, f32[768]{0:T(1024)}, f32[768]{0:T(1024)}) custom-call(f32[100,8,128]{2,1,0:T(8,128)S(1)} %bitcast.10, f32[100,8,128]{2,1,0:T(8,128)S(1)} %collective-permute-done.3.other_ref), custom_call_target="tpu_custom_call" | custom-call | tf_op jit(solution)/shard_map/finish/pallas_call | solution.py:904
Async XLA Ops:
  0.6 3.7 %collective-permute-start = (s32[4,512]{1,0:T(4,128)}, s32[4,512]{1,0:T(4,128)S(1)}, u32[]{:S(2)}, u32[]{:S(2)}) collective-permute-start(s32[4,512]{1,0:T(4,128)} %own_hbm.1), channel_id=1, source_target_pairs={{0,1},{1,2},{2,3},{4,5},{5,6},{6,7},{8,9},{9,10},{10,11},{12,13},{... | collective-permute-start | bytes 24584 | tf_op jit(solution)/shard_map/ppermute | solution.py:842
  3.0 5.4 %collective-permute-start.1 = (s32[4,512]{1,0:T(4,128)}, s32[4,512]{1,0:T(4,128)S(1)}, u32[]{:S(2)}, u32[]{:S(2)}) collective-permute-start(s32[4,512]{1,0:T(4,128)} %own_hbm.1), channel_id=1, source_target_pairs={{1,0},{2,1},{3,2},{5,4},{6,5},{7,6},{9,8},{10,9},{11,10},{13,12},{... | collective-permute-start | bytes 24584 | tf_op jit(solution)/shard_map/ppermute | solution.py:843
  69.1 1.8 %collective-permute-start.2 = (f32[100,8,128]{2,1,0:T(8,128)S(1)}, f32[100,8,128]{2,1,0:T(8,128)S(1)}, u32[]{:S(2)}, u32[]{:S(2)}) collective-permute-start(f32[100,8,128]{2,1,0:T(8,128)S(1)} %get-tuple-element.30), channel_id=1, source_target_pairs={{0,1},{1,0},{2,3},{3,2},{4,5},{5,4},{6,7},{7,6},{8,9},{9,8},{10,11... | collective-permute-start | bytes 1228808 | tf_op jit(solution)/shard_map/ppermute | solution.py:806
  103.2 1.7 %collective-permute-start.3 = (f32[100,8,128]{2,1,0:T(8,128)S(1)}, f32[100,8,128]{2,1,0:T(8,128)S(1)}, u32[]{:S(2)}, u32[]{:S(2)}) collective-permute-start(f32[100,8,128]{2,1,0:T(8,128)S(1)} %bitcast.9), channel_id=1, source_target_pairs={{0,1},{1,0},{2,3},{3,2},{4,5},{5,4},{6,7},{7,6},{8,9},{9,8},{10,11... | collective-permute-start | bytes 1228808 | tf_op jit(solution)/shard_map/ppermute | solution.py:806

commit v5 on v4

--- a/solution.py
+++ b/solution.py
@@ -34,7 +34,7 @@
 
 
 def stats_kernel(
-    sizes, own_hbm, left_ref, right_ref, len_hbm, embed_hbm, taps_hbm, bias_hbm, scorer_hbm, grad_hbm,
+    sizes, own_hbm, even_ref, odd_ref, len_hbm, embed_hbm, taps_hbm, bias_hbm, scorer_hbm, grad_hbm,
     emb_hbm, conv_hbm, cot_hbm, mark_hbm, pack_ref, sums_ref,
     own_ref, len_ref, embed_ref, taps_ref, bias_ref, scorer_ref, grad_ref,
     split_ref, table_ref, rows_ref, turn_ref, line_ref, seen_ref, order_ref, run_ref, emb_ref, conv_ref, cot_ref, sems,
@@ -63,13 +63,17 @@
             line = jnp.broadcast_to(line, (RUNS, LANES))
             line = pltpu.roll(line, shift, 1) if shift else line
             run_ref[r * RUNS + s : r * RUNS + s + 1, :] = line[0:1]
+    odd = lax.axis_index("seq") % 2 == 1
     for r in range(rows):
         own = run_ref[r * RUNS : (r + 1) * RUNS, :]
+        tail = slice(width - LANES, width)
+        left = jnp.where(odd, even_ref[r : r + 1, tail], odd_ref[r : r + 1, tail])
+        right = jnp.where(odd, odd_ref[r : r + 1, 0:LANES], even_ref[r : r + 1, 0:LANES])
         before = pltpu.roll(pltpu.roll(own, 1, 0), back, 1)
-        edge = pltpu.roll(jnp.broadcast_to(left_ref[r : r + 1, width - LANES : width], (RUNS, LANES)), OFF, 1)
+        edge = pltpu.roll(jnp.broadcast_to(left, (RUNS, LANES)), OFF, 1)
         before = jnp.where(sub == 0, edge, before)
         after = pltpu.roll(pltpu.roll(own, RUNS - 1, 0), OFF + run, 1)
-        edge = pltpu.roll(jnp.broadcast_to(right_ref[r : r + 1, 0:LANES], (RUNS, LANES)), OFF + run, 1)
+        edge = pltpu.roll(jnp.broadcast_to(right, (RUNS, LANES)), OFF + run, 1)
         after = jnp.where(sub == RUNS - 1, edge, after)
         ids = jnp.where(lane < OFF, before, jnp.where(lane < OFF + run, pltpu.roll(own, OFF, 1), after))
         place = base + lane - OFF
@@ -148,7 +152,7 @@
         emb_ref[pl.ds(step * lines, lines)] = total.reshape(lines, vr, feat)
 
     chunks, tiles = span // lines, feat // LANES
-    trips = next(n for n in (3, 1) if chunks % n == 0 and tiles % n == 0)
+    trips = next(n for n in (1,) if chunks % n == 0 and tiles % n == 0)
 
     def some_chunks(trip, carry):
         for i in range(chunks // trips):
@@ -748,7 +752,8 @@
                 pay_ref[v * tiles + pair * per + i] = part - seen * embed_ref[v * 8 : v * 8 + 8, wide]
         return carry
 
-    lax.fori_loop(0, feat // WIDE, gather, 0)
+    for pair in range(feat // WIDE):
+        gather(pair, 0)
 
     end = vocab // 8 * tiles
     pay_ref[end:] = jnp.zeros((total_tiles - end, 8, LANES), f32)
@@ -838,9 +843,9 @@
 
     params = pltpu.CompilerParams(vmem_limit_bytes=60 * 1024 * 1024)
 
-    up = [(i, i + 1) for i in range(count - 1)]
-    left = pltpu.with_memory_space_constraint(lax.ppermute(byte_ids, "seq", up), pltpu.VMEM)
-    right = pltpu.with_memory_space_constraint(lax.ppermute(byte_ids, "seq", [(j, i) for i, j in up]), pltpu.VMEM)
+    pairs_of = [[(i, i + 1) for i in range(first, count - 1, 2)] for first in range(2)]
+    near = [lax.ppermute(byte_ids, "seq", some + [(j, i) for i, j in some]) for some in pairs_of]
+    near = [pltpu.with_memory_space_constraint(x, pltpu.VMEM) for x in near]
 
     pairs = feat // WIDE
     bf16 = jnp.bfloat16
@@ -869,7 +874,7 @@
         ],
         compiler_params=params, name="stats",
     )(
-        byte_ids, left, right, lengths, embed, conv_weight, conv_bias, score_weight,
+        byte_ids, *near, lengths, embed, conv_weight, conv_bias, score_weight,
         out_grad.reshape(rows * half, feat),
     )
     first = exchanged(first)

time: 107 us -> 104 us (0.972)
  blocking collectives: 55 us -> 59.1 us
  waiting for transfers between devices: 7.52 us -> 3.83 us
  starting transfers between devices: 3.76 us -> 1.28 us
    all_to_all x2, blocking collectives: 23.2 us -> 27.3 us  [exchanged(): return lax.all_to_all(x, AXES, 0, 0, tiled=True)]
    ppermute x2, waiting for transfers between devices: 4.08 us -> 0.38 us  [on_device(): lax.ppermute(byte_ids, 'seq', some + [(j, i) for i, j in some])]
    ppermute x2, starting transfers between devices: 3.65 us -> 1.17 us  [on_device(): lax.ppermute(byte_ids, 'seq', some + [(j, i) for i, j in some])]
where the time goes in v5:
time: 104 us
  blocking collectives  59.1 us (57%)
  Pallas kernels  38.2 us (37%)
  waiting for transfers between devices  3.83 us (4%)
  starting transfers between devices  1.28 us (1%)
    all_to_all x2, blocking collectives, traded(): return lax.all_to_all(x, AXES, 0, 0, tiled=True, axis_index_groups=groups)  31.8 us
    all_to_all x2, blocking collectives, exchanged(): return lax.all_to_all(x, AXES, 0, 0, tiled=True)  27.3 us
    pallas_call x1, Pallas kernels, on_device(): pl.pallas_call(functools.partial(back_kernel, sizes), out_shape=(pltpu.HB...  20.8 us
    pallas_call x1, Pallas kernels, on_device(): pl.pallas_call(functools.partial(stats_kernel, sizes), out_shape=(*(pltpu...  13.3 us
    ppermute x2, waiting for transfers between devices, partner(): return lax.ppermute(x, axis, [(i, i ^ step) for i in range(n)])  3.44 us
    pallas_call x1, Pallas kernels, on_device(): pl.pallas_call(functools.partial(score_kernel, sizes), out_shape=(pltpu.H...  2.66 us
  transfers between devices with their start and end apart: 4, of which 3 were waited for; matrix products, arithmetic and copies ran while one was open for 0% of the time, Pallas kernels for 0%

profile of v5, /device:TPU:0, one launch (start us, length us, event | category | flops | bytes accessed | tf_op | source)
XLA Modules:
  0.0 103.6 jit_solution(13601162430014306869)
XLA Ops:
  0.6 0.5 collective-permute-start
  1.2 0.6 collective-permute-start.1
  1.8 0.4 collective-permute-done.even_ref
  2.2 0.0 collective-permute-done.1.odd_ref
  2.2 13.3 %stats.1 = (f32[72,32,768]{2,1,0:T(8,128)}, f32[68,32,768]{2,1,0:T(8,128)}, f32[32,32,768]{2,1,0:T(8,128)}, bf16[256,2304]{1,0:T(8,128)(2,1)}, f32[26,32,128]{2,1,0:T(8,128)}, /*index=5*/f32[32,1,128]{2,1,0:T(1,128)S(1)}) custom-call(s32[4,512]{1,0:T(4,128)} %own_hbm.1, s32[4,512]{1,0:T(4,128)S(1)} %collective-permute-done.even_ref, ...), custom_call_target="tpu_custom_call" | custom-call | tf_op jit(solution)/shard_map/stats/pallas_call | solution.py:863
  15.5 17.9 %all_to_all.20.first_ref.first_hbm = f32[32,1,128]{2,1,0:T(1,128)} all-to-all(f32[32,1,128]{2,1,0:T(1,128)S(1)} %get-tuple-element.20), channel_id=1, replica_groups=mesh['rows'=8,'seq'=4] {'rows','seq'}, dimensions={0} | all-to-all | bytes 32768 | tf_op jit(solution)/shard_map/all_to_all | solution.py:806
  33.4 2.7 %score.1 = (f32[20,32,128]{2,1,0:T(8,128)}, f32[32,1,128]{2,1,0:T(1,128)S(1)}) custom-call(f32[32,1,128]{2,1,0:T(1,128)} %all_to_all.20.first_ref.first_hbm, f32[26,32,128]{2,1,0:T(8,128)} %get-tuple-element.21.dots_ref.pack_hbm), custom_call_target="tpu_custom_call" | custom-call | tf_op jit(solution)/shard_map/score/pallas_call | solution.py:882
  36.1 9.4 %all_to_all.21.second_hbm = f32[32,1,128]{2,1,0:T(1,128)} all-to-all(f32[32,1,128]{2,1,0:T(1,128)S(1)} %get-tuple-element.22), channel_id=1, replica_groups=mesh['rows'=8,'seq'=4] {'rows','seq'}, dimensions={0} | all-to-all | bytes 32768 | tf_op jit(solution)/shard_map/all_to_all | solution.py:806
  45.4 20.8 %back.1 = (f32[1024,768]{1,0:T(8,128)}, f32[100,8,128]{2,1,0:T(8,128)S(1)}, f32[100,8,128]{2,1,0:T(8,128)S(1)}) custom-call(f32[32,1,128]{2,1,0:T(1,128)} %all_to_all.20.first_ref.first_hbm, f32[32,1,128]{2,1,0:T(1,128)} %all_to_all.21.second_hbm, f32[26,32,128]{2,1,0:T(8,128)} %get-tuple-element.21.dots_ref.pack_hbm, ...), custom_call_target="tpu_custom_call" | custom-call | tf_op jit(solution)/shard_map/back/pallas_call | solution.py:893
  66.2 0.1 collective-permute-start.2
  66.3 1.7 %collective-permute-done.2 = f32[100,8,128]{2,1,0:T(8,128)S(1)} collective-permute-done((f32[100,8,128]{2,1,0:T(8,128)S(1)}, f32[100,8,128]{2,1,0:T(8,128)S(1)}, u32[]{:S(2)}, u32[]{:S(2)}) %collective-permute-start.2) | collective-permute-done | bytes 409632 | tf_op jit(solution)/shard_map/ppermute | solution.py:811
  68.0 0.1 add.3
  68.1 16.1 %all_to_all.22 = f32[16,50,1,128]{3,2,1,0:T(1,128)S(1)} all-to-all(f32[16,50,1,128]{3,2,1,0:T(1,128)S(1)} %bitcast.12), channel_id=1, replica_groups={{0,2,4,6,8,10,12,14,16,18,20,22,24,26,28,30},{1,3,5,7,9,11,13,15,17,19,..., dimensions={0} | all-to-all | bytes 819200 | tf_op jit(solution)/shard_map/all_to_all | solution.py:820
  84.2 0.3 reduce_sum.9
  84.4 0.2 broadcast_in_dim.2
  84.6 15.7 %all_to_all.23 = f32[16,50,1,128]{3,2,1,0:T(1,128)S(1)} all-to-all(f32[16,50,1,128]{3,2,1,0:T(1,128)S(1)} %broadcast_in_dim.2), channel_id=1, replica_groups={{0,2,4,6,8,10,12,14,16,18,20,22,24,26,28,30},{1,3,5,7,9,11,13,15,17,19,..., dimensions={0} | all-to-all | bytes 819200 | tf_op jit(solution)/shard_map/all_to_all | solution.py:820
  100.4 0.0 collective-permute-start.3
  100.4 1.7 %collective-permute-done.3.other_ref = f32[100,8,128]{2,1,0:T(8,128)S(1)} collective-permute-done((f32[100,8,128]{2,1,0:T(8,128)S(1)}, f32[100,8,128]{2,1,0:T(8,128)S(1)}, u32[]{:S(2)}, u32[]{:S(2)}) %collective-permute-start.3) | collective-permute-done | bytes 409632 | tf_op jit(solution)/shard_map/ppermute | solution.py:811
  102.1 1.5 %finish.1 = (f32[192,8,128]{2,1,0:T(8,128)}, f32[4,768]{1,0:T(4,128)}, f32[768]{0:T(1024)}, f32[768]{0:T(1024)}) custom-call(f32[100,8,128]{2,1,0:T(8,128)S(1)} %bitcast.10, f32[100,8,128]{2,1,0:T(8,128)S(1)} %collective-permute-done.3.other_ref), custom_call_target="tpu_custom_call" | custom-call | tf_op jit(solution)/shard_map/finish/pallas_call | solution.py:909
Async XLA Ops:
  0.6 1.6 %collective-permute-start = (s32[4,512]{1,0:T(4,128)}, s32[4,512]{1,0:T(4,128)S(1)}, u32[]{:S(2)}, u32[]{:S(2)}) collective-permute-start(s32[4,512]{1,0:T(4,128)} %own_hbm.1), channel_id=1, source_target_pairs={{0,1},{2,3},{1,0},{3,2},{4,5},{6,7},{5,4},{7,6},{8,9},{10,11},{9,8... | collective-permute-start | bytes 24584 | tf_op jit(solution)/shard_map/ppermute | solution.py:847
  1.2 1.0 %collective-permute-start.1 = (s32[4,512]{1,0:T(4,128)}, s32[4,512]{1,0:T(4,128)S(1)}, u32[]{:S(2)}, u32[]{:S(2)}) collective-permute-start(s32[4,512]{1,0:T(4,128)} %own_hbm.1), channel_id=1, source_target_pairs={{1,2},{2,1},{5,6},{6,5},{9,10},{10,9},{13,14},{14,13},{17,18},{18,... | collective-permute-start | bytes 24584 | tf_op jit(solution)/shard_map/ppermute | solution.py:847
  66.2 1.8 %collective-permute-start.2 = (f32[100,8,128]{2,1,0:T(8,128)S(1)}, f32[100,8,128]{2,1,0:T(8,128)S(1)}, u32[]{:S(2)}, u32[]{:S(2)}) collective-permute-start(f32[100,8,128]{2,1,0:T(8,128)S(1)} %get-tuple-element.30), channel_id=1, source_target_pairs={{0,1},{1,0},{2,3},{3,2},{4,5},{5,4},{6,7},{7,6},{8,9},{9,8},{10,11... | collective-permute-start | bytes 1228808 | tf_op jit(solution)/shard_map/ppermute | solution.py:811
  100.4 1.7 %collective-permute-start.3 = (f32[100,8,128]{2,1,0:T(8,128)S(1)}, f32[100,8,128]{2,1,0:T(8,128)S(1)}, u32[]{:S(2)}, u32[]{:S(2)}) collective-permute-start(f32[100,8,128]{2,1,0:T(8,128)S(1)} %bitcast.9), channel_id=1, source_target_pairs={{0,1},{1,0},{2,3},{3,2},{4,5},{5,4},{6,7},{7,6},{8,9},{9,8},{10,11... | collective-permute-start | bytes 1228808 | tf_op jit(solution)/shard_map/ppermute | solution.py:811

commit v6 on v5

--- a/solution.py
+++ b/solution.py
@@ -151,17 +151,38 @@
         total = total + lax.dot_general(marks, split_ref[1], TN, preferred_element_type=f32)
         emb_ref[pl.ds(step * lines, lines)] = total.reshape(lines, vr, feat)
 
+    def convolution(begin, end):
+        for r in range(rows):
+            sub = slice(r * RUNS, (r + 1) * RUNS)
+            length = len_ref[r]
+            for tile in range(feat // LANES):
+                cols = slice(tile * LANES, (tile + 1) * LANES)
+                taps = [jnp.broadcast_to(rows_ref[k : k + 1, cols], (RUNS, LANES)) for k in range(kernel)]
+                window = [emb_ref[begin + k, sub, cols] for k in range(kernel - 1)]
+                for i in range(begin, end):
+                    window.append(emb_ref[i + kernel - 1, sub, cols])
+                    total = taps[0] * window[0]
+                    for k in range(1, kernel):
+                        total = total + taps[k] * window[k]
+                    window = window[1:]
+                    real = base < length - (i - 2)
+                    if i < 2:
+                        real = real & (base >= 2 - i)
+                    conv_ref[i, sub, cols] = jnp.where(real, total, 0.0)
+
     chunks, tiles = span // lines, feat // LANES
-    trips = next(n for n in (1,) if chunks % n == 0 and tiles % n == 0)
-
-    def some_chunks(trip, carry):
-        for i in range(chunks // trips):
-            embedding(trip * (chunks // trips) + i)
-        for i in range(tiles // trips):
-            products(trip * (tiles // trips) + i)
-        return carry
-
-    lax.fori_loop(0, trips, some_chunks, 0)
+    done = 0
+    for step in range(chunks):
+        embedding(step)
+        if step < tiles:
+            products(step)
+        ready = min(step * lines - (kernel - 1), run + 4)
+        if ready > done:
+            convolution(done, ready)
+            done = ready
+    for tile in range(chunks, tiles):
+        products(tile)
+    convolution(done, run + 4)
     for i in range(vocab // vr):
         seen = jnp.sum(seen_ref[i * vr : (i + 1) * vr, :], axis=1, keepdims=True)
         pack_ref[SEEN + i] = jnp.broadcast_to(seen, (vr, LANES))
@@ -176,27 +197,6 @@
     order = (iota((size, size), 1) == order % RUNS * half + order // RUNS).astype(f32)
     order_ref[...] = order.astype(jnp.bfloat16)
 
-    def convolution(step, carry):
-        r, pair = step % rows, step // rows
-        sub = pl.ds(pl.multiple_of(r * RUNS, RUNS), RUNS)
-        length = len_ref[r]
-        for tile in range(WIDE // LANES):
-            cols = pl.ds(pl.multiple_of(pair * WIDE + tile * LANES, LANES), LANES)
-            taps = [jnp.broadcast_to(rows_ref[k : k + 1, cols], (RUNS, LANES)) for k in range(kernel)]
-            window = [emb_ref[k, sub, cols] for k in range(kernel - 1)]
-            for j in range(-2, run + 2):
-                window.append(emb_ref[j + LEFT, sub, cols])
-                total = taps[0] * window[0]
-                for k in range(1, kernel):
-                    total = total + taps[k] * window[k]
-                window = window[1:]
-                real = base < length - j
-                if j < 0:
-                    real = real & (base >= -j)
-                conv_ref[j + 2, sub, cols] = jnp.where(real, total, 0.0)
-        return carry
-
-    lax.fori_loop(0, rows * (feat // WIDE), convolution, 0)
     keeps.append(pltpu.make_async_copy(conv_ref, conv_hbm, sems.at[2, 0]))
     keeps[-1].start()
 

time: 104 us -> 103 us (level)
  Pallas kernels: 38.2 us -> 36.8 us
    pallas_call x1, Pallas kernels: 13.3 us -> 11.8 us  [on_device(): pl.pallas_call(functools.partial(stats_kernel, sizes), out_shape=(*(pltpu...]
where the time goes in v6:
time: 103 us; the launch traced here: 102 us
  blocking collectives  59.1 us (57%)
  Pallas kernels  36.8 us (36%)
  waiting for transfers between devices  3.83 us (4%)
  starting transfers between devices  1.28 us (1%)
    all_to_all x2, blocking collectives, traded(): return lax.all_to_all(x, AXES, 0, 0, tiled=True, axis_index_groups=groups)  31.8 us
    all_to_all x2, blocking collectives, exchanged(): return lax.all_to_all(x, AXES, 0, 0, tiled=True)  27.3 us
    pallas_call x1, Pallas kernels, on_device(): pl.pallas_call(functools.partial(back_kernel, sizes), out_shape=(pltpu.HB...  20.8 us
    pallas_call x1, Pallas kernels, on_device(): pl.pallas_call(functools.partial(stats_kernel, sizes), out_shape=(*(pltpu...  11.8 us
    ppermute x2, waiting for transfers between devices, partner(): return lax.ppermute(x, axis, [(i, i ^ step) for i in range(n)])  3.44 us
    pallas_call x1, Pallas kernels, on_device(): pl.pallas_call(functools.partial(score_kernel, sizes), out_shape=(pltpu.H...  2.66 us
  transfers between devices with their start and end apart: 4, of which 3 were waited for; matrix products, arithmetic and copies ran while one was open for 0% of the time, Pallas kernels for 0%

profile of v6, /device:TPU:0, one launch (start us, length us, event | category | flops | bytes accessed | tf_op | source)
XLA Modules:
  0.0 102.1 jit_solution(16124294073071449666)
XLA Ops:
  0.6 0.5 collective-permute-start
  1.2 0.6 collective-permute-start.1
  1.8 0.4 collective-permute-done.even_ref
  2.2 0.0 collective-permute-done.1.odd_ref
  2.2 11.8 %stats.1 = (f32[72,32,768]{2,1,0:T(8,128)}, f32[68,32,768]{2,1,0:T(8,128)}, f32[32,32,768]{2,1,0:T(8,128)}, bf16[256,2304]{1,0:T(8,128)(2,1)}, f32[26,32,128]{2,1,0:T(8,128)}, /*index=5*/f32[32,1,128]{2,1,0:T(1,128)S(1)}) custom-call(s32[4,512]{1,0:T(4,128)} %own_hbm.1, s32[4,512]{1,0:T(4,128)S(1)} %collective-permute-done.even_ref, ...), custom_call_target="tpu_custom_call" | custom-call | tf_op jit(solution)/shard_map/stats/pallas_call | solution.py:863
  14.0 17.9 %all_to_all.20.first_ref.first_hbm = f32[32,1,128]{2,1,0:T(1,128)} all-to-all(f32[32,1,128]{2,1,0:T(1,128)S(1)} %get-tuple-element.20), channel_id=1, replica_groups=mesh['rows'=8,'seq'=4] {'rows','seq'}, dimensions={0} | all-to-all | bytes 32768 | tf_op jit(solution)/shard_map/all_to_all | solution.py:806
  31.9 2.7 %score.1 = (f32[20,32,128]{2,1,0:T(8,128)}, f32[32,1,128]{2,1,0:T(1,128)S(1)}) custom-call(f32[32,1,128]{2,1,0:T(1,128)} %all_to_all.20.first_ref.first_hbm, f32[26,32,128]{2,1,0:T(8,128)} %get-tuple-element.21.dots_ref.pack_hbm), custom_call_target="tpu_custom_call" | custom-call | tf_op jit(solution)/shard_map/score/pallas_call | solution.py:882
  34.6 9.4 %all_to_all.21.second_hbm = f32[32,1,128]{2,1,0:T(1,128)} all-to-all(f32[32,1,128]{2,1,0:T(1,128)S(1)} %get-tuple-element.22), channel_id=1, replica_groups=mesh['rows'=8,'seq'=4] {'rows','seq'}, dimensions={0} | all-to-all | bytes 32768 | tf_op jit(solution)/shard_map/all_to_all | solution.py:806
  43.9 20.8 %back.1 = (f32[1024,768]{1,0:T(8,128)}, f32[100,8,128]{2,1,0:T(8,128)S(1)}, f32[100,8,128]{2,1,0:T(8,128)S(1)}) custom-call(f32[32,1,128]{2,1,0:T(1,128)} %all_to_all.20.first_ref.first_hbm, f32[32,1,128]{2,1,0:T(1,128)} %all_to_all.21.second_hbm, f32[26,32,128]{2,1,0:T(8,128)} %get-tuple-element.21.dots_ref.pack_hbm, ...), custom_call_target="tpu_custom_call" | custom-call | tf_op jit(solution)/shard_map/back/pallas_call | solution.py:893
  64.7 0.1 collective-permute-start.2
  64.9 1.7 %collective-permute-done.2 = f32[100,8,128]{2,1,0:T(8,128)S(1)} collective-permute-done((f32[100,8,128]{2,1,0:T(8,128)S(1)}, f32[100,8,128]{2,1,0:T(8,128)S(1)}, u32[]{:S(2)}, u32[]{:S(2)}) %collective-permute-start.2) | collective-permute-done | bytes 409632 | tf_op jit(solution)/shard_map/ppermute | solution.py:811
  66.6 0.1 add.3
  66.6 16.1 %all_to_all.22 = f32[16,50,1,128]{3,2,1,0:T(1,128)S(1)} all-to-all(f32[16,50,1,128]{3,2,1,0:T(1,128)S(1)} %bitcast.12), channel_id=1, replica_groups={{0,2,4,6,8,10,12,14,16,18,20,22,24,26,28,30},{1,3,5,7,9,11,13,15,17,19,..., dimensions={0} | all-to-all | bytes 819200 | tf_op jit(solution)/shard_map/all_to_all | solution.py:820
  82.7 0.3 reduce_sum.9
  82.9 0.2 broadcast_in_dim.2
  83.2 15.7 %all_to_all.23 = f32[16,50,1,128]{3,2,1,0:T(1,128)S(1)} all-to-all(f32[16,50,1,128]{3,2,1,0:T(1,128)S(1)} %broadcast_in_dim.2), channel_id=1, replica_groups={{0,2,4,6,8,10,12,14,16,18,20,22,24,26,28,30},{1,3,5,7,9,11,13,15,17,19,..., dimensions={0} | all-to-all | bytes 819200 | tf_op jit(solution)/shard_map/all_to_all | solution.py:820
  98.9 0.0 collective-permute-start.3
  98.9 1.7 %collective-permute-done.3.other_ref = f32[100,8,128]{2,1,0:T(8,128)S(1)} collective-permute-done((f32[100,8,128]{2,1,0:T(8,128)S(1)}, f32[100,8,128]{2,1,0:T(8,128)S(1)}, u32[]{:S(2)}, u32[]{:S(2)}) %collective-permute-start.3) | collective-permute-done | bytes 409632 | tf_op jit(solution)/shard_map/ppermute | solution.py:811
  100.6 1.5 %finish.1 = (f32[192,8,128]{2,1,0:T(8,128)}, f32[4,768]{1,0:T(4,128)}, f32[768]{0:T(1024)}, f32[768]{0:T(1024)}) custom-call(f32[100,8,128]{2,1,0:T(8,128)S(1)} %bitcast.10, f32[100,8,128]{2,1,0:T(8,128)S(1)} %collective-permute-done.3.other_ref), custom_call_target="tpu_custom_call" | custom-call | tf_op jit(solution)/shard_map/finish/pallas_call | solution.py:909
Async XLA Ops:
  0.6 1.6 %collective-permute-start = (s32[4,512]{1,0:T(4,128)}, s32[4,512]{1,0:T(4,128)S(1)}, u32[]{:S(2)}, u32[]{:S(2)}) collective-permute-start(s32[4,512]{1,0:T(4,128)} %own_hbm.1), channel_id=1, source_target_pairs={{0,1},{2,3},{1,0},{3,2},{4,5},{6,7},{5,4},{7,6},{8,9},{10,11},{9,8... | collective-permute-start | bytes 24584 | tf_op jit(solution)/shard_map/ppermute | solution.py:847
  1.2 1.0 %collective-permute-start.1 = (s32[4,512]{1,0:T(4,128)}, s32[4,512]{1,0:T(4,128)S(1)}, u32[]{:S(2)}, u32[]{:S(2)}) collective-permute-start(s32[4,512]{1,0:T(4,128)} %own_hbm.1), channel_id=1, source_target_pairs={{1,2},{2,1},{5,6},{6,5},{9,10},{10,9},{13,14},{14,13},{17,18},{18,... | collective-permute-start | bytes 24584 | tf_op jit(solution)/shard_map/ppermute | solution.py:847
  64.7 1.8 %collective-permute-start.2 = (f32[100,8,128]{2,1,0:T(8,128)S(1)}, f32[100,8,128]{2,1,0:T(8,128)S(1)}, u32[]{:S(2)}, u32[]{:S(2)}) collective-permute-start(f32[100,8,128]{2,1,0:T(8,128)S(1)} %get-tuple-element.30), channel_id=1, source_target_pairs={{0,1},{1,0},{2,3},{3,2},{4,5},{5,4},{6,7},{7,6},{8,9},{9,8},{10,11... | collective-permute-start | bytes 1228808 | tf_op jit(solution)/shard_map/ppermute | solution.py:811
  98.9 1.7 %collective-permute-start.3 = (f32[100,8,128]{2,1,0:T(8,128)S(1)}, f32[100,8,128]{2,1,0:T(8,128)S(1)}, u32[]{:S(2)}, u32[]{:S(2)}) collective-permute-start(f32[100,8,128]{2,1,0:T(8,128)S(1)} %bitcast.9), channel_id=1, source_target_pairs={{0,1},{1,0},{2,3},{3,2},{4,5},{5,4},{6,7},{7,6},{8,9},{9,8},{10,11... | collective-permute-start | bytes 1228808 | tf_op jit(solution)/shard_map/ppermute | solution.py:811

commit v7 on v6

--- a/solution.py
+++ b/solution.py
@@ -369,8 +369,16 @@
 REACH = range(-3, 4)
 
 
-def score_kernel(sizes, first_ref, dots_ref, state_ref, sums_ref, rows_ref):
+def score_kernel(sizes, first_hbm, dots_hbm, state_hbm, sums_ref, first_ref, dots_ref, state_ref, rows_ref, sems):
     rows, width, run, feat, vocab, kernel = sizes
+    fetch = (
+        pltpu.make_async_copy(dots_hbm.at[0:SEEN], dots_ref, sems.at[0]),
+        pltpu.make_async_copy(first_hbm, first_ref, sems.at[1]),
+    )
+    for copy in fetch:
+        copy.start()
+    for copy in fetch:
+        copy.wait()
     start = lax.axis_index("seq") * width
     unpack_rows(dots_ref, rows_ref)
     bias = rows_ref[BIAS : BIAS + 1, :]
@@ -389,6 +397,11 @@
     probs = [p / whole for p in parts]
     weights = [own * p / n for p, n in zip(probs, counts)]
 
+    for i in range(4):
+        state_ref[i] = weights[i]
+        state_ref[4 + i] = probs[i]
+    early = pltpu.make_async_copy(state_ref.at[0:8], state_hbm.at[0:8], sems.at[2])
+    early.start()
     holds = {(b, d): at.holds(b, d) for b in SIZES for d in REACH}
 
     def blend(values):
@@ -454,6 +467,12 @@
     shared = own / pair_count
     bases = [per_block(with_grad, shared), per_block(with_half, shared), per_block(with_mixed, own)]
 
+    for i in range(4):
+        for f in range(3):
+            state_ref[8 + 4 * f + i] = bases[f][i]
+    late = pltpu.make_async_copy(state_ref.at[8:], state_hbm.at[8:], sems.at[3])
+    late.start()
+
     def total_of(x):
         return jnp.sum(jnp.sum(x, axis=1, keepdims=True), axis=0, keepdims=True)
 
@@ -473,12 +492,9 @@
         total_of(shared * sum(halver[d] * shifted(normed_bias, d) for d in REACH)),
         total_of(own * sum(mixer[d] * shifted(normed_bias, d) for d in REACH)),
     ]
-    for i, b in enumerate(SIZES):
-        state_ref[i] = weights[i]
-        state_ref[4 + i] = probs[i]
-        for f in range(3):
-            state_ref[8 + 4 * f + i] = bases[f][i]
     sums_ref[...] = spread(sums, sums_ref.shape[0])
+    early.wait()
+    late.wait()
 
 
 def back_kernel(
@@ -528,6 +544,11 @@
             copy.start()
     for copy in small[4:]:
         copy.start()
+    order = iota((size, size), 0)
+    order = (iota((size, size), 1) == order % half * RUNS + order // half).astype(f32)
+    order_ref[...] = order.astype(jnp.bfloat16)
+    turn_ref[...] = jnp.zeros_like(turn_ref)
+    acc_ref[...] = jnp.zeros_like(acc_ref)
     for copy in small[:4]:
         copy.wait()
 
@@ -573,11 +594,6 @@
 
     for i, x in enumerate(narrow + paired):
         narrow_ref[i] = x
-    order = iota((size, size), 0)
-    order = (iota((size, size), 1) == order % half * RUNS + order // half).astype(f32)
-    order_ref[...] = order.astype(jnp.bfloat16)
-    turn_ref[...] = jnp.zeros_like(turn_ref)
-    acc_ref[...] = jnp.zeros_like(acc_ref)
     phase = (start + run * iota((RUNS, LANES), 0)) % 3
     at_phase = [phase == p for p in range(3)]
 
@@ -882,7 +898,10 @@
     states, second = pl.pallas_call(
         functools.partial(score_kernel, sizes),
         out_shape=(pltpu.HBM(state.shape, f32), pltpu.VMEM(sums.shape, f32)),
-        in_specs=[VMEM] * 2, out_specs=(VMEM, VMEM), scratch_shapes=[pltpu.VMEM((8, feat), f32)],
+        in_specs=[HBM] * 2, out_specs=(HBM, VMEM),
+        scratch_shapes=[
+            scratch(sums), pltpu.VMEM((SEEN, vr, LANES), f32), scratch(state), pltpu.VMEM((8, feat), f32), sem((4,)),
+        ],
         compiler_params=params, name="score",
     )(first, packed)
     second = exchanged(second)

time: 103 us -> 103 us (level)
  no operation moved by 1% of the time
where the time goes in v7:
time: 103 us; the launch traced here: 102 us
  blocking collectives  59.1 us (57%)
  Pallas kernels  36.7 us (36%)
  waiting for transfers between devices  3.83 us (4%)
  starting transfers between devices  1.28 us (1%)
    all_to_all x2, blocking collectives, traded(): return lax.all_to_all(x, AXES, 0, 0, tiled=True, axis_index_groups=groups)  31.8 us
    all_to_all x2, blocking collectives, exchanged(): return lax.all_to_all(x, AXES, 0, 0, tiled=True)  27.3 us
    pallas_call x1, Pallas kernels, on_device(): pl.pallas_call(functools.partial(back_kernel, sizes), out_shape=(pltpu.HB...  20.8 us
    pallas_call x1, Pallas kernels, on_device(): pl.pallas_call(functools.partial(stats_kernel, sizes), out_shape=(*(pltpu...  11.8 us
    ppermute x2, waiting for transfers between devices, partner(): return lax.ppermute(x, axis, [(i, i ^ step) for i in range(n)])  3.44 us
    pallas_call x1, Pallas kernels, on_device(): pl.pallas_call(functools.partial(score_kernel, sizes), out_shape=(pltpu.H...  2.58 us
  transfers between devices with their start and end apart: 4, of which 3 were waited for; matrix products, arithmetic and copies ran while one was open for 0% of the time, Pallas kernels for 0%

profile of v7, /device:TPU:0, one launch (start us, length us, event | category | flops | bytes accessed | tf_op | source)
XLA Modules:
  0.0 102.1 jit_solution(2973442852940150960)
XLA Ops:
  0.6 0.5 collective-permute-start
  1.2 0.6 collective-permute-start.1
  1.8 0.4 collective-permute-done.even_ref
  2.2 0.0 collective-permute-done.1.odd_ref
  2.2 11.8 %stats.1 = (f32[72,32,768]{2,1,0:T(8,128)}, f32[68,32,768]{2,1,0:T(8,128)}, f32[32,32,768]{2,1,0:T(8,128)}, bf16[256,2304]{1,0:T(8,128)(2,1)}, f32[26,32,128]{2,1,0:T(8,128)}, /*index=5*/f32[32,1,128]{2,1,0:T(1,128)S(1)}) custom-call(s32[4,512]{1,0:T(4,128)} %own_hbm.1, s32[4,512]{1,0:T(4,128)S(1)} %collective-permute-done.even_ref, ...), custom_call_target="tpu_custom_call" | custom-call | tf_op jit(solution)/shard_map/stats/pallas_call | solution.py:879
  14.0 17.9 %all_to_all.20.first_hbm = f32[32,1,128]{2,1,0:T(1,128)} all-to-all(f32[32,1,128]{2,1,0:T(1,128)S(1)} %get-tuple-element.20), channel_id=1, replica_groups=mesh['rows'=8,'seq'=4] {'rows','seq'}, dimensions={0} | all-to-all | bytes 32768 | tf_op jit(solution)/shard_map/all_to_all | solution.py:822
  31.9 2.6 %score.1 = (f32[20,32,128]{2,1,0:T(8,128)}, f32[32,1,128]{2,1,0:T(1,128)S(1)}) custom-call(f32[32,1,128]{2,1,0:T(1,128)} %all_to_all.20.first_hbm, f32[26,32,128]{2,1,0:T(8,128)} %get-tuple-element.21.dots_hbm.pack_hbm), custom_call_target="tpu_custom_call" | custom-call | tf_op jit(solution)/shard_map/score/pallas_call | solution.py:898
  34.5 9.4 %all_to_all.21.second_hbm = f32[32,1,128]{2,1,0:T(1,128)} all-to-all(f32[32,1,128]{2,1,0:T(1,128)S(1)} %get-tuple-element.22), channel_id=1, replica_groups=mesh['rows'=8,'seq'=4] {'rows','seq'}, dimensions={0} | all-to-all | bytes 32768 | tf_op jit(solution)/shard_map/all_to_all | solution.py:822
  43.9 20.8 %back.1 = (f32[1024,768]{1,0:T(8,128)}, f32[100,8,128]{2,1,0:T(8,128)S(1)}, f32[100,8,128]{2,1,0:T(8,128)S(1)}) custom-call(f32[32,1,128]{2,1,0:T(1,128)} %all_to_all.20.first_hbm, f32[32,1,128]{2,1,0:T(1,128)} %all_to_all.21.second_hbm, f32[26,32,128]{2,1,0:T(8,128)} %get-tuple-element.21.dots_hbm.pack_hbm, f32[20,32,128]{2,1,0:T(8,128)} %get-tuple-element.23.state_hbm, ...), custom_call_target="tpu_custom_call" | custom-call | tf_op jit(solution)/shard_map/back/pallas_call | solution.py:912
  64.7 0.1 collective-permute-start.2
  64.8 1.7 %collective-permute-done.2 = f32[100,8,128]{2,1,0:T(8,128)S(1)} collective-permute-done((f32[100,8,128]{2,1,0:T(8,128)S(1)}, f32[100,8,128]{2,1,0:T(8,128)S(1)}, u32[]{:S(2)}, u32[]{:S(2)}) %collective-permute-start.2) | collective-permute-done | bytes 409632 | tf_op jit(solution)/shard_map/ppermute | solution.py:827
  66.5 0.1 add.3
  66.6 16.1 %all_to_all.22 = f32[16,50,1,128]{3,2,1,0:T(1,128)S(1)} all-to-all(f32[16,50,1,128]{3,2,1,0:T(1,128)S(1)} %bitcast.12), channel_id=1, replica_groups={{0,2,4,6,8,10,12,14,16,18,20,22,24,26,28,30},{1,3,5,7,9,11,13,15,17,19,..., dimensions={0} | all-to-all | bytes 819200 | tf_op jit(solution)/shard_map/all_to_all | solution.py:836
  82.6 0.3 reduce_sum.9
  82.9 0.2 broadcast_in_dim.2
  83.1 15.7 %all_to_all.23 = f32[16,50,1,128]{3,2,1,0:T(1,128)S(1)} all-to-all(f32[16,50,1,128]{3,2,1,0:T(1,128)S(1)} %broadcast_in_dim.2), channel_id=1, replica_groups={{0,2,4,6,8,10,12,14,16,18,20,22,24,26,28,30},{1,3,5,7,9,11,13,15,17,19,..., dimensions={0} | all-to-all | bytes 819200 | tf_op jit(solution)/shard_map/all_to_all | solution.py:836
  98.9 0.0 collective-permute-start.3
  98.9 1.7 %collective-permute-done.3.other_ref = f32[100,8,128]{2,1,0:T(8,128)S(1)} collective-permute-done((f32[100,8,128]{2,1,0:T(8,128)S(1)}, f32[100,8,128]{2,1,0:T(8,128)S(1)}, u32[]{:S(2)}, u32[]{:S(2)}) %collective-permute-start.3) | collective-permute-done | bytes 409632 | tf_op jit(solution)/shard_map/ppermute | solution.py:827
  100.6 1.5 %finish.1 = (f32[192,8,128]{2,1,0:T(8,128)}, f32[4,768]{1,0:T(4,128)}, f32[768]{0:T(1024)}, f32[768]{0:T(1024)}) custom-call(f32[100,8,128]{2,1,0:T(8,128)S(1)} %bitcast.10, f32[100,8,128]{2,1,0:T(8,128)S(1)} %collective-permute-done.3.other_ref), custom_call_target="tpu_custom_call" | custom-call | tf_op jit(solution)/shard_map/finish/pallas_call | solution.py:928
Async XLA Ops:
  0.6 1.6 %collective-permute-start = (s32[4,512]{1,0:T(4,128)}, s32[4,512]{1,0:T(4,128)S(1)}, u32[]{:S(2)}, u32[]{:S(2)}) collective-permute-start(s32[4,512]{1,0:T(4,128)} %own_hbm.1), channel_id=1, source_target_pairs={{0,1},{2,3},{1,0},{3,2},{4,5},{6,7},{5,4},{7,6},{8,9},{10,11},{9,8... | collective-permute-start | bytes 24584 | tf_op jit(solution)/shard_map/ppermute | solution.py:863
  1.2 1.0 %collective-permute-start.1 = (s32[4,512]{1,0:T(4,128)}, s32[4,512]{1,0:T(4,128)S(1)}, u32[]{:S(2)}, u32[]{:S(2)}) collective-permute-start(s32[4,512]{1,0:T(4,128)} %own_hbm.1), channel_id=1, source_target_pairs={{1,2},{2,1},{5,6},{6,5},{9,10},{10,9},{13,14},{14,13},{17,18},{18,... | collective-permute-start | bytes 24584 | tf_op jit(solution)/shard_map/ppermute | solution.py:863
  64.7 1.8 %collective-permute-start.2 = (f32[100,8,128]{2,1,0:T(8,128)S(1)}, f32[100,8,128]{2,1,0:T(8,128)S(1)}, u32[]{:S(2)}, u32[]{:S(2)}) collective-permute-start(f32[100,8,128]{2,1,0:T(8,128)S(1)} %get-tuple-element.30), channel_id=1, source_target_pairs={{0,1},{1,0},{2,3},{3,2},{4,5},{5,4},{6,7},{7,6},{8,9},{9,8},{10,11... | collective-permute-start | bytes 1228808 | tf_op jit(solution)/shard_map/ppermute | solution.py:827
  98.9 1.7 %collective-permute-start.3 = (f32[100,8,128]{2,1,0:T(8,128)S(1)}, f32[100,8,128]{2,1,0:T(8,128)S(1)}, u32[]{:S(2)}, u32[]{:S(2)}) collective-permute-start(f32[100,8,128]{2,1,0:T(8,128)S(1)} %bitcast.9), channel_id=1, source_target_pairs={{0,1},{1,0},{2,3},{3,2},{4,5},{5,4},{6,7},{7,6},{8,9},{9,8},{10,11... | collective-permute-start | bytes 1228808 | tf_op jit(solution)/shard_map/ppermute | solution.py:827
